TPU v7x, 32 devices: a whole 2x2x4 slice. The times are simulated.
32 devices in a mesh: grp: 4 (over z), seq: 8 (over y, x, core).
Axes of the slice: x: 2, y: 2, z: 4, core: 2. Of those that a mesh axis runs over, the one named last changes fastest.
Arguments:
- tokens: bfloat16 [16, 1024, 512], P('grp', 'seq'), may hold values from -6 to 6
- segments: int32 [16, 1024], P('grp', 'seq'), may hold values from 0 to 7, never falling along the last dimension, each value on 1 to 256 neighbouring positions
- cotangent: float32 [16, 1024, 512], P('grp', 'seq'), may hold values from -6 to 6
- first_gain: bfloat16 [512], P('seq'), may hold values from 0.099609375 to 1.8984375
- value_weight: bfloat16 [512, 1024], P('seq'), may hold values from -0.25 to 0.25
- value_bias: bfloat16 [1024], P('seq'), may hold values from -3 to 3
- decay_alpha: bfloat16 [512, 16], P('seq'), may hold values from -5 to -1
- decay_delta: bfloat16 [512, 16], P('seq'), may hold values from -4 to -1
- decay_beta: bfloat16 [512, 16], P('seq'), may hold values from -4 to 4
- decay_eta: bfloat16 [512, 16], P('seq'), may hold values from -1.5 to 1.5
- skip_omega: bfloat16 [512], P('seq'), may hold values from -4 to 4
- mix_weight: bfloat16 [512, 2176], P('seq'), may hold values from -0.25 to 0.25
- mix_bias: bfloat16 [2176], P('seq'), may hold values from -3 to 3
- latent_gains: bfloat16 [2, 128], P(None, 'seq'), may hold values from -3 to 3
- query_offset: bfloat16 [128], P('seq'), may hold values from -4 to 4
- position_bias: bfloat16 [128], P('seq'), may hold values from -4 to 4
- attend_weight: bfloat16 [1024, 512], P('seq'), may hold values from -0.75 to 0.75
- second_gain: bfloat16 [512], P('seq'), may hold values from 0.099609375 to 1.8984375
- up_weight: bfloat16 [512, 1024], P('seq'), may hold values from -0.25 to 0.25
- up_bias: bfloat16 [1024], P('seq'), may hold values from -3 to 3
- down_weight: bfloat16 [1024, 512], P('seq'), may hold values from -0.1875 to 0.1875
- down_bias: bfloat16 [512], P('seq'), may hold values from -3 to 3
Outputs:
- layer_output: float32 [16, 1024, 512], P('grp', 'seq')
- tokens_grad: float32 [16, 1024, 512], P('grp', 'seq')
- first_gain_grad: float32 [512], P('seq')
- value_weight_grad: float32 [512, 1024], P('seq')
- value_bias_grad: float32 [1024], P('seq')
- decay_alpha_grad: float32 [512, 16], P('seq')
- decay_delta_grad: float32 [512, 16], P('seq')
- decay_beta_grad: float32 [512, 16], P('seq')
- decay_eta_grad: float32 [512, 16], P('seq')
- skip_omega_grad: float32 [512], P('seq')
- mix_weight_grad: float32 [512, 2176], P('seq')
- mix_bias_grad: float32 [2176], P('seq')
- latent_gains_grad: float32 [2, 128], P(None, 'seq')
- query_offset_grad: float32 [128], P('seq')
- position_bias_grad: float32 [128], P('seq')
- attend_weight_grad: float32 [1024, 512], P('seq')
- second_gain_grad: float32 [512], P('seq')
- up_weight_grad: float32 [512, 1024], P('seq')
- up_bias_grad: float32 [1024], P('seq')
- down_weight_grad: float32 [1024, 512], P('seq')
- down_bias_grad: float32 [512], P('seq')
Inputs may be any that keep to these rules, and one draw needn't show every extreme that they name: `segments`: along each sequence the segment numbers never fall; each number covers 1 to 256 consecutive tokens, and one covers exactly 256.
All inputs are finite; a program needn't handle non-finite values.
Results may differ from a plain program's by a relative error of at most 0.028.
Values may be sent and summed in bfloat16 or wider, within the bound.
No kernel may reach another device: no remote copies, remote signals or barrier semaphores. Data moves between devices by JAX's collectives and lax.ppermute only.
A program may use at most 192 MiB of HBM per device.

v0:
```python
from functools import partial

import jax
import jax.numpy as jnp
from jax import lax
from jax.sharding import PartitionSpec as P

EPSILON = 1e-06
HIGH = lax.Precision.HIGHEST


def shifted(shard, axis, by):
    length = lax.axis_size(axis)
    pairs = [(i, i + by) for i in range(length) if 0 <= i + by < length]
    return lax.ppermute(shard, axis, pairs)


def entering_2(part, axis, combine, identity):
    place = lax.axis_index(axis)
    gathered = jax.tree.map(lambda a: lax.all_gather(a, axis), part)
    state = jax.tree.map(lambda a, e: jnp.zeros_like(a) + jnp.asarray(e, a.dtype), part, identity)

    def one(turn, state):
        return combine(
            state, jax.tree.map(lambda a: lax.dynamic_index_in_dim(a, turn, 0, False), gathered)
        )

    return lax.fori_loop(0, place, one, state)


def carried_in(shard, axis, combine, identity):
    length, place = (lax.axis_size(axis), lax.axis_index(axis))
    everything = jax.tree.map(
        lambda part, kind: lax.all_gather(part.astype(kind), axis),
        shard,
        jax.tree.map(lambda a: jnp.bfloat16 if a.dtype == jnp.float32 else a.dtype, shard),
    )
    start = jax.tree.map(
        lambda part, zero: jnp.broadcast_to(jnp.asarray(zero, part.dtype), part.shape),
        shard,
        identity,
    )

    def turn(k, before):
        at = length - 1 - k
        reached = at > place
        new = combine(
            before, jax.tree.map(lambda part, own: part[at].astype(own.dtype), everything, shard)
        )
        return jax.tree.map(lambda a, b: jnp.where(reached, a, b), new, before)

    return lax.fori_loop(0, length, turn, start)


def rms_norm(values, gain):
    return values * lax.rsqrt(jnp.mean(values * values, axis=-1, keepdims=True) + EPSILON) * gain


def project(inputs, weight):
    return jnp.einsum("stk,kn->stn", inputs, weight, preferred_element_type=jnp.float32)


def project_back(grad_low, weight):
    return jnp.einsum("stn,kn->stk", grad_low, weight, preferred_element_type=jnp.float32)


def weight_grad(inputs, grad_low):
    return jnp.einsum("stk,stn->kn", inputs, grad_low, preferred_element_type=jnp.float32)


def link(earlier, later):
    return (earlier[0] * later[0], later[1] + later[0] * earlier[1])


def decay_log(alpha, delta):
    return jnp.log(1.0 - jax.nn.sigmoid(alpha) * jax.nn.sigmoid(delta))


def smooth_local(segment, keep_first, normed, alpha, delta, beta, eta):
    rows, length, width = normed.shape
    block = length // 8
    log_decay = decay_log(alpha, delta)
    inflow = jax.nn.sigmoid(alpha) * beta
    places = jnp.arange(block).astype(jnp.float32)
    powers = jnp.exp(places[:, None, None] * log_decay)
    kernel = jnp.einsum("tcj,cj->tc", powers, eta * inflow, precision=HIGH)
    offset = jnp.arange(block)[:, None] - jnp.arange(block)[None, :]
    toeplitz = jnp.where((offset >= 0)[:, :, None], kernel[jnp.clip(offset, 0, block - 1)], 0.0)
    pieces = normed.reshape(rows, 8, block, width)
    labels = segment.reshape(rows, 8, block)
    same = (labels[:, :, :, None] == labels[:, :, None, :]).astype(jnp.float32)
    inner = jnp.einsum("tkc,sntk,snkc->sntc", toeplitz, same, pieces, precision=HIGH)
    to_end = jnp.exp((block - 1.0 - places)[:, None, None] * log_decay)
    tail = (labels == labels[:, :, -1:]).astype(jnp.float32)
    finals = jnp.einsum("snk,snkc,kcj->sncj", tail, pieces, to_end, precision=HIGH) * inflow
    joined = (labels[:, 1:, 0] == labels[:, :-1, -1]).astype(jnp.float32)
    previous = jnp.concatenate([keep_first[:, None], joined], axis=1)
    whole = previous * (labels[:, :, -1] == labels[:, :, 0]).astype(jnp.float32)
    across = jnp.exp(block * log_decay)
    state = jnp.zeros((rows, width, alpha.shape[1]), jnp.float32)
    entries = []
    for index in range(8):
        entries.append(state)
        state = finals[:, index] + across * whole[:, index, None, None] * state
    entering = jnp.stack(entries, axis=1)
    onward = jnp.exp((places + 1.0)[:, None, None] * log_decay)
    linked = previous[:, :, None] * (labels == labels[:, :, :1]).astype(jnp.float32)
    carried = (
        jnp.einsum("sncj,tcj->sntc", entering * eta, onward, precision=HIGH) * linked[:, :, :, None]
    )
    series = (inner + carried).reshape(rows, length, width)
    through_flag = keep_first * (segment[:, -1] == segment[:, 0]).astype(jnp.float32)
    through = jnp.exp(length * log_decay)[None] * through_flag[:, None, None]
    return (series, through, state)


def smooth_carry(segment, keep_first, alpha, delta, eta, entering):
    length = segment.shape[1]
    log_decay = decay_log(alpha, delta)
    places = jnp.arange(length).astype(jnp.float32)
    onward = jnp.exp((places + 1.0)[:, None, None] * log_decay)
    linked = keep_first[:, None] * (segment == segment[:, :1]).astype(jnp.float32)
    return jnp.einsum("scj,tcj->stc", entering * eta, onward, precision=HIGH) * linked[:, :, None]


def mix_gate(series, values, omega):
    return jax.nn.silu(series + omega * values)


def split_gates(width, latent_width, base, gains, offset):
    update = jax.nn.sigmoid(base[..., :width])
    latent = jax.nn.silu(base[..., width : width + latent_width])
    reset = jax.nn.silu(base[..., width + latent_width : -width])
    extra = base[..., -width:]
    query = (latent * gains[0] + offset) * latent_width ** (-0.5)
    key = latent * gains[1]
    return (update, query, key, reset, extra)


def bias_table(position):
    size = position.shape[0]
    offset = jnp.arange(size)[:, None] - jnp.arange(size)[None, :]
    return jnp.where(offset >= 0, position[jnp.clip(offset, 0, size - 1)], 0.0)


def block_scores(query_low, key_low, table, allowed):
    scores = jnp.einsum("nid,njd->nij", query_low, key_low, preferred_element_type=jnp.float32)
    return jnp.where(allowed, scores + table, -1e30)


def blend(extra, projected, update, inputs):
    return inputs + update * (jax.nn.silu(extra + projected) - inputs)


def collect_forward(
    first_gain,
    value_weight,
    value_bias,
    decay_alpha,
    decay_delta,
    decay_beta,
    decay_eta,
    skip_omega,
    mix_weight,
    mix_bias,
    latent_gains,
    query_offset,
    position_bias,
    attend_weight,
    second_gain,
    up_weight,
    up_bias,
    down_weight,
    down_bias,
):
    return (
        lax.all_gather(first_gain, "seq", axis=0, tiled=True),
        lax.all_gather(value_weight, "seq", axis=0, tiled=True),
        lax.all_gather(value_bias, "seq", axis=0, tiled=True),
        lax.all_gather(decay_alpha, "seq", axis=0, tiled=True),
        lax.all_gather(decay_delta, "seq", axis=0, tiled=True),
        lax.all_gather(decay_beta, "seq", axis=0, tiled=True),
        lax.all_gather(decay_eta, "seq", axis=0, tiled=True),
        lax.all_gather(skip_omega, "seq", axis=0, tiled=True),
        lax.all_gather(mix_weight, "seq", axis=0, tiled=True),
        lax.all_gather(mix_bias, "seq", axis=0, tiled=True),
        lax.all_gather(latent_gains, "seq", axis=1, tiled=True),
        lax.all_gather(query_offset, "seq", axis=0, tiled=True),
        lax.all_gather(position_bias, "seq", axis=0, tiled=True),
        lax.all_gather(attend_weight, "seq", axis=0, tiled=True),
        lax.all_gather(second_gain, "seq", axis=0, tiled=True),
        lax.all_gather(up_weight, "seq", axis=0, tiled=True),
        lax.all_gather(up_bias, "seq", axis=0, tiled=True),
        lax.all_gather(down_weight, "seq", axis=0, tiled=True),
        lax.all_gather(down_bias, "seq", axis=0, tiled=True),
    )


def collect_backward(
    first_gain,
    value_weight,
    decay_alpha,
    decay_delta,
    decay_beta,
    decay_eta,
    skip_omega,
    mix_weight,
    latent_gains,
    position_bias,
    attend_weight,
    second_gain,
    up_weight,
    down_weight,
):
    return (
        lax.all_gather(first_gain, "seq", axis=0, tiled=True),
        lax.all_gather(value_weight, "seq", axis=0, tiled=True),
        lax.all_gather(decay_alpha, "seq", axis=0, tiled=True),
        lax.all_gather(decay_delta, "seq", axis=0, tiled=True),
        lax.all_gather(decay_beta, "seq", axis=0, tiled=True),
        lax.all_gather(decay_eta, "seq", axis=0, tiled=True),
        lax.all_gather(skip_omega, "seq", axis=0, tiled=True),
        lax.all_gather(mix_weight, "seq", axis=0, tiled=True),
        lax.all_gather(latent_gains, "seq", axis=1, tiled=True),
        lax.all_gather(position_bias, "seq", axis=0, tiled=True),
        lax.all_gather(attend_weight, "seq", axis=0, tiled=True),
        lax.all_gather(second_gain, "seq", axis=0, tiled=True),
        lax.all_gather(up_weight, "seq", axis=0, tiled=True),
        lax.all_gather(down_weight, "seq", axis=0, tiled=True),
    )


def split_sums(
    first_gain,
    value_weight,
    value_bias,
    decay_alpha,
    decay_delta,
    decay_beta,
    decay_eta,
    skip_omega,
    mix_weight,
    mix_bias,
    latent_gains,
    query_offset,
    position_bias,
    attend_weight,
    second_gain,
    up_weight,
    up_bias,
    down_weight,
    down_bias,
):
    return (
        lax.psum_scatter(
            first_gain.astype(jnp.bfloat16), "seq", scatter_dimension=0, tiled=True
        ).astype(jnp.float32),
        lax.psum_scatter(
            value_weight.astype(jnp.bfloat16), "seq", scatter_dimension=0, tiled=True
        ).astype(jnp.float32),
        lax.psum_scatter(
            value_bias.astype(jnp.bfloat16), "seq", scatter_dimension=0, tiled=True
        ).astype(jnp.float32),
        lax.psum_scatter(
            decay_alpha.astype(jnp.bfloat16), "seq", scatter_dimension=0, tiled=True
        ).astype(jnp.float32),
        lax.psum_scatter(
            decay_delta.astype(jnp.bfloat16), "seq", scatter_dimension=0, tiled=True
        ).astype(jnp.float32),
        lax.psum_scatter(
            decay_beta.astype(jnp.bfloat16), "seq", scatter_dimension=0, tiled=True
        ).astype(jnp.float32),
        lax.psum_scatter(
            decay_eta.astype(jnp.bfloat16), "seq", scatter_dimension=0, tiled=True
        ).astype(jnp.float32),
        lax.psum_scatter(
            skip_omega.astype(jnp.bfloat16), "seq", scatter_dimension=0, tiled=True
        ).astype(jnp.float32),
        lax.psum_scatter(
            mix_weight.astype(jnp.bfloat16), "seq", scatter_dimension=0, tiled=True
        ).astype(jnp.float32),
        lax.psum_scatter(
            mix_bias.astype(jnp.bfloat16), "seq", scatter_dimension=0, tiled=True
        ).astype(jnp.float32),
        lax.psum_scatter(
            latent_gains.astype(jnp.bfloat16), "seq", scatter_dimension=1, tiled=True
        ).astype(jnp.float32),
        lax.psum_scatter(
            query_offset.astype(jnp.bfloat16), "seq", scatter_dimension=0, tiled=True
        ).astype(jnp.float32),
        lax.psum_scatter(
            position_bias.astype(jnp.bfloat16), "seq", scatter_dimension=0, tiled=True
        ).astype(jnp.float32),
        lax.psum_scatter(
            attend_weight.astype(jnp.bfloat16), "seq", scatter_dimension=0, tiled=True
        ).astype(jnp.float32),
        lax.psum_scatter(
            second_gain.astype(jnp.bfloat16), "seq", scatter_dimension=0, tiled=True
        ).astype(jnp.float32),
        lax.psum_scatter(
            up_weight.astype(jnp.bfloat16), "seq", scatter_dimension=0, tiled=True
        ).astype(jnp.float32),
        lax.psum_scatter(
            up_bias.astype(jnp.bfloat16), "seq", scatter_dimension=0, tiled=True
        ).astype(jnp.float32),
        lax.psum_scatter(
            down_weight.astype(jnp.bfloat16), "seq", scatter_dimension=0, tiled=True
        ).astype(jnp.float32),
        lax.psum_scatter(
            down_bias.astype(jnp.bfloat16), "seq", scatter_dimension=0, tiled=True
        ).astype(jnp.float32),
    )


def group_sums(
    first_gain,
    value_weight,
    value_bias,
    decay_alpha,
    decay_delta,
    decay_beta,
    decay_eta,
    skip_omega,
    mix_weight,
    mix_bias,
    latent_gains,
    query_offset,
    position_bias,
    attend_weight,
    second_gain,
    up_weight,
    up_bias,
    down_weight,
    down_bias,
):
    return (
        lax.psum(first_gain.astype(jnp.bfloat16), "grp").astype(jnp.float32),
        lax.psum(value_weight.astype(jnp.bfloat16), "grp").astype(jnp.float32),
        lax.psum(value_bias.astype(jnp.bfloat16), "grp").astype(jnp.float32),
        lax.psum(decay_alpha.astype(jnp.bfloat16), "grp").astype(jnp.float32),
        lax.psum(decay_delta.astype(jnp.bfloat16), "grp").astype(jnp.float32),
        lax.psum(decay_beta.astype(jnp.bfloat16), "grp").astype(jnp.float32),
        lax.psum(decay_eta.astype(jnp.bfloat16), "grp").astype(jnp.float32),
        lax.psum(skip_omega.astype(jnp.bfloat16), "grp").astype(jnp.float32),
        lax.psum(mix_weight.astype(jnp.bfloat16), "grp").astype(jnp.float32),
        lax.psum(mix_bias.astype(jnp.bfloat16), "grp").astype(jnp.float32),
        lax.psum(latent_gains.astype(jnp.bfloat16), "grp").astype(jnp.float32),
        lax.psum(query_offset.astype(jnp.bfloat16), "grp").astype(jnp.float32),
        lax.psum(position_bias.astype(jnp.bfloat16), "grp").astype(jnp.float32),
        lax.psum(attend_weight.astype(jnp.bfloat16), "grp").astype(jnp.float32),
        lax.psum(second_gain.astype(jnp.bfloat16), "grp").astype(jnp.float32),
        lax.psum(up_weight.astype(jnp.bfloat16), "grp").astype(jnp.float32),
        lax.psum(up_bias.astype(jnp.bfloat16), "grp").astype(jnp.float32),
        lax.psum(down_weight.astype(jnp.bfloat16), "grp").astype(jnp.float32),
        lax.psum(down_bias.astype(jnp.bfloat16), "grp").astype(jnp.float32),
    )


def per_device(
    tokens,
    segments,
    cotangent,
    first_gain,
    value_weight,
    value_bias,
    decay_alpha,
    decay_delta,
    decay_beta,
    decay_eta,
    skip_omega,
    mix_weight,
    mix_bias,
    latent_gains,
    query_offset,
    position_bias,
    attend_weight,
    second_gain,
    up_weight,
    up_bias,
    down_weight,
    down_bias,
):
    gathered = collect_forward(
        first_gain,
        value_weight,
        value_bias,
        decay_alpha,
        decay_delta,
        decay_beta,
        decay_eta,
        skip_omega,
        mix_weight,
        mix_bias,
        latent_gains,
        query_offset,
        position_bias,
        attend_weight,
        second_gain,
        up_weight,
        up_bias,
        down_weight,
        down_bias,
    )
    (
        gain_one,
        value_full,
        value_shift,
        alpha_full,
        delta_full,
        beta_full,
        eta_full,
        omega_full,
        mix_full,
        mix_shift,
        gains_full,
        offset_full,
        bias_full,
        attend_full,
        gain_two,
        up_full,
        up_shift,
        down_full,
        down_shift,
    ) = gathered
    width = tokens.shape[2]
    latent_width = gains_full.shape[1]
    span = bias_full.shape[0]
    inputs = tokens.astype(jnp.float32)
    normed = rms_norm(inputs, gain_one.astype(jnp.float32))
    normed_low = normed.astype(jnp.bfloat16)
    value_linear = project(normed_low, value_full) + value_shift.astype(jnp.float32)
    value_low = jax.nn.silu(value_linear).astype(jnp.bfloat16)
    earlier_label = shifted(segments[:, -1], "seq", 1)
    keep_first = (segments[:, 0] == earlier_label).astype(jnp.float32)
    local_series, through, final_state = smooth_local(
        segments,
        keep_first,
        normed,
        alpha_full.astype(jnp.float32),
        delta_full.astype(jnp.float32),
        beta_full.astype(jnp.float32),
        eta_full.astype(jnp.float32),
    )
    _, entering = entering_2(
        (through, final_state), "seq", link, (jnp.ones_like(through), jnp.zeros_like(final_state))
    )
    carried = smooth_carry(
        segments,
        keep_first,
        alpha_full.astype(jnp.float32),
        delta_full.astype(jnp.float32),
        eta_full.astype(jnp.float32),
        entering,
    )
    smoothed = local_series + carried
    mixed_low = mix_gate(smoothed, normed, omega_full.astype(jnp.float32)).astype(jnp.bfloat16)
    base = project(mixed_low, mix_full) + mix_shift.astype(jnp.float32)
    offset_value = offset_full.astype(jnp.float32)
    update, query, key, reset, extra = split_gates(
        width, latent_width, base, gains_full.astype(jnp.float32), offset_value
    )
    query_low = query.astype(jnp.bfloat16)
    key_low = key.astype(jnp.bfloat16)
    places = jnp.arange(span)
    allowed = (places[:, None] >= places[None, :])[None] & (
        segments[:, :, None] == segments[:, None, :]
    )
    scores = block_scores(query_low, key_low, bias_table(bias_full.astype(jnp.float32)), allowed)
    highest = jnp.max(scores, axis=-1, keepdims=True)
    log_total = highest + jnp.log(jnp.sum(jnp.exp(scores - highest), axis=-1, keepdims=True))
    probs_low = jnp.exp(scores - log_total).astype(jnp.bfloat16)
    attended = jnp.einsum("nij,njd->nid", probs_low, value_low, preferred_element_type=jnp.float32)
    gated_low = (attended * reset).astype(jnp.bfloat16)
    projected = project(gated_low, attend_full)
    middle = blend(extra, projected, update, inputs)
    second_low = rms_norm(middle, gain_two.astype(jnp.float32)).astype(jnp.bfloat16)
    up_linear = project(second_low, up_full) + up_shift.astype(jnp.float32)
    hidden_low = jax.nn.silu(up_linear).astype(jnp.bfloat16)
    layer_output = middle + project(hidden_low, down_full) + down_shift.astype(jnp.float32)
    again = collect_backward(
        first_gain,
        value_weight,
        decay_alpha,
        decay_delta,
        decay_beta,
        decay_eta,
        skip_omega,
        mix_weight,
        latent_gains,
        position_bias,
        attend_weight,
        second_gain,
        up_weight,
        down_weight,
    )
    (
        back_gain_one,
        back_value,
        back_alpha,
        back_delta,
        back_beta,
        back_eta,
        back_omega,
        back_mix,
        back_gains,
        back_bias,
        back_attend,
        back_gain_two,
        back_up,
        back_down,
    ) = again
    alpha_value = back_alpha.astype(jnp.float32)
    delta_value = back_delta.astype(jnp.float32)
    beta_value = back_beta.astype(jnp.float32)
    eta_value = back_eta.astype(jnp.float32)
    down_bias_grad = jnp.sum(cotangent, axis=(0, 1))
    output_low = cotangent.astype(jnp.bfloat16)
    down_weight_grad = weight_grad(hidden_low, output_low)
    _, up_silu = jax.vjp(jax.nn.silu, up_linear)
    (grad_up,) = up_silu(project_back(output_low, back_down))
    up_bias_grad = jnp.sum(grad_up, axis=(0, 1))
    up_low = grad_up.astype(jnp.bfloat16)
    up_weight_grad = weight_grad(second_low, up_low)
    _, second_norm = jax.vjp(rms_norm, middle, back_gain_two.astype(jnp.float32))
    grad_second, second_gain_grad = second_norm(project_back(up_low, back_up))
    grad_middle = cotangent + grad_second
    _, blend_back = jax.vjp(blend, extra, projected, update, inputs)
    grad_extra, grad_projected, grad_update, grad_inputs = blend_back(grad_middle)
    extra_grad_low = grad_projected.astype(jnp.bfloat16)
    attend_weight_grad = weight_grad(gated_low, extra_grad_low)
    grad_gated = project_back(extra_grad_low, back_attend)
    grad_reset = grad_gated * attended
    attended_grad_low = (grad_gated * reset).astype(jnp.bfloat16)
    table, table_back = jax.vjp(bias_table, back_bias.astype(jnp.float32))
    scores = block_scores(query_low, key_low, table, allowed)
    probs = jnp.exp(scores - log_total)
    probs_again = probs.astype(jnp.bfloat16)
    grad_probs = jnp.einsum(
        "nid,njd->nij", attended_grad_low, value_low, preferred_element_type=jnp.float32
    )
    grad_value = jnp.einsum(
        "nij,nid->njd", probs_again, attended_grad_low, preferred_element_type=jnp.float32
    )
    grad_scores = probs * (grad_probs - jnp.sum(probs * grad_probs, axis=-1, keepdims=True))
    (position_bias_grad,) = table_back(jnp.sum(grad_scores, axis=0))
    scores_low = grad_scores.astype(jnp.bfloat16)
    grad_query = jnp.einsum("nij,njd->nid", scores_low, key_low, preferred_element_type=jnp.float32)
    grad_key = jnp.einsum("nij,nid->njd", scores_low, query_low, preferred_element_type=jnp.float32)
    _, gates_back = jax.vjp(
        partial(split_gates, width, latent_width),
        base,
        back_gains.astype(jnp.float32),
        offset_value,
    )
    grad_base, latent_gains_grad, query_offset_grad = gates_back(
        (grad_update, grad_query, grad_key, grad_reset, grad_extra)
    )
    mix_bias_grad = jnp.sum(grad_base, axis=(0, 1))
    base_low = grad_base.astype(jnp.bfloat16)
    mix_weight_grad = weight_grad(mixed_low, base_low)
    _, mixed_back = jax.vjp(mix_gate, smoothed, normed, back_omega.astype(jnp.float32))
    grad_smoothed, grad_normed_skip, skip_omega_grad = mixed_back(project_back(base_low, back_mix))
    _, carry_back = jax.vjp(
        partial(smooth_carry, segments, keep_first), alpha_value, delta_value, eta_value, entering
    )
    alpha_late, delta_late, eta_late, direct = carry_back(grad_smoothed)
    (_, through_again, _), local_back = jax.vjp(
        partial(smooth_local, segments, keep_first),
        normed,
        alpha_value,
        delta_value,
        beta_value,
        eta_value,
    )
    _, adjoint = carried_in(
        (through_again, direct), "seq", link, (jnp.ones_like(through_again), jnp.zeros_like(direct))
    )
    grad_normed_state, alpha_early, delta_early, decay_beta_grad, eta_early = local_back(
        (grad_smoothed, adjoint * entering, adjoint)
    )
    decay_alpha_grad = alpha_late + alpha_early
    decay_delta_grad = delta_late + delta_early
    decay_eta_grad = eta_late + eta_early
    _, value_silu = jax.vjp(jax.nn.silu, value_linear)
    (grad_value_linear,) = value_silu(grad_value)
    value_bias_grad = jnp.sum(grad_value_linear, axis=(0, 1))
    value_grad_low = grad_value_linear.astype(jnp.bfloat16)
    value_weight_grad = weight_grad(normed_low, value_grad_low)
    grad_normed = grad_normed_skip + grad_normed_state + project_back(value_grad_low, back_value)
    _, first_norm = jax.vjp(rms_norm, inputs, back_gain_one.astype(jnp.float32))
    grad_first, first_gain_grad = first_norm(grad_normed)
    tokens_grad = grad_inputs + grad_first
    local = (
        first_gain_grad,
        value_weight_grad,
        value_bias_grad,
        decay_alpha_grad,
        decay_delta_grad,
        decay_beta_grad,
        decay_eta_grad,
        skip_omega_grad,
        mix_weight_grad,
        mix_bias_grad,
        latent_gains_grad,
        query_offset_grad,
        position_bias_grad,
        attend_weight_grad,
        second_gain_grad,
        up_weight_grad,
        up_bias_grad,
        down_weight_grad,
        down_bias_grad,
    )
    summed = group_sums(*split_sums(*local))
    return (layer_output, tokens_grad) + tuple(summed)


def solution(mesh):
    in_specs = (
        P("grp", "seq", None),
        P("grp", "seq"),
        P("grp", "seq", None),
        P("seq"),
        P("seq", None),
        P("seq"),
        P("seq", None),
        P("seq", None),
        P("seq", None),
        P("seq", None),
        P("seq"),
        P("seq", None),
        P("seq"),
        P(None, "seq"),
        P("seq"),
        P("seq"),
        P("seq", None),
        P("seq"),
        P("seq", None),
        P("seq"),
        P("seq", None),
        P("seq"),
    )
    out_specs = (
        P("grp", "seq", None),
        P("grp", "seq", None),
        P("seq"),
        P("seq", None),
        P("seq"),
        P("seq", None),
        P("seq", None),
        P("seq", None),
        P("seq", None),
        P("seq"),
        P("seq", None),
        P("seq"),
        P(None, "seq"),
        P("seq"),
        P("seq"),
        P("seq", None),
        P("seq"),
        P("seq", None),
        P("seq"),
        P("seq", None),
        P("seq"),
    )
    return jax.shard_map(
        per_device, mesh=mesh, in_specs=in_specs, out_specs=out_specs, check_vma=False
    )
```

profile of v0, /device:TPU:0, one launch (start us, length us, event | category | flops | bytes accessed | tf_op | source)
XLA Modules:
  0.0 873.3 jit_solution(14439155778990594622)
XLA Ops:
  20.9 24.4 %all-reduce.31 = (bf16[512]{0:T(512)(128)(2,1)S(1)}, bf16[128]{0:T(256)(128)(2,1)}, bf16[128]{0:T(256)(128)(2,1)}, bf16[2176]{0:T(1024)(128)(2,1)}, bf16[512]{0:T(512)(128)(2,1)}, /*index=5*/bf16[512]{0:T(512)(128)(2,1)}) all-reduce(bf16[512]{0:T(512)(128)(2,1)S(1)} %dynamic-update-slice, ...), channel_id=1, replica_groups=mesh['grp'=4,'seq'=8] {'seq'}, use_global_device_ids=true, to_apply=%add.14 | all-reduce | flops 3968 | bytes 15872
  48.2 7.5 copy.590
  55.8 10.7 %all-gather.1 = bf16[8,64,16]{1,2,0:T(8,128)(2,1)S(1)} all-gather(bf16[1,64,16]{1,2,0:T(8,128)(2,1)S(1)} %bitcast.466), channel_id=1, replica_groups=mesh['grp'=4,'seq'=8] {'seq'}, dimensions={0}, use_global_device_ids=true | all-gather | bytes 18432 | tf_op jit(solution)/shard_map/all_gather | solution.py:183
  66.6 7.8 all-gather.2
  74.5 9.3 %all-gather.4 = bf16[8,64,16]{1,2,0:T(8,128)(2,1)S(1)} all-gather(bf16[1,64,16]{1,2,0:T(8,128)(2,1)S(1)} %bitcast.468), channel_id=1, replica_groups=mesh['grp'=4,'seq'=8] {'seq'}, dimensions={0}, use_global_device_ids=true | all-gather | bytes 18432 | tf_op jit(solution)/shard_map/all_gather | solution.py:181
  84.0 7.8 all-gather.3
  92.7 11.7 %fusion.30 = f32[512,4,8,16]{3,2,1,0:T(8,128)} fusion(f32[4,8,16,512]{2,1,0,3:T(8,128)} %copy.590, f32[16]{0:T(128)S(1)} %broadcast_subtract_fusion, f32[512,16]{1,0:T(8,128)S(1)} %copy.588), kind=kOutput, calls=%fused_computation.48 | convolution fusion | flops 50462720 | bytes 2129984 | tf_op jit(solution)/shard_map/snk,snkc,kcj->sncj/dot_general | solution.py:95
  104.4 5.1 copy.591
  127.3 9.4 %all-gather.5 = bf16[8,16,2]{1,2,0:T(2,128)(2,1)S(1)} all-gather(bf16[1,16,2]{1,2,0:T(2,128)(2,1)} %bitcast.478), channel_id=1, replica_groups=mesh['grp'=4,'seq'=8] {'seq'}, dimensions={0}, use_global_device_ids=true | all-gather | bytes 576 | tf_op jit(solution)/shard_map/all_gather | solution.py:187
  149.5 4.1 fusion.6
  153.7 7.6 copy.676
  162.5 97.2 %gather_fusion.1 = f32[16384]{0:T(1024)S(1)} fusion(f32[128]{0:T(128)S(1)} %convert_element_type.371, s32[16384]{0:T(1024)S(1)} %copy-done.42), kind=kCustom, calls=%fused_computation.1 | custom fusion | bytes 196608 | tf_op jit(solution)/shard_map/gather | solution.py:143
  260.5 7.9 all-gather.6
  269.0 8.6 all-gather.7
  291.7 7.4 copy.604
  299.2 13.6 %fusion.9 = f32[4,8,16,512]{2,1,0,3:T(8,128)} fusion(f32[4,8,512,16]{3,1,0,2:T(8,128)} %copy.676, f32[4,8,16]{2,1,0:T(8,128)S(1)} %compare_select_fusion.2, f32[4,8,512,16]{3,1,0,2:T(8,128)} %copy.604, f32[16]{0:T(128)S(1)} %copy-done.97, f32[512,16]{1,0:T(8,128)S(1)} %copy.588), kind=kOutput, calls=%fused_computation.19 | convolution fusion | flops 50987008 | bytes 3180608
  312.8 5.2 copy.605
  318.0 10.1 %all_gather.112 = bf16[8,4,512,16]{2,3,1,0:T(8,128)(2,1)} all-gather(bf16[1,4,512,16]{2,3,1,0:T(8,128)(2,1)S(1)} %copy-done.37), channel_id=1, replica_groups=mesh['grp'=4,'seq'=8] {'seq'}, dimensions={0}, use_global_device_ids=true | all-gather | bytes 589824 | tf_op jit(solution)/shard_map/all_gather | solution.py:34
  328.2 3.9 multiply_convert_fusion.3
  333.5 6.4 fusion.33
  353.0 4.3 multiply_reduce_fusion.6
  361.1 4.0 fusion.202
  384.5 7.8 copy.616
  392.3 12.0 %fusion.14 = f32[512,4,8,16]{3,2,1,0:T(8,128)} fusion(f32[4,8,16,512]{2,1,0,3:T(8,128)} %copy.616, f32[4,8,16]{2,1,0:T(8,128)S(1)} %compare_select_fusion.2, f32[16]{0:T(128)S(1)} %copy-done.98, f32[512,16]{1,0:T(8,128)S(1)} %copy.588), kind=kOutput, calls=%fused_computation.25 | convolution fusion | flops 50724864 | bytes 2132032 | tf_op jit(solution)/shard_map/transpose(jvp(sncj,tcj->sntc))/dot_general | solution.py:109
  406.8 9.0 %broadcast_multiply_fusion = (bf16[4,512,16]{2,0,1:T(4,128)(2,1)}, f32[4,512,16]{2,0,1:T(4,128)}) fusion(f32[512,16]{1,0:T(8,128)S(1)} %copy-done.39, f32[512,128,4]{1,2,0:T(4,128)} %copy.614, f32[512,16]{1,0:T(8,128)S(1)} %copy.588, f32[128]{0:T(128)S(1)} %copy-done.136), kind=kOutput, calls=%fused_computation.174 | convolution fusion | flops 51445760 | bytes 1311232 | tf_op jit(solution)/shard_map/transpose(jvp(scj,tcj->stc))/dot_general | solution.py:123
  417.6 6.0 copy.617
  424.9 17.5 %all-gather = bf16[32,512,16]{1,2,0:T(8,128)(2,1)} all-gather(bf16[4,512,16]{1,2,0:T(8,128)(2,1)S(1)} %copy.615), channel_id=2, replica_groups=mesh['grp'=4,'seq'=8] {'seq'}, dimensions={0}, use_global_device_ids=true | all-gather | bytes 589824 | tf_op jit(solution)/shard_map/all_gather | solution.py:34
  449.0 17.5 %fusion.22 = f32[512,16]{1,0:T(8,128)S(1)} fusion(f32[16]{0:T(128)S(1)} %copy-done.98, f32[512,16]{1,0:T(8,128)S(1)} %copy.588, f32[4,8,512,16]{3,1,0,2:T(8,128)} %copy.604, f32[4,8,16,512]{2,1,0,3:T(8,128)} %copy.616, f32[4,8,16]{2,1,0:T(8,128)S(1)} %compare_select_fusion.2), kind=kOutput, calls=%fused_computation.38 | convolution fusion | flops 51109888 | bytes 2164800 | tf_op jit(solution)/shard_map/transpose(jvp(sncj,tcj->sntc))/dot_general | solution.py:109
  466.8 8.0 while.29
  483.3 8.4 copy.624
  495.2 17.0 %fusion.20 = f32[512,16]{1,0:T(8,128)S(1)} fusion(f32[512,4,8,16]{3,2,1,0:T(8,128)} %copy.624, f32[4,8,16,512]{2,1,0,3:T(8,128)} %copy.590, f32[16]{0:T(128)S(1)} %copy-done.95, f32[512,16]{1,0:T(8,128)S(1)} %copy.588), kind=kOutput, calls=%fused_computation.35 | convolution fusion | flops 50847744 | bytes 2162752 | tf_op jit(solution)/shard_map/transpose(jvp(snk,snkc,kcj->sncj))/dot_general | solution.py:95
  512.9 10.8 %fusion.27 = f32[512,16]{1,0:T(8,128)} fusion(f32[512,128,4]{1,2,0:T(4,128)} %copy.614, f32[512,16]{1,0:T(8,128)S(1)} %copy.588, f32[128]{0:T(128)S(1)} %copy-done.137, f32[4,512,16]{2,0,1:T(4,128)S(1)} %copy-done.17, f32[512,16]{1,0:T(8,128)} %copy.607), kind=kOutput, calls=%fused_computation.45 | convolution fusion | flops 54550528 | bytes 1278464 | tf_op jit(solution)/shard_map/transpose(jvp(scj,tcj->stc))/dot_general | solution.py:123
  527.0 5.4 fusion.18
  532.7 8.5 multiply_bitcast_fusion.2
  541.2 20.7 %fusion.7 = f32[16,16,1,512,1]{3,2,4,1,0:T(1,128)S(1)} fusion(pred[4,8,16,16,1]{1,4,0,3,2:T(4,128)(4,1)S(1)} %copy-done.21, f32[16,16,4,8,512]{4,1,0,3,2:T(8,128)} %multiply_bitcast_fusion.2), kind=kOutput, calls=%fused_computation.15 | convolution fusion | flops 50331648 | bytes 17309696 | tf_op jit(solution)/shard_map/transpose(jvp(tkc,sntk,snkc->sntc))/dot_general | solution.py:92
  566.3 4.9 fusion.25
  576.0 4.0 multiply_reduce_fusion
  580.8 4.5 fusion.4
  588.1 8.4 copy.687
  596.5 13.9 %bitcast_add_fusion = f32[4,8,16,512]{2,1,0,3:T(8,128)} fusion(f32[4,8,512,16]{3,1,0,2:T(8,128)} %copy.687, f32[4,8,16]{2,1,0:T(8,128)S(1)} %copy-done.44, f32[512,4,8,16]{3,2,1,0:T(8,128)} %copy.624, f32[16]{0:T(128)S(1)} %copy-done.96, f32[512,16]{1,0:T(8,128)S(1)} %copy.588), kind=kOutput, calls=%fused_computation.22 | convolution fusion | flops 50987008 | bytes 3180608 | tf_op jit(solution)/shard_map/transpose(jvp(snk,snkc,kcj->sncj))/dot_general | solution.py:95
  611.2 6.1 copy.625
  620.7 3.8 fusion.71
  625.4 4.0 fusion.78
  629.7 113.8 %scatter_custom_fusion.1 = f32[128]{0:T(128)S(1)} fusion(s32[16384]{0:T(1024)} %fusion.155, f32[16384]{0:T(1024)S(1)} %bitcast.462, f32[]{:T(128)} %constant.119.clone.1), kind=kCustom, calls=%fused_computation.346 | custom fusion | flops 16384 | bytes 1024 | tf_op jit(solution)/shard_map/transpose(jvp())/scatter-add | solution.py:143
  745.8 23.8 %all-reduce.30 = (bf16[512]{0:T(512)(128)(2,1)S(1)}, bf16[512]{0:T(512)(128)(2,1)S(1)}, bf16[1024]{0:T(1024)(128)(2,1)S(1)}, bf16[512]{0:T(512)(128)(2,1)S(1)}, ...) all-reduce(bf16[512]{0:T(512)(128)(2,1)} %dynamic-update-slice.6, ...), channel_id=1, replica_groups=mesh['grp'=4,'seq'=8] {'seq'}, use_global_device_ids=true, to_apply=%add.20 | all-reduce | flops 7040 | bytes 28160
  777.0 31.8 %reduce-scatter.33.cloned.1.call-done = bf16[64,16]{1,0:T(8,128)(2,1)} async-done(((bf16[512,16]{1,0:T(8,128)(2,1)}), bf16[64,16]{1,0:T(8,128)(2,1)}) %reduce-scatter.33.cloned.1.call-update) | async-done | bytes 2064
  809.6 19.5 %all-reduce.32 = (bf16[64]{0:T(256)(128)(2,1)S(1)}, bf16[128]{0:T(256)(128)(2,1)S(1)}, bf16[64,16]{0,1:T(8,128)(2,1)S(1)}, bf16[64,16]{0,1:T(8,128)(2,1)S(1)}, b...) all-reduce(bf16[64]{0:T(256)(128)(2,1)S(1)} %dynamic-slice.8, ...), channel_id=1, replica_groups=mesh['grp'=4,'seq'=8] {'grp'}, use_global_device_ids=true, to_apply=%region_13.14 | all-reduce | flops 4944 | bytes 19776 | tf_op jit(solution)/shard_map/psum | solution.py:337
  836.7 21.2 %all-reduce.36.cloned.1.call-done = (bf16[64,1024]{1,0:T(8,128)(2,1)}, bf16[64,2176]{1,0:T(8,128)(2,1)}, bf16[128,512]{1,0:T(8,128)(2,1)}, bf16[64,1024]{1,0:T(8,128)(2,1)}, bf16[128,512]{1,0:T(8,128)(2,1)}) async-done(((bf16[64,1024]{1,0:T(8,128)(2,1)}, bf16[64,2176]{1,0:T(8,128)(2,1)}, bf16[128,512]{1,0:T(8,128)(2,1)}, bf16[64,1024]{1,0:T(8,128)(2,1)}, bf16[128,512]{1,0:T(8,128)(2,1)}), ...) | async-done | bytes 802832 | tf_op jit(solution)/shard_map/psum | solution.py:338
  (538 shorter events, 177.9 us)
Async XLA Ops:
  7.2 321.0 %all-gather.22.cloned.1.call-start = ((), (), s32[]{:S(2)}) async-start(), calls=%async_computation.13 | async-start | bytes 1179648 | tf_op jit(solution)/shard_map/all_gather | solution.py:178
  8.7 102.5 %collective-permute-start = (s32[4]{0:T(128)}, s32[4]{0:T(128)}, u32[]{:S(2)}, u32[]{:S(2)}) collective-permute-start(s32[4]{0:T(128)} %get-tuple-element.381), channel_id=1, source_target_pairs={{0,1},{1,2},{2,3},{3,4},{4,5},{5,6},{6,7},{8,9},{9,10},{10,11},{11... | collective-permute-start | bytes 56 | tf_op jit(solution)/shard_map/ppermute | solution.py:15
  11.6 320.6 %all-gather.16.cloned.1.call-start = ((), (), s32[]{:S(2)}) async-start(), calls=%async_computation.10 | async-start | bytes 1179648 | tf_op jit(solution)/shard_map/all_gather | solution.py:20
  12.4 80.2 %copy-start.94 = (f32[16]{0:T(128)}, f32[16]{0:T(128)S(1)}, u32[]{:S(2)}) copy-start(f32[16]{0:T(128)S(1)} %broadcast_subtract_fusion) | copy-start | bytes 196
  48.0 93.9 %copy-start.3 = (f32[4,128,512]{2,1,0:T(8,128)}, f32[4,128,512]{2,1,0:T(8,128)S(1)}, u32[]{:S(2)}) copy-start(f32[4,128,512]{2,1,0:T(8,128)S(1)} %fusion.69) | copy-start | bytes 3145732
  48.2 26.4 %copy-start.105 = (bf16[64,16]{0,1:T(8,128)(2,1)S(1)}, bf16[64,16]{0,1:T(8,128)(2,1)}, u32[]{:S(2)}) copy-start(bf16[64,16]{0,1:T(8,128)(2,1)} %param.33) | copy-start | bytes 6148
  48.2 35.8 %copy-start.106 = (bf16[64,16]{0,1:T(8,128)(2,1)S(1)}, bf16[64,16]{0,1:T(8,128)(2,1)}, u32[]{:S(2)}) copy-start(bf16[64,16]{0,1:T(8,128)(2,1)} %param.34) | copy-start | bytes 6148
  109.5 30.5 %copy-start.7 = (f32[512,4,8,16]{0,3,1,2:T(8,128)}, f32[512,4,8,16]{0,3,1,2:T(8,128)S(1)}, u32[]{:S(2)}) copy-start(f32[512,4,8,16]{0,3,1,2:T(8,128)S(1)} %copy.591) | copy-start | bytes 3145732
  116.8 215.3 %all-gather.18.cloned.1.call-start = ((), (), s32[]{:S(2)}) async-start(), calls=%async_computation.11 | async-start | bytes 1179648 | tf_op jit(solution)/shard_map/all_gather | solution.py:20
  118.4 226.6 %all-gather.20.cloned.1.call-start = ((), (), s32[]{:S(2)}) async-start(), calls=%async_computation.12 | async-start | bytes 2506752 | tf_op jit(solution)/shard_map/all_gather | solution.py:185
  119.0 234.0 %all-gather.24.cloned.1.call-start = ((), (), s32[]{:S(2)}) async-start(), calls=%async_computation.14 | async-start | bytes 1179648 | tf_op jit(solution)/shard_map/all_gather | solution.py:190
  119.6 237.8 %all-gather.26.cloned.1.call-start = ((), (), s32[]{:S(2)}) async-start(), calls=%async_computation.15 | async-start | bytes 1179648 | tf_op jit(solution)/shard_map/all_gather | solution.py:192
  120.2 240.9 %all-gather.28.cloned.1.call-start = ((), (), s32[]{:S(2)}) async-start(), calls=%async_computation.16 | async-start | bytes 1179648 | tf_op jit(solution)/shard_map/all_gather | solution.py:194
  120.9 508.5 %reduce-scatter.27.cloned.1.call-start = ((), (), s32[]{:S(2)}) async-start(), calls=%async_computation.20 | async-start | bytes 1179648 | tf_op jit(solution)/shard_map/reduce_scatter | solution.py:300
  161.2 181.2 %copy-start.57 = (f32[512]{0:T(512)}, f32[512]{0:T(512)S(1)}, u32[]{:S(2)}) copy-start(f32[512]{0:T(512)S(1)} %convert_element_type.364) | copy-start | bytes 6148
  162.4 98.1 %copy-start.118 = (bf16[128]{0:T(256)(128)(2,1)S(1)}, bf16[128]{0:T(256)(128)(2,1)}, u32[]{:S(2)}) copy-start(bf16[128]{0:T(256)(128)(2,1)} %param.31) | copy-start | bytes 772
  162.4 106.6 %copy-start.116 = (bf16[512]{0:T(512)(128)(2,1)S(1)}, bf16[512]{0:T(512)(128)(2,1)}, u32[]{:S(2)}) copy-start(bf16[512]{0:T(512)(128)(2,1)} %get-tuple-element.418) | copy-start | bytes 3076
  162.4 106.6 %copy-start.119 = (bf16[128]{0:T(256)(128)(2,1)S(1)}, bf16[128]{0:T(256)(128)(2,1)}, u32[]{:S(2)}) copy-start(bf16[128]{0:T(256)(128)(2,1)} %param.45) | copy-start | bytes 772
  162.4 115.8 %copy-start.40 = (pred[4,8,16,16,1]{3,2,1,0,4:T(8,128)(4,1)S(1)}, pred[4,8,16,16,1]{3,2,1,0,4:T(8,128)(4,1)}, u32[]{:S(2)}) copy-start(pred[4,8,16,16,1]{3,2,1,0,4:T(8,128)(4,1)} %get-tuple-element.485) | copy-start | bytes 24580
  162.4 120.8 %copy-start.128 = (bf16[64]{0:T(256)(128)(2,1)S(1)}, bf16[64]{0:T(256)(128)(2,1)}, u32[]{:S(2)}) copy-start(bf16[64]{0:T(256)(128)(2,1)} %param.47) | copy-start | bytes 388
  162.4 122.1 %copy-start.56 = (s32[4,128]{1,0:T(4,128)S(1)}, s32[4,128]{1,0:T(4,128)}, u32[]{:S(2)}) copy-start(s32[4,128]{1,0:T(4,128)} %param.27) | copy-start | bytes 6148
  162.4 122.1 %copy-start.100 = (s32[4]{0:T(128)S(1)}, s32[4]{0:T(128)}, u32[]{:S(2)}) copy-start(s32[4]{0:T(128)} %get-tuple-element.382) | copy-start | bytes 52
  162.4 122.1 %copy-start.101 = (f32[4]{0:T(128)S(1)}, f32[4]{0:T(128)}, u32[]{:S(2)}) copy-start(f32[4]{0:T(128)} %get-tuple-element.459) | copy-start | bytes 52
  162.5 122.2 %copy-start.77 = (f32[4]{0:T(128)S(1)}, f32[4]{0:T(128)}, u32[]{:S(2)}) copy-start(f32[4]{0:T(128)} %copy-done.76) | copy-start | bytes 52
  162.5 123.4 %copy-start.68 = (f32[4]{0:T(128)S(1)}, f32[4]{0:T(128)}, u32[]{:S(2)}) copy-start(f32[4]{0:T(128)} %copy-done.67) | copy-start | bytes 52
  162.5 124.1 %copy-start.74 = (f32[4]{0:T(128)S(1)}, f32[4]{0:T(128)}, u32[]{:S(2)}) copy-start(f32[4]{0:T(128)} %copy-done.73) | copy-start | bytes 52
  162.5 124.9 %copy-start.87 = (f32[4]{0:T(128)S(1)}, f32[4]{0:T(128)}, u32[]{:S(2)}) copy-start(f32[4]{0:T(128)} %copy-done.86) | copy-start | bytes 52
  162.5 125.6 %copy-start.71 = (f32[4]{0:T(128)S(1)}, f32[4]{0:T(128)}, u32[]{:S(2)}) copy-start(f32[4]{0:T(128)} %copy-done.70) | copy-start | bytes 52
  162.5 126.3 %copy-start.84 = (f32[4]{0:T(128)S(1)}, f32[4]{0:T(128)}, u32[]{:S(2)}) copy-start(f32[4]{0:T(128)} %copy-done.83) | copy-start | bytes 52
  162.5 127.1 %copy-start.81 = (f32[4]{0:T(128)S(1)}, f32[4]{0:T(128)}, u32[]{:S(2)}) copy-start(f32[4]{0:T(128)} %copy-done.80) | copy-start | bytes 52
  269.0 102.5 %copy-start.52 = (f32[512]{0:T(512)}, f32[512]{0:T(512)S(1)}, u32[]{:S(2)}) copy-start(f32[512]{0:T(512)S(1)} %convert_element_type.377) | copy-start | bytes 6148
  368.0 261.5 %reduce-scatter.25.cloned.1.call-start = ((), (), s32[]{:S(2)}) async-start(), calls=%async_computation.19 | async-start | bytes 1179648 | tf_op jit(solution)/shard_map/reduce_scatter | solution.py:294
  466.7 162.8 %reduce-scatter.21.cloned.1.call-start = ((), (), s32[]{:S(2)}) async-start(), calls=%async_computation.17 | async-start | bytes 1179648 | tf_op jit(solution)/shard_map/reduce_scatter | solution.py:258
  474.8 154.7 %reduce-scatter.29.cloned.1.call-start = ((), (), s32[]{:S(2)}) async-start(), calls=%async_computation.21 | async-start | bytes 1179648 | tf_op jit(solution)/shard_map/reduce_scatter | solution.py:306
  495.1 134.4 %reduce-scatter.23.cloned.1.call-start = ((), (), s32[]{:S(2)}) async-start(), calls=%async_computation.18 | async-start | bytes 2506752 | tf_op jit(solution)/shard_map/reduce_scatter | solution.py:279
  532.5 241.4 %reduce-scatter.39.cloned.1.call-start = ((), (), s32[]{:S(2)}) async-start(), calls=%async_computation.26 | async-start | bytes 36864
  585.3 189.3 %reduce-scatter.31.cloned.1.call-start = ((), (), s32[]{:S(2)}) async-start(), calls=%async_computation.22 | async-start | bytes 147456
  596.5 179.0 %reduce-scatter.35.cloned.1.call-start = ((), (), s32[]{:S(2)}) async-start(), calls=%async_computation.24 | async-start | bytes 147456
  617.3 158.9 %reduce-scatter.37.cloned.1.call-start = ((), (), s32[]{:S(2)}) async-start(), calls=%async_computation.25 | async-start | bytes 147456
  620.7 188.1 %reduce-scatter.33.cloned.1.call-start = ((), (), s32[]{:S(2)}) async-start(), calls=%async_computation.23 | async-start | bytes 147456
  624.5 119.0 %copy-start.6 = (f32[4,128,512]{2,1,0:T(8,128)S(1)}, f32[4,128,512]{2,1,0:T(8,128)}, u32[]{:S(2)}) copy-start(f32[4,128,512]{2,1,0:T(8,128)} %copy-done.5) | copy-start | bytes 3145732
  624.5 119.1 %copy-start.36 = (f32[4,128,128]{2,1,0:T(8,128)S(1)}, f32[4,128,128]{2,1,0:T(8,128)}, u32[]{:S(2)}) copy-start(f32[4,128,128]{2,1,0:T(8,128)} %copy-done.34) | copy-start | bytes 786436
  625.3 232.6 %all-reduce.36.cloned.1.call-start = ((), (), s32[]{:S(2)}) async-start(), calls=%async_computation.27 | async-start | bytes 1605632 | tf_op jit(solution)/shard_map/psum | solution.py:338
  629.4 116.4 %copy-start.113 = (bf16[1024]{0:T(1024)(128)(2,1)S(1)}, bf16[1024]{0:T(1024)(128)(2,1)}, u32[]{:S(2)}) copy-start(bf16[1024]{0:T(1024)(128)(2,1)} %get-tuple-element.510) | copy-start | bytes 6148
  629.4 116.4 %copy-start.114 = (bf16[1024]{0:T(1024)(128)(2,1)S(1)}, bf16[1024]{0:T(1024)(128)(2,1)}, u32[]{:S(2)}) copy-start(bf16[1024]{0:T(1024)(128)(2,1)} %get-tuple-element.508) | copy-start | bytes 6148
  629.4 116.4 %copy-start.115 = (bf16[512]{0:T(512)(128)(2,1)S(1)}, bf16[512]{0:T(512)(128)(2,1)}, u32[]{:S(2)}) copy-start(bf16[512]{0:T(512)(128)(2,1)} %get-tuple-element.359) | copy-start | bytes 3076
  629.4 116.4 %copy-start.120 = (bf16[128]{0:T(256)(128)(2,1)S(1)}, bf16[128]{0:T(256)(128)(2,1)}, u32[]{:S(2)}) copy-start(bf16[128]{0:T(256)(128)(2,1)} %get-tuple-element.367) | copy-start | bytes 772
  629.4 140.9 %copy-start.110 = (f32[8,1,128]{2,1,0:T(1,128)S(1)}, f32[8,1,128]{2,1,0:T(1,128)}, u32[]{:S(2)}) copy-start(f32[8,1,128]{2,1,0:T(1,128)} %convert_element_type.438) | copy-start | bytes 12292
  (113 other events, 865.8 us)
Sparse Core Ops, SparseCore 0:
  11.7 25.7 all-gather.21
  117.0 24.0 all-gather.15
  143.5 23.4 all-gather.17
  168.7 28.4 all-gather.19
  199.0 23.4 all-gather.23
  224.3 23.4 all-gather.25
  249.7 23.4 all-gather.27
  368.1 43.7 reduce-scatter.26
  466.8 36.3 reduce-scatter.24
  506.2 36.0 reduce-scatter.20
  545.5 35.9 reduce-scatter.28
  584.7 41.8 reduce-scatter.22
  629.6 31.2 reduce-scatter.38
  664.6 33.3 reduce-scatter.30
  701.4 33.3 reduce-scatter.34
  738.6 33.4 reduce-scatter.36
  775.5 33.3 reduce-scatter.32
  811.6 46.2 all-reduce.35
where the time goes:
time: 884 us; the launch traced here: 873 us
  other arithmetic  226 us (26%)
  local copies, waits for them, and re-layouts  222 us (25%)
  matrix products  188 us (21%)
  blocking collectives  157 us (18%)
  waiting for transfers between devices  55.6 us (6%)
  between operations  20.8 us (2%)
    scatter-add x1, other arithmetic, bias_table(): return jnp.where(offset >= 0, position[jnp.clip(offset, 0, size - 1)], 0.0)  114 us
    gather x2, local copies, waits for them, and re-layouts, bias_table(): return jnp.where(offset >= 0, position[jnp.clip(offset, 0, size - 1)], 0.0)  97.3 us
    unnamed x2, blocking collectives  48.2 us
    dot_general x3, matrix products, smooth_local(): jnp.einsum('snk,snkc,kcj->sncj', tail, pieces, to_end, precision=HIGH)  42.6 us
    unnamed x23, waiting for transfers between devices  34.3 us
    dot_general x2, matrix products, smooth_local(): jnp.einsum('sncj,tcj->sntc', entering * eta, onward, precision=HIGH)  29.5 us
    unnamed x327, local copies, waits for them, and re-layouts  28.3 us
    all_gather x2, blocking collectives, carried_in(): lax.all_gather(part.astype(kind), axis)  27.7 us
  transfers between devices with their start and end apart: 19, of which 2 were waited for; matrix products, arithmetic and copies ran while one was open for 70% of the time, Pallas kernels for 0%

commit v1 on v0

v1 whole, which is shorter than its diff:
```python
from functools import partial

import jax
import jax.numpy as jnp
from jax import lax
from jax.experimental import pallas as pl
from jax.experimental.pallas import tpu as pltpu
from jax.sharding import PartitionSpec as P

EPSILON = 1e-06
F32 = jnp.float32
BF = jnp.bfloat16
TILE = 128
SUBS = 8
ROWS_SMALL = 88
NN = (((1,), (0,)), ((), ()))
NT = (((1,), (1,)), ((), ()))
TN = (((0,), (0,)), ((), ()))


def dot(a, b, dims=NN):
    return lax.dot_general(a, b, dims, preferred_element_type=F32)


def sig(v):
    return 0.5 * jnp.tanh(0.5 * v) + 0.5


def struct(shape, dtype):
    return jax.ShapeDtypeStruct(shape, dtype)


VM = pl.BlockSpec(memory_space=pltpu.VMEM)
HB = pl.BlockSpec(memory_space=pl.ANY)
PARAMS = pltpu.CompilerParams(vmem_limit_bytes=56 << 20)


def whole(body, outs, scratch=(), in_specs=None, n_in=None, name=None):
    return pl.pallas_call(
        body,
        out_shape=outs,
        in_specs=in_specs if in_specs is not None else [VM] * n_in,
        out_specs=jax.tree.map(lambda _: VM, outs),
        scratch_shapes=list(scratch),
        compiler_params=PARAMS,
        name=name,
    )


def tiles(m_size, n_size, tm, tn, fn):
    nm, nn = m_size // tm, n_size // tn

    def body(i, _):
        fn(pl.multiple_of((i % nm) * tm, tm), pl.multiple_of((i // nm) * tn, tn))
        return 0

    lax.fori_loop(0, nm * nn, body, 0)


def rows_loop(total, step, fn):
    def body(i, _):
        fn(pl.multiple_of(i * step, step))
        return 0

    lax.fori_loop(0, total // step, body, 0)


def ceil_div(a, b):
    return -(-a // b)


def spread(n, devices):
    return max(ceil_div((d * n) % TILE + n, TILE) for d in range(devices))


def place_kernel(flat_ref, dec_ref, out_ref, *, plan):
    me = lax.axis_index("seq")
    out_ref[...] = jnp.zeros_like(out_ref)
    held = dec_ref.shape[0]
    row = lax.broadcasted_iota(jnp.int32, (held, TILE), 0)
    lane = lax.broadcasted_iota(jnp.int32, (held, TILE), 1)
    pick = jnp.where(lane == row + (me * held) % TILE, 1.0, 0.0).astype(BF)
    out_ref[0 : dec_ref.shape[1], :] = dot(dec_ref[...], pick, TN)
    for at, off, n, nt in plan:
        low, high = off // TILE * TILE, ceil_div(off + n, TILE) * TILE
        values = jnp.broadcast_to(flat_ref[:, low:high].astype(F32), (SUBS, high - low)).astype(BF)
        row = lax.broadcasted_iota(jnp.int32, (high - low, nt * TILE), 0) - (off - low)
        lane = lax.broadcasted_iota(jnp.int32, (high - low, nt * TILE), 1)
        hit = (lane == row + (me * n) % TILE) & (row >= 0) & (row < n)
        moved = dot(values, jnp.where(hit, 1.0, 0.0).astype(BF))
        for j in range(nt):
            out_ref[at + j : at + j + 1, :] = moved[0:1, j * TILE : (j + 1) * TILE]


def assemble(src, low, high, n, total, devices):
    parts = [None] * ceil_div(total, TILE)
    for d in range(devices):
        t = d * n // TILE
        block = src[d, low:high, :]
        parts[t] = block if parts[t] is None else parts[t] + block
    return parts


def chunk_labels(lab_ref, steps):
    return lab_ref[pl.ds(0, SUBS, stride=steps), :], lab_ref[pl.ds(steps - 1, SUBS, stride=steps), :]


def lanes_of(t):
    return slice(t * TILE, (t + 1) * TILE)


def one_way(src_ref, lab_ref, ref_label, dk_ref, out_ref, dims, steps, width, reverse, unroll=8):
    for lt in range(width // TILE):
        lanes = lanes_of(lt)
        decay = [jnp.broadcast_to(dk_ref[h : h + 1, lanes], (SUBS, TILE)) for h in range(dims)]

        def step(i, state, lt=lt, decay=decay):
            state = list(state)
            for u in range(unroll):
                t = i * unroll + u
                if reverse:
                    t = steps - 1 - t
                x = src_ref[lt, pl.ds(t, SUBS, stride=steps), :]
                l = lab_ref[pl.ds(t, SUBS, stride=steps), :]
                x = jnp.where(l == ref_label, x, 0.0)
                state = [decay[h] * state[h] + x for h in range(dims)]
            return tuple(state)

        zero = jnp.zeros((SUBS, TILE), F32)
        final = lax.fori_loop(0, steps // unroll, step, (zero,) * dims)
        for h in range(dims):
            out_ref[h * SUBS : (h + 1) * SUBS, lanes] = final[h]


def norm_scale(x):
    return lax.rsqrt(jnp.mean(x * x, axis=-1, keepdims=True) + EPSILON)


def head_kernel(
    small_ref, tok_ref, seg_ref, pd_ref, pv_ref, pz_ref, pm_ref, dk_ref, nrm_ref, low_ref, lab_ref,
    fin_ref, msg_ref, scr_ref, *, devices, dims, nv, nm,
):
    tokens, width = tok_ref.shape
    seqs, length = seg_ref.shape
    steps = tokens // SUBS
    for t, part in enumerate(assemble(small_ref, 0, 72, width // devices, width, devices)):
        pd_ref[:, lanes_of(t)] = part
    for t, part in enumerate(assemble(small_ref, 72, 80, nv // devices, nv, devices)):
        pv_ref[:, lanes_of(t)] = part
    z = small_ref[0, 72:80, :]
    for d in range(1, devices):
        z = z + small_ref[d, 72:80, :]
    pz_ref[...] = z
    n = nm // devices
    cells = [None] * (nm // TILE)
    for d in range(devices):
        first, lane = divmod(d * n, TILE)
        for j in range(ceil_div(lane + n, TILE)):
            piece = small_ref[d, 80 + j : 81 + j, :]
            cells[first + j] = piece if cells[first + j] is None else cells[first + j] + piece
    for t, piece in enumerate(cells):
        pm_ref[:, lanes_of(t)] = jnp.broadcast_to(piece, (SUBS, TILE))

    rate = 1.0 / (1.0 + jnp.exp(-pd_ref[0:dims, :]))
    damping = 1.0 / (1.0 + jnp.exp(-pd_ref[dims : 2 * dims, :]))
    decay = 1.0 - rate * damping
    dk_ref[0:dims, :] = decay
    dk_ref[dims : 2 * dims, :] = pd_ref[3 * dims : 4 * dims, :] * rate * pd_ref[2 * dims : 3 * dims, :]
    power, k = decay, 1
    while k < steps:
        power, k = power * power, k * 2
    dk_ref[2 * dims : 3 * dims, :] = power

    gain = pd_ref[4 * dims : 4 * dims + 1, :]

    def norm(r):
        x = tok_ref[pl.ds(r, 64), :].astype(F32)
        y = x * norm_scale(x) * gain
        for t in range(width // TILE):
            nrm_ref[t, pl.ds(r, 64), :] = y[:, lanes_of(t)]
        low_ref[pl.ds(r, 64), :] = y.astype(BF)

    rows_loop(tokens, 64, norm)

    labels = seg_ref[...].astype(F32)
    row = lax.broadcasted_iota(jnp.int32, (length, length), 0)
    col = lax.broadcasted_iota(jnp.int32, (length, length), 1)
    for s in range(seqs):
        diagonal = jnp.where(row == col, labels[s : s + 1, :], 0.0).astype(BF)
        lab_ref[s * length : (s + 1) * length, :] = dot(diagonal, jnp.ones((length, TILE), BF))

    first, last = chunk_labels(lab_ref, steps)
    one_way(nrm_ref, lab_ref, last, dk_ref, fin_ref, dims, steps, width, False)
    through = (first == last) & (first == pltpu.roll(last, 1, 0))
    for lt in range(width // TILE):
        lanes = lanes_of(lt)
        for h in range(dims):
            own = fin_ref[h * SUBS : (h + 1) * SUBS, lanes]
            before = pltpu.roll(own, 1, 0) * power[h : h + 1, lanes]
            scr_ref[h * SUBS : (h + 1) * SUBS, :] = own + jnp.where(through, before, 0.0)
        half = SUBS // seqs
        msg_ref[0 : dims * seqs, lanes] = scr_ref[
            pl.ds(half - 1, dims * seqs, stride=half), :
        ].astype(BF)
        ends = lab_ref[pl.ds(length - 1, seqs, stride=length), :]
        tail = jnp.concatenate([ends, jnp.zeros((16 - seqs, TILE), F32)], axis=0)
        msg_ref[dims * seqs : dims * seqs + 16, lanes] = tail.astype(BF)


def entering(msgs, own_label, even, scr_refs, lab_scr, start, dims, seqs, power):
    half = SUBS // seqs
    gates = []
    for m, scr in zip(msgs, scr_refs):
        scr[pl.ds(start, dims * seqs, stride=half), :] = m[0 : dims * seqs, :].astype(F32)
        tail = m[dims * seqs : dims * seqs + 16, :].astype(F32)
        lab_scr[pl.ds(start, seqs, stride=half), :] = tail[0:seqs, :]
        gates.append(even & (lab_scr[...] == own_label))
    result = []
    for h in range(dims):
        total, reach = None, None
        for gate, scr in zip(gates, scr_refs):
            part = jnp.where(gate, scr[h * SUBS : (h + 1) * SUBS, :], 0.0)
            if total is None:
                total, reach = part, power[h : h + 1, :] * power[h : h + 1, :]
                far = reach
            else:
                total, far = total + part * far, far * reach
        result.append(total)
    return result


def scan_kernel(*refs, reach, dims, seqs):
    nrm_ref, lab_ref, dk_ref, pd_ref, fin_ref = refs[:5]
    msgs = refs[5 : 5 + reach]
    z_ref, mlow_ref, sp_ref = refs[5 + reach : 8 + reach]
    ent_ref, lab_scr, ys_ref = refs[8 + reach : 11 + reach]
    scr_refs = refs[11 + reach :]
    tokens = nrm_ref.shape[0]
    steps = tokens // SUBS
    half = SUBS // seqs
    first, last = chunk_labels(lab_ref, steps)
    place = lax.broadcasted_iota(jnp.int32, (SUBS, TILE), 0)
    even = place % half == 0
    power = dk_ref[2 * dims : 3 * dims, :]
    arrivals = entering(msgs, first, even, scr_refs, lab_scr, 0, dims, seqs, power)
    inside = first == last
    joined = first == pltpu.roll(last, 1, 0)
    for h in range(dims):
        e = arrivals[h]
        own = fin_ref[h * SUBS : (h + 1) * SUBS, :]
        onward = pltpu.roll(own + jnp.where(inside, e * power[h : h + 1, :], 0.0), 1, 0)
        ent_ref[h * SUBS : (h + 1) * SUBS, :] = jnp.where(even, e, jnp.where(joined, onward, 0.0))
    decay = [jnp.broadcast_to(dk_ref[h : h + 1, :], (SUBS, TILE)) for h in range(dims)]
    weight = [jnp.broadcast_to(dk_ref[dims + h : dims + h + 1, :], (SUBS, TILE)) for h in range(dims)]
    unroll = 4

    def step(i, carry):
        before, state = carry[0], list(carry[1:])
        for u in range(unroll):
            t = i * unroll + u
            x = nrm_ref[pl.ds(t, SUBS, stride=steps), :]
            l = lab_ref[pl.ds(t, SUBS, stride=steps), :]
            same = l == before
            before = l
            sums = [None] * 4
            for h in range(dims):
                kept = jnp.where(same, state[h], 0.0)
                sp_ref[t, h * SUBS : (h + 1) * SUBS, :] = kept
                state[h] = decay[h] * kept + x
                term = weight[h] * state[h]
                sums[h % 4] = term if sums[h % 4] is None else sums[h % 4] + term
            ys_ref[pl.ds(t, SUBS, stride=steps), :] = (sums[0] + sums[1]) + (sums[2] + sums[3])
        return (before,) + tuple(state)

    start = tuple(ent_ref[h * SUBS : (h + 1) * SUBS, :] for h in range(dims))
    lax.fori_loop(0, steps // unroll, step, (first,) + start)
    omega = pd_ref[4 * dims + 1 : 4 * dims + 2, :]

    def gate(r):
        v = ys_ref[pl.ds(r, 64), :] + omega * nrm_ref[pl.ds(r, 64), :]
        z_ref[pl.ds(r, 64), :] = v
        mlow_ref[pl.ds(r, 64), :] = (v * sig(v)).astype(BF)

    rows_loop(tokens, 64, gate)


def load_weights(pieces, dst, sem, rows, start, cols, place):
    me = lax.axis_index("seq")
    copies = []
    for k, piece in enumerate(pieces):
        p = me ^ k
        copies.append(
            pltpu.make_async_copy(
                piece.at[pl.ds(start, rows), pl.ds(0, cols)],
                dst.at[pl.ds(pl.multiple_of(p * rows, rows), rows), pl.ds(0, cols)],
                sem.at[place, k],
            )
        )
    for c in copies:
        c.start()
    return copies


def split_sizes(width, latent, nv):
    return {"u": 0, "l": width, "r": width + latent, "e": width + latent + nv}


def front_kernel(*refs, devices):
    pieces = refs[:devices]
    nlow, mlow, pv, pm, pz, lab, seg = refs[devices : devices + 7]
    vlow, dval, upd, ext, lat, rs, ad, glow, probs, qlow, klow = refs[devices + 7 : devices + 18]
    w, res, sem = refs[devices + 18 :]
    tokens, width = nlow.shape
    nv = vlow.shape[1]
    zw = lat.shape[1]
    seqs, length = seg.shape
    rows = width // devices
    copies = load_weights(pieces, w, sem, rows, 0, w.shape[1], 0)
    for c in copies:
        c.wait()

    def value(m, n):
        v = dot(nlow[pl.ds(m, 256), :], w[:, pl.ds(n, 256)]) + pv[0:1, pl.ds(n, 256)]
        s = sig(v)
        vlow[pl.ds(m, 256), pl.ds(n, 256)] = (v * s).astype(BF)
        dval[pl.ds(m, 256), pl.ds(n, 256)] = (s * (1.0 + v * (1.0 - s))).astype(BF)

    tiles(tokens, nv, 256, 256, value)
    at = split_sizes(width, zw, nv)

    def base(m, n, start, size):
        cols = pl.multiple_of(start + n, TILE)
        wcols = pl.multiple_of(nv + start + n, TILE)
        return dot(mlow[pl.ds(m, 256), :], w[:, pl.ds(wcols, size)]) + pm[0:1, pl.ds(cols, size)]

    def update(m, n):
        upd[pl.ds(m, 256), pl.ds(n, 256)] = sig(base(m, n, at["u"], 256))

    tiles(tokens, width, 256, 256, update)

    def extra(m, n):
        ext[pl.ds(m, 256), pl.ds(n, 256)] = base(m, n, at["e"], 256)

    tiles(tokens, width, 256, 256, extra)

    def reset(m, n):
        res[pl.ds(m, 256), pl.ds(n, 256)] = base(m, n, at["r"], 256)

    tiles(tokens, nv, 256, 256, reset)

    def latent(m, n):
        v = base(m, n, at["l"], zw)
        lat[pl.ds(m, 256), :] = v
        y = v * sig(v)
        qlow[pl.ds(m, 256), :] = ((y * pz[2:3, :] + pz[4:5, :]) * zw ** (-0.5)).astype(BF)
        klow[pl.ds(m, 256), :] = (y * pz[3:4, :]).astype(BF)

    tiles(tokens, zw, 256, zw, latent)

    row = lax.broadcasted_iota(jnp.int32, (length, length), 0)
    col = lax.broadcasted_iota(jnp.int32, (length, length), 1)
    flip = jnp.where((row + col) % length == 0, 1.0, 0.0).astype(BF)
    bias = dot(pz[...].astype(BF), flip)[5:6, :]
    table = pltpu.roll(jnp.broadcast_to(bias, (length, length)), 0, 1, stride=1, stride_axis=0)
    causal = row >= col

    def attend(r):
        here = pl.ds(r, length)
        label_j = seg[pl.ds(r // length, 1), :].astype(F32)
        allowed = causal & (lab[here, :] == label_j)
        scores = dot(qlow[here, :], klow[here, :], NT) + table
        scores = jnp.where(allowed, scores, -1e30)
        weights = jnp.exp(scores - jnp.max(scores, axis=-1, keepdims=True))
        prob = weights / jnp.sum(weights, axis=-1, keepdims=True)
        probs[here, :] = prob
        plow = prob.astype(BF)
        for n in range(nv // 256):
            cols = slice(n * 256, (n + 1) * 256)
            a = dot(plow, vlow[here, cols])
            v = res[here, cols]
            s = sig(v)
            y = v * s
            rs[here, cols] = y.astype(BF)
            ad[here, cols] = (a * (s * (1.0 + v * (1.0 - s)))).astype(BF)
            glow[here, cols] = (a * y).astype(BF)

    rows_loop(tokens, length, attend)


def column_sum(ref, row, cols, values, first):
    total = jnp.sum(values, axis=0, keepdims=True)

    @pl.when(first)
    def _():
        ref[row : row + 1, cols] = total

    @pl.when(jnp.logical_not(first))
    def _():
        ref[row : row + 1, cols] = ref[row : row + 1, cols] + total


def put_pieces(src, own, sib, devices, depth, rows, at, src_cols, cols):
    me = lax.axis_index("seq")
    for p in range(devices):
        k = me ^ p
        kc = k // 2

        def put(dst, p=p, kc=kc):
            for z in range(depth):
                begin = (p * depth + z) * rows
                dst[kc, z, at : at + rows, cols] = src[begin : begin + rows, src_cols].astype(BF)

        pl.when(k % 2 == 0)(partial(put, own))
        pl.when(k % 2 == 1)(partial(put, sib))


def middle_kernel(*refs, devices, depth, dims):
    pieces = refs[:devices]
    tok, cot, upd, ext, rs, ad, glow, pd, pv = refs[devices : devices + 9]
    out, gin, attg, blu, blre, v512, v1024, own, sib = refs[devices + 9 : devices + 18]
    w2, wup, proj, mid, slow, dup, hlow, clow, ulow, elow, gmid, grad, sem = refs[devices + 18 :]
    tokens, width = tok.shape
    nv = rs.shape[1]
    nf = dup.shape[1]
    rows2, rows1 = nv // devices, width // devices
    copies = load_weights(pieces, w2, sem, rows2, 0, 2 * width, 0)
    copies += load_weights(pieces, wup, sem, rows1, rows2, nf, 1)
    for c in copies:
        c.wait()
    down = pl.ds(width, width)

    def project(m, n):
        proj[pl.ds(m, 256), pl.ds(n, 256)] = dot(glow[pl.ds(m, 256), :], w2[:, pl.ds(n, 256)])

    tiles(tokens, width, 256, 256, project)
    gain = pd[4 * dims + 2 : 4 * dims + 3, :]

    def blend(r):
        here = pl.ds(r, 64)
        x = tok[here, :].astype(F32)
        pre = ext[here, :] + proj[here, :]
        s = sig(pre)
        m = x + upd[here, :] * (pre * s - x)
        mid[here, :] = m
        slow[here, :] = (m * norm_scale(m) * gain).astype(BF)

    rows_loop(tokens, 64, blend)

    def up(m, n):
        v = dot(slow[pl.ds(m, 256), :], wup[:, pl.ds(n, 256)]) + pv[1:2, pl.ds(n, 256)]
        s = sig(v)
        hlow[pl.ds(m, 256), pl.ds(n, 256)] = (v * s).astype(BF)
        dup[pl.ds(m, 256), pl.ds(n, 256)] = s * (1.0 + v * (1.0 - s))

    tiles(tokens, nf, 256, 256, up)

    def down_forward(m, n):
        at, cols = pl.ds(m, 256), pl.ds(n, 256)
        y = dot(hlow[at, :], w2[:, pl.ds(pl.multiple_of(width + n, 256), 256)])
        out[at, cols] = mid[at, cols] + y + pd[4 * dims + 3 : 4 * dims + 4, cols]
        c = cot[at, cols]
        clow[at, cols] = c.astype(BF)
        column_sum(v512, 0, cols, c, m == 0)

    tiles(tokens, width, 256, 256, down_forward)

    def up_back(m, n):
        at, cols = pl.ds(m, 256), pl.ds(n, 256)
        g = dot(clow[at, :], w2[cols, down], NT) * dup[at, cols]
        ulow[at, cols] = g.astype(BF)
        column_sum(v1024, 0, cols, g, m == 0)

    tiles(tokens, nf, 256, 256, up_back)

    def down_grad(m, n):
        grad[pl.ds(m, 256), pl.ds(pl.multiple_of(width + n, 256), 256)] = dot(
            hlow[:, pl.ds(m, 256)], clow[:, pl.ds(n, 256)], TN
        ).astype(BF)

    tiles(nf, width, 256, 256, down_grad)

    def second_back(m, n):
        proj[pl.ds(m, 256), pl.ds(n, 256)] += 0.0
        gmid[pl.ds(m, 256), pl.ds(n, 256)] = dot(ulow[pl.ds(m, 256), :], wup[pl.ds(n, 256), :], NT)

    tiles(tokens, width, 256, 256, second_back)
    everything = slice(0, width)

    def middle_back(r):
        here = pl.ds(r, 64)
        start = r == 0
        m = mid[here, :]
        g = gmid[here, :]
        scale = norm_scale(m)
        n = m * scale
        column_sum(v512, 1, everything, g * n, start)
        g = g * gain
        gm = cot[here, :] + scale * (g - n * jnp.mean(g * n, axis=-1, keepdims=True))
        x = tok[here, :].astype(F32)
        pre = ext[here, :] + proj[here, :]
        s = sig(pre)
        u = upd[here, :]
        ge = gm * u * (s * (1.0 + pre * (1.0 - s)))
        gu = gm * (pre * s - x) * (u * (1.0 - u))
        gin[here, :] = gm * (1.0 - u)
        low = ge.astype(BF)
        elow[here, :] = low
        blre[here, pl.ds(nv, width)] = low
        blu[here, :] = gu.astype(BF)
        column_sum(v512, 2, everything, gu, start)
        column_sum(v512, 3, everything, ge, start)

    rows_loop(tokens, 64, middle_back)

    def gated_back(m, n):
        at, cols = pl.ds(m, 256), pl.ds(n, 256)
        g = dot(elow[at, :], w2[cols, pl.ds(0, width)], NT)
        gr = g * ad[at, cols].astype(F32)
        blre[at, cols] = gr.astype(BF)
        attg[at, cols] = (g * rs[at, cols].astype(F32)).astype(BF)
        column_sum(v1024, 1, cols, gr, m == 0)

    tiles(tokens, nv, 256, 256, gated_back)

    def attend_grad(m, n):
        grad[pl.ds(m, 256), pl.ds(n, 256)] = dot(
            glow[:, pl.ds(m, 256)], elow[:, pl.ds(n, 256)], TN
        ).astype(BF)

    tiles(nv, width, 256, 256, attend_grad)
    r2, r1 = rows2 // depth, rows1 // depth
    put_pieces(grad, own, sib, devices, depth, r2, 0, slice(0, 2 * width), slice(0, 2 * width))

    def up_grad(m, n):
        grad[pl.ds(m, 256), pl.ds(n, 256)] = dot(
            slow[:, pl.ds(m, 256)], ulow[:, pl.ds(n, 256)], TN
        ).astype(BF)

    tiles(width, nf, 256, 256, up_grad)
    put_pieces(grad, own, sib, devices, depth, r1, r2, slice(0, nf), slice(0, nf))


def back_kernel(*refs, devices, dims):
    pieces = refs[:devices]
    probs, attg, vlow, dval, qlow, klow, lat, blu, blre, z, nrm, pd, pz, dk, lab = refs[
        devices : devices + 15
    ]
    vgl, bll, gs, gnp, w512, w1024, w128, msg, ach = refs[devices + 15 : devices + 24]
    w, gq, gk, scr, sem = refs[devices + 24 :]
    tokens, width = z.shape
    nv = vlow.shape[1]
    zw = lat.shape[1]
    seqs = tokens // probs.shape[1]
    length = probs.shape[1]
    steps = tokens // SUBS
    rows = width // devices
    copies = load_weights(pieces, w, sem, rows, 0, w.shape[1], 0)
    row = lax.broadcasted_iota(jnp.int32, (length, length), 0)
    col = lax.broadcasted_iota(jnp.int32, (length, length), 1)

    def attend(r, total):
        here = pl.ds(pl.multiple_of(r * length, length), length)
        p = probs[here, :]
        plow = p.astype(BF)
        gp = dot(attg[here, :], vlow[here, :], NT)
        gsc = p * (gp - jnp.sum(p * gp, axis=-1, keepdims=True))
        low = gsc.astype(BF)
        gq[here, :] = dot(low, klow[here, :])
        gk[here, :] = dot(low, qlow[here, :], TN)
        for n in range(nv // 256):
            cols = slice(n * 256, (n + 1) * 256)
            gv = dot(plow, attg[here, cols], TN) * dval[here, cols].astype(F32)
            vgl[here, cols] = gv.astype(BF)
            column_sum(w1024, 0, cols, gv, r == 0)
        return total + gsc

    total = lax.fori_loop(0, seqs, attend, jnp.zeros((length, length), F32))
    flip = jnp.where((row + col) % length == 0, 1.0, 0.0)
    turned = lax.dot_general(
        total, flip, NN, precision=lax.Precision.HIGHEST, preferred_element_type=F32
    )
    turned = pltpu.roll(turned, 0, 1, stride=1, stride_axis=0)
    w128[...] = jnp.zeros_like(w128)
    w128[5:6, :] = jnp.sum(turned, axis=0, keepdims=True)

    def latent_back(r):
        here = pl.ds(r, 128)
        v = lat[here, :]
        s = sig(v)
        y = v * s
        q = gq[here, :] * zw ** (-0.5)
        k = gk[here, :]
        g = (q * pz[2:3, :] + k * pz[3:4, :]) * (s * (1.0 + v * (1.0 - s)))
        bll[here, :] = g.astype(BF)
        start = r == 0
        every = slice(0, zw)
        column_sum(w128, 0, every, g, start)
        column_sum(w128, 2, every, q * y, start)
        column_sum(w128, 3, every, k * y, start)
        column_sum(w128, 4, every, q, start)

    rows_loop(tokens, 128, latent_back)
    for c in copies:
        c.wait()
    at = split_sizes(width, zw, nv)

    def mixed_back(m, n):
        here, cols = pl.ds(m, 256), pl.ds(n, 256)
        g = dot(blu[here, :], w[cols, nv : nv + width], NT)
        g = g + dot(bll[here, :], w[cols, nv + at["l"] : nv + at["r"]], NT)
        g = g + dot(blre[here, :], w[cols, nv + at["r"] :], NT)
        v = z[here, cols]
        s = sig(v)
        g = g * (s * (1.0 + v * (1.0 - s)))
        t = n // TILE
        for j in range(256 // TILE):
            gs[t + j, here, :] = g[:, lanes_of(j)]
        column_sum(w512, 0, cols, g * two(nrm, t, here), m == 0)

    tiles(tokens, width, 256, 256, mixed_back)
    first, last = chunk_labels(lab, steps)
    one_way(gs, lab, first, dk, ach, dims, steps, width, True)
    power = dk[2 * dims : 3 * dims, :]
    through = (first == last) & (last == pltpu.roll(first, SUBS - 1, 0))
    for lt in range(width // TILE):
        lanes = lanes_of(lt)
        for h in range(dims):
            here = slice(h * SUBS, (h + 1) * SUBS)
            after = pltpu.roll(ach[here, lanes], SUBS - 1, 0) * power[h : h + 1, lanes]
            scr[here, :] = ach[here, lanes] + jnp.where(through, after, 0.0)
        half = SUBS // seqs
        msg[0 : dims * seqs, lanes] = scr[pl.ds(0, dims * seqs, stride=half), :].astype(BF)
        starts = lab[pl.ds(0, seqs, stride=length), :]
        tail = jnp.concatenate([starts, jnp.zeros((16 - seqs, TILE), F32)], axis=0)
        msg[dims * seqs : dims * seqs + 16, lanes] = tail.astype(BF)

    def normed_back(m, n):
        here, cols = pl.ds(m, 256), pl.ds(n, 256)
        omega = pd[4 * dims + 1 : 4 * dims + 2, cols]
        gnp[here, cols] = two(gs, n // TILE, here) * omega + dot(vgl[here, :], w[cols, 0:nv], NT)

    tiles(tokens, width, 256, 256, normed_back)


def two(ref, t, here):
    return jnp.concatenate([ref[t + j, here, :] for j in range(256 // TILE)], axis=1)


def weight_kernel(
    nlow, mlow, vgl, blu, bll, blre, own, sib, grad, *, devices, depth
):
    tokens, width = nlow.shape
    nv = vgl.shape[1]
    zw = bll.shape[1]
    at = split_sizes(width, zw, nv)

    def piece(lhs, rhs, start, cols):
        def fn(m, n):
            grad[pl.ds(m, 256), pl.ds(pl.multiple_of(start + n, TILE), cols)] = dot(
                lhs[:, pl.ds(m, 256)], rhs[:, pl.ds(n, cols)], TN
            ).astype(BF)

        tiles(width, rhs.shape[1], 256, cols, fn)

    piece(nlow, vgl, 0, 256)
    piece(mlow, blu, nv, 256)
    piece(mlow, bll, nv + at["l"], zw)
    piece(mlow, blre, nv + at["r"], 256)
    full = slice(0, grad.shape[1])
    put_pieces(grad, own, sib, devices, depth, width // devices // depth, 0, full, full)


def last_kernel(*refs, reach, devices, dims, seqs, nm):
    sp, nrm, gs, gnp, lab, dk, pdb, ach = refs[:8]
    msgs = refs[8 : 8 + reach]
    tok, gin, pd, v512, v1024, w512, w1024, w128 = refs[8 + reach : 16 + reach]
    tg, own, sib = refs[16 + reach : 19 + reach]
    ent, lab_scr, gnb, gnf, sd, sv, sm = refs[19 + reach : 26 + reach]
    scr_refs = refs[26 + reach :]
    tokens = nrm.shape[0]
    width = tok.shape[1]
    steps = tokens // SUBS
    half = SUBS // seqs
    lt = pl.program_id(0)
    first, last = chunk_labels(lab, steps)
    place = lax.broadcasted_iota(jnp.int32, (SUBS, TILE), 0)
    odd = place % half == half - 1
    power = dk[2 * dims : 3 * dims, :]
    arrivals = entering(msgs, last, odd, scr_refs, lab_scr, half - 1, dims, seqs, power)
    inside = first == last
    joined = last == pltpu.roll(first, SUBS - 1, 0)
    for h in range(dims):
        e = arrivals[h]
        here = slice(h * SUBS, (h + 1) * SUBS)
        onward = pltpu.roll(
            ach[here, :] + jnp.where(inside, e * power[h : h + 1, :], 0.0), SUBS - 1, 0
        )
        ent[here, :] = jnp.where(odd, e, jnp.where(joined, onward, 0.0))
    unroll = 4
    group = 8
    zero = jnp.zeros((SUBS, TILE), F32)
    cols = pl.ds(pl.multiple_of(lt * TILE, TILE), TILE)
    for base in range(0, dims, group):
        span = range(base, base + group)
        decay = [jnp.broadcast_to(dk[h : h + 1, :], (SUBS, TILE)) for h in span]
        weight = [jnp.broadcast_to(dk[dims + h : dims + h + 1, :], (SUBS, TILE)) for h in span]

        def step(i, carry, base=base, decay=decay, weight=weight):
            after = carry[0]
            a, g0, g1 = (list(carry[1 + j * group : 1 + (j + 1) * group]) for j in range(3))
            for u in range(unroll):
                t = steps - 1 - (i * unroll + u)
                here = pl.ds(t, SUBS, stride=steps)
                x = nrm[here, :]
                g = gs[here, :]
                l = lab[here, :]
                same = l == after
                after = l
                sums = [gnp[here, :] if base == 0 else gnb[here, :], zero]
                for j in range(group):
                    h = base + j
                    a[j] = decay[j] * jnp.where(same, a[j], 0.0) + g
                    g0[j] = g0[j] + a[j] * x
                    g1[j] = g1[j] + a[j] * sp[t, h * SUBS : (h + 1) * SUBS, :]
                    sums[j % 2] = sums[j % 2] + weight[j] * a[j]
                gnb[here, :] = sums[0] + sums[1]
            return (after,) + tuple(a) + tuple(g0) + tuple(g1)

        start = tuple(ent[h * SUBS : (h + 1) * SUBS, :] for h in span)
        done = lax.fori_loop(0, steps // unroll, step, (last,) + start + (zero,) * (2 * group))
        for j in range(group):
            h = base + j
            g0 = jnp.sum(done[1 + group + j], axis=0, keepdims=True)
            g1 = jnp.sum(done[1 + 2 * group + j], axis=0, keepdims=True)
            rate = 1.0 / (1.0 + jnp.exp(-pdb[h : h + 1, :]))
            damping = 1.0 / (1.0 + jnp.exp(-pdb[dims + h : dims + h + 1, :]))
            beta = pdb[2 * dims + h : 2 * dims + h + 1, :]
            eta = pdb[3 * dims + h : 3 * dims + h + 1, :]
            grad_decay = g1 * eta * rate * beta
            grad_rate = g0 * eta * beta - damping * grad_decay
            sd[h : h + 1, cols] = grad_rate * rate * (1.0 - rate)
            sd[dims + h : dims + h + 1, cols] = -grad_decay * rate * damping * (1.0 - damping)
            sd[2 * dims + h : 2 * dims + h + 1, cols] = g0 * rate * eta
            sd[3 * dims + h : 3 * dims + h + 1, cols] = g0 * rate * beta
    gnf[:, cols] = gnb[...]

    @pl.when(lt == pl.num_programs(0) - 1)
    def _():
        top = 4 * dims
        gain = pd[top : top + 1, :]
        sd[top : top + 8, :] = jnp.zeros((8, width), F32)

        def norm(r):
            here = pl.ds(r, 64)
            x = tok[here, :].astype(F32)
            q = norm_scale(x)
            m = x * q
            gn = gnf[here, :]
            sd[top : top + 1, :] += jnp.sum(gn * m, axis=0, keepdims=True)
            gn = gn * gain
            tg[here, :] = gin[here, :] + q * (gn - m * jnp.mean(gn * m, axis=-1, keepdims=True))

        rows_loop(tokens, 64, norm)
        sd[top + 1 : top + 2, :] = w512[0:1, :]
        sd[top + 2 : top + 3, :] = v512[1:2, :]
        sd[top + 3 : top + 4, :] = v512[0:1, :]
        nv = v1024.shape[1]
        zw = w128.shape[1]
        sv[...] = jnp.zeros_like(sv)
        sv[0:1, :] = w1024[0:1, :]
        sv[1:2, :] = v1024[0:1, :]
        at = split_sizes(width, zw, nv)
        sm[...] = jnp.zeros_like(sm)
        sm[0:1, 0:width] = v512[2:3, :]
        sm[0:1, at["l"] : at["r"]] = w128[0:1, :]
        sm[0:1, at["r"] : at["e"]] = v1024[1:2, :]
        sm[0:1, at["e"] : nm] = v512[3:4, :]
        me = lax.axis_index("seq")
        zrow = lax.broadcasted_iota(jnp.int32, (8, TILE), 0)
        zpart = jnp.where(zrow >= 2, w128[...], 0.0)
        for p in range(devices):
            k = me ^ p
            kc = k // 2

            def put(dst, p=p, kc=kc):
                dst[kc, 0:72, :] = sd[:, lanes_of(p * (width // devices) // TILE)]
                dst[kc, 72:80, :] = sv[:, lanes_of(p * (nv // devices) // TILE)] + zpart
                begin = p * (nm // devices) // TILE
                dst[kc, 80:88, :] = jnp.zeros((8, TILE), F32)
                for j in range(spread(nm // devices, devices)):
                    dst[kc, 80 + j : 81 + j, :] = sm[0:1, lanes_of(begin + j)]

            pl.when(k % 2 == 0)(partial(put, own))
            pl.when(k % 2 == 1)(partial(put, sib))


def hop(x, axis, k):
    length = lax.axis_size(axis)
    return lax.ppermute(x, axis, [(i, i ^ k) for i in range(length)])


def fold_kernel(own, got, *outs):
    for k, out in enumerate(outs):
        out[...] = (own[k].astype(F32) + got[k].astype(F32)).astype(out.dtype)


def fold(own, sib, dtype):
    got = hop(sib, "seq", 1)
    outs = [struct(own.shape[1:], F32)] + [struct(own.shape[1:], dtype)] * (own.shape[0] - 1)
    return whole(fold_kernel, outs, n_in=2, name="fold")(own, got)


def across(parts):
    return [parts[0]] + [hop(part, "seq", 2 * k) for k, part in enumerate(parts) if k]


def deal_kernel(*refs, count, depth):
    ins, outs, scr = refs[:count], refs[count:-1], refs[-1]
    me = lax.axis_index("grp")
    total = ins[0][...]
    for other in ins[1:]:
        total = total + other[...].astype(F32)
    scr[...] = total
    for k in range(depth):
        outs[k][...] = scr[me ^ k].astype(outs[k].dtype)


def deal(parts, depth):
    shape = parts[0].shape
    outs = [struct(shape[1:], F32)] + [struct(shape[1:], BF)] * (depth - 1)
    body = partial(deal_kernel, count=len(parts), depth=depth)
    mine = whole(body, outs, [pltpu.VMEM(shape, F32)], n_in=len(parts), name="deal")(*parts)
    return [mine[0]] + [hop(part, "grp", k) for k, part in enumerate(mine) if k]


def join_kernel(*refs):
    total = refs[0][...]
    for other in refs[1:-1]:
        total = total + other[...].astype(F32)
    refs[-1][...] = total.astype(BF)


def join(parts):
    depth = len(parts)
    mine = whole(join_kernel, struct(parts[0].shape, BF), n_in=depth, name="join")(*parts)
    return [mine] + [hop(mine, "grp", k) for k in range(1, depth)]


def spread_a_kernel(*refs, depth, r2, width):
    ins, (attend, down, up, scr) = refs[:depth], refs[depth:]
    me = lax.axis_index("grp")
    for k in range(depth):
        scr[me ^ k] = ins[k][...].astype(F32)
    r1 = up.shape[0] // depth
    for z in range(depth):
        attend[z * r2 : (z + 1) * r2, :] = scr[z, 0:r2, 0:width]
        down[z * r2 : (z + 1) * r2, :] = scr[z, 0:r2, width:]
        up[z * r1 : (z + 1) * r1, :] = scr[z, r2:, :]


def spread_b_kernel(*refs, depth):
    ins, (value, mix, scr) = refs[:depth], refs[depth:]
    me = lax.axis_index("grp")
    for k in range(depth):
        scr[me ^ k] = ins[k][...].astype(F32)
    r = value.shape[0] // depth
    nv = value.shape[1]
    for z in range(depth):
        value[z * r : (z + 1) * r, :] = scr[z, :, 0:nv]
        mix[z * r : (z + 1) * r, :] = scr[z, :, nv:]


def final_kernel(*refs, depth, plan, held, dims):
    ins, dec, flat, scr = refs[:depth], refs[depth], refs[depth + 1], refs[depth + 2]
    grp, me = lax.axis_index("grp"), lax.axis_index("seq")
    for k in range(depth):
        scr[grp ^ k] = ins[k][...]
    total = scr[0]
    for z in range(1, depth):
        total = total + scr[z]
    row = lax.broadcasted_iota(jnp.int32, (held, TILE), 0)
    lane = lax.broadcasted_iota(jnp.int32, (held, TILE), 1)
    pick = jnp.where(lane == row + (me * held) % TILE, 1.0, 0.0)
    dec[...] = lax.dot_general(
        pick, total[0 : 4 * dims, :], NT, precision=lax.Precision.HIGHEST, preferred_element_type=F32
    )
    flat[...] = jnp.zeros_like(flat)
    for j, (at, _, n, nt) in enumerate(plan):
        values = [total[at + i : at + i + 1, :] for i in range(nt)]
        values = values[0] if nt == 1 else jnp.concatenate(values, axis=1)
        values = jnp.broadcast_to(values, (SUBS, nt * TILE))
        lanes = nt * TILE
        moved = pltpu.roll(values, (lanes - (me * n) % TILE) % lanes, 1)
        flat[j : j + 1, 0:lanes] = moved[0:1, :]


def total_kernel(*refs):
    total = refs[0][...]
    for other in refs[1:-1]:
        total = total + other[...]
    refs[-1][...] = total


def gather_pieces(x, devices):
    near = [x] + [hop(x, "seq", 2 * k) for k in range(1, devices // 2)]
    far = [hop(part, "seq", 1) for part in near]
    return [part for pair in zip(near, far) for part in pair]


def per_device(
    tokens, segments, cotangent, first_gain, value_weight, value_bias, decay_alpha, decay_delta,
    decay_beta, decay_eta, skip_omega, mix_weight, mix_bias, latent_gains, query_offset,
    position_bias, attend_weight, second_gain, up_weight, up_bias, down_weight, down_bias,
):
    devices = lax.axis_size("seq")
    depth = lax.axis_size("grp")
    seqs, length, width = tokens.shape
    count = seqs * length
    steps = count // SUBS
    dims = decay_alpha.shape[1]
    nv = value_weight.shape[1]
    nf = up_weight.shape[1]
    nm = mix_weight.shape[1]
    zw = query_offset.shape[0] * devices
    reach = max(1, devices // 4)
    held = width // devices

    vectors = [
        (72, value_bias), (73, up_bias), (80, mix_bias), (64, first_gain), (65, skip_omega),
        (66, second_gain), (67, down_bias), (74, latent_gains[0]), (75, latent_gains[1]),
        (76, query_offset), (77, position_bias),
    ]
    plan, off = [], 0
    for at, v in vectors:
        plan.append((at, off, v.shape[0], spread(v.shape[0], devices)))
        off += v.shape[0]
    padded = ceil_div(off, TILE) * TILE
    flat = jnp.concatenate([v for _, v in vectors] + [jnp.zeros((padded - off,), BF)])[None]
    decs = jnp.concatenate([decay_alpha, decay_delta, decay_beta, decay_eta], axis=1)
    placed = whole(
        partial(place_kernel, plan=plan), struct((ROWS_SMALL, TILE), F32), n_in=2, name="place"
    )(flat, decs)
    small = lax.all_gather(placed, "seq", axis=0, tiled=False)

    w1 = gather_pieces(jnp.concatenate([value_weight, mix_weight], axis=1), devices)
    w2 = gather_pieces(
        jnp.concatenate([jnp.concatenate([attend_weight, down_weight], axis=1), up_weight], axis=0),
        devices,
    )

    tok = tokens.reshape(count, width)
    cot = cotangent.reshape(count, width)
    blocks = width // TILE
    msg_rows = dims * seqs + 16
    pd, pv, pz, pm, dk, nrm, nlow, lab, fin, msg = whole(
        partial(head_kernel, devices=devices, dims=dims, nv=nv, nm=nm),
        [
            struct((72, width), F32), struct((8, nv), F32), struct((8, TILE), F32),
            struct((8, nm), F32), struct((3 * dims, width), F32), struct((blocks, count, TILE), F32),
            struct((count, width), BF), struct((count, TILE), F32),
            struct((dims * SUBS, width), F32), struct((msg_rows, width), BF),
        ],
        [pltpu.VMEM((dims * SUBS, TILE), F32)],
        n_in=3,
        name="head",
    )(small, tok, segments)

    onward = [
        lax.ppermute(msg, "seq", [(i, i + k) for i in range(devices - k)])
        for k in range(1, reach + 1)
    ]

    def lane_block(rows):
        return pl.BlockSpec((rows, TILE), lambda i: (0, i))

    tile_block = pl.BlockSpec((None, count, TILE), lambda i: (i, 0, 0))

    def fixed(shape):
        return pl.BlockSpec(shape, lambda i: (0,) * len(shape))

    arrivals = [pltpu.VMEM((dims * SUBS, TILE), F32)] * reach
    z, mlow, sp = pl.pallas_call(
        partial(scan_kernel, reach=reach, dims=dims, seqs=seqs),
        grid=(blocks,),
        in_specs=[
            tile_block, fixed((count, TILE)), lane_block(3 * dims), lane_block(72),
            lane_block(dims * SUBS),
        ] + [lane_block(msg_rows)] * reach,
        out_specs=[
            lane_block(count), lane_block(count),
            pl.BlockSpec((steps, dims * SUBS, TILE), lambda i: (0, 0, i)),
        ],
        out_shape=[
            struct((count, width), F32), struct((count, width), BF),
            struct((steps, dims * SUBS, width), F32),
        ],
        scratch_shapes=[
            pltpu.VMEM((dims * SUBS, TILE), F32), pltpu.VMEM((SUBS, TILE), F32),
            pltpu.VMEM((count, TILE), F32),
        ] + arrivals,
        compiler_params=PARAMS,
        name="scan",
    )(nrm, lab, dk, pd, fin, *onward)

    def sems(n):
        return pltpu.SemaphoreType.DMA((n, devices))

    vlow, dval, upd, ext, lat, rs, ad, glow, probs, qlow, klow = whole(
        partial(front_kernel, devices=devices),
        [
            struct((count, nv), BF), struct((count, nv), BF), struct((count, width), F32),
            struct((count, width), F32), struct((count, zw), F32), struct((count, nv), BF),
            struct((count, nv), BF), struct((count, nv), BF), struct((count, length), F32),
            struct((count, zw), BF), struct((count, zw), BF),
        ],
        [pltpu.VMEM((width, nv + nm), BF), pltpu.VMEM((count, nv), F32), sems(1)],
        in_specs=[HB] * devices + [VM] * 7,
        name="front",
    )(*w1, nlow, mlow, pv, pm, pz, lab, segments)

    half = devices // 2
    rows2, rows1 = nv // devices // depth, held // depth
    piece_a = struct((half, depth, rows2 + rows1, 2 * width), BF)
    out, gin, attg, blu, blre, v512, v1024, own_a, sib_a = whole(
        partial(middle_kernel, devices=devices, depth=depth, dims=dims),
        [
            struct((count, width), F32), struct((count, width), F32), struct((count, nv), BF),
            struct((count, width), BF), struct((count, nv + width), BF), struct((8, width), F32),
            struct((8, nv), F32), piece_a, piece_a,
        ],
        [
            pltpu.VMEM((nv, 2 * width), BF), pltpu.VMEM((width, nf), BF),
            pltpu.VMEM((count, width), F32), pltpu.VMEM((count, width), F32),
            pltpu.VMEM((count, width), BF), pltpu.VMEM((count, nf), F32),
            pltpu.VMEM((count, nf), BF), pltpu.VMEM((count, width), BF),
            pltpu.VMEM((count, nf), BF), pltpu.VMEM((count, width), BF),
            pltpu.VMEM((count, width), F32), pltpu.VMEM((nv, 2 * width), BF), sems(2),
        ],
        in_specs=[HB] * devices + [VM] * 9,
        name="middle",
    )(*w2, tok, cot, upd, ext, rs, ad, glow, pd, pv)

    vgl, bll, gs, gnp, w512, w1024, w128, back_msg, ach = whole(
        partial(back_kernel, devices=devices, dims=dims),
        [
            struct((count, nv), BF), struct((count, zw), BF), struct((blocks, count, TILE), F32),
            struct((count, width), F32), struct((8, width), F32), struct((8, nv), F32),
            struct((8, TILE), F32), struct((msg_rows, width), BF),
            struct((dims * SUBS, width), F32),
        ],
        [
            pltpu.VMEM((width, nv + nm), BF), pltpu.VMEM((count, zw), F32),
            pltpu.VMEM((count, zw), F32), pltpu.VMEM((dims * SUBS, TILE), F32), sems(1),
        ],
        in_specs=[HB] * devices + [VM] * 15,
        name="back",
    )(*w1, probs, attg, vlow, dval, qlow, klow, lat, blu, blre, z, nrm, pd, pz, dk, lab)

    backward = [
        lax.ppermute(back_msg, "seq", [(i + k, i) for i in range(devices - k)])
        for k in range(1, reach + 1)
    ]

    piece_b = struct((half, depth, rows1, nv + nm), BF)
    own_b, sib_b = whole(
        partial(weight_kernel, devices=devices, depth=depth),
        [piece_b, piece_b],
        [pltpu.VMEM((width, nv + nm), BF)],
        n_in=6,
        name="weights",
    )(nlow, mlow, vgl, blu, bll, blre)

    piece_c = struct((half, ROWS_SMALL, TILE), F32)
    wide = ceil_div(nm, TILE) + 2
    tokens_grad, own_c, sib_c = pl.pallas_call(
        partial(last_kernel, reach=reach, devices=devices, dims=dims, seqs=seqs, nm=nm),
        grid=(blocks,),
        in_specs=[
            pl.BlockSpec((steps, dims * SUBS, TILE), lambda i: (0, 0, i)), tile_block,
            tile_block, lane_block(count), fixed((count, TILE)), lane_block(3 * dims),
            lane_block(72), lane_block(dims * SUBS),
        ] + [lane_block(msg_rows)] * reach + [
            fixed((count, width)), fixed((count, width)), fixed((72, width)), fixed((8, width)),
            fixed((8, nv)), fixed((8, width)), fixed((8, nv)), fixed((8, TILE)),
        ],
        out_specs=[
            fixed((count, width)), fixed(piece_c.shape), fixed(piece_c.shape),
        ],
        out_shape=[struct((count, width), F32), piece_c, piece_c],
        scratch_shapes=[
            pltpu.VMEM((dims * SUBS, TILE), F32), pltpu.VMEM((SUBS, TILE), F32),
            pltpu.VMEM((count, TILE), F32), pltpu.VMEM((count, width), F32),
            pltpu.VMEM((72, width), F32), pltpu.VMEM((8, nv), F32),
            pltpu.VMEM((8, wide * TILE), F32),
        ] + arrivals,
        compiler_params=PARAMS,
        name="last",
    )(
        sp, nrm, gs, gnp, lab, dk, pd, ach, *backward, tok, gin, pd, v512, v1024, w512, w1024, w128
    )

    sum_a = join(deal(across(fold(own_a, sib_a, BF)), depth))
    attend_grad, down_grad, up_grad = whole(
        partial(spread_a_kernel, depth=depth, r2=rows2, width=width),
        [
            struct((nv // devices, width), F32), struct((nf // devices, width), F32),
            struct((held, nf), F32),
        ],
        [pltpu.VMEM((depth,) + piece_a.shape[2:], F32)],
        n_in=depth,
        name="spread_a",
    )(*sum_a)
    sum_b = join(deal(across(fold(own_b, sib_b, BF)), depth))
    value_grad, mix_grad = whole(
        partial(spread_b_kernel, depth=depth),
        [struct((held, nv), F32), struct((held, nm), F32)],
        [pltpu.VMEM((depth,) + piece_b.shape[2:], F32)],
        n_in=depth,
        name="spread_b",
    )(*sum_b)
    parts_c = across(fold(own_c, sib_c, F32))
    shard_c = whole(total_kernel, struct(piece_c.shape[1:], F32), n_in=half, name="total")(*parts_c)
    all_c = [shard_c] + [hop(shard_c, "grp", k) for k in range(1, depth)]
    most = max(nt for _, _, _, nt in plan)
    dec_grad, flat_grad = whole(
        partial(final_kernel, depth=depth, plan=plan, held=held, dims=dims),
        [struct((held, 4 * dims), F32), struct((16, most * TILE), F32)],
        [pltpu.VMEM((depth,) + piece_c.shape[1:], F32)],
        n_in=depth,
        name="final",
    )(*all_c)
    grads = [flat_grad[j, :n] for j, (_, _, n, _) in enumerate(plan)]
    value_b, up_b, mix_b, first_g, omega, second_g, down_b, g0, g1, qoff, posb = grads
    return (
        out.reshape(tokens.shape),
        tokens_grad.reshape(tokens.shape),
        first_g,
        value_grad,
        value_b,
        dec_grad[:, 0:dims],
        dec_grad[:, dims : 2 * dims],
        dec_grad[:, 2 * dims : 3 * dims],
        dec_grad[:, 3 * dims :],
        omega,
        mix_grad,
        mix_b,
        jnp.stack([g0, g1]),
        qoff,
        posb,
        attend_grad,
        second_g,
        up_grad,
        up_b,
        down_grad,
        down_b,
    )


def solution(mesh):
    vec, mat = P("seq"), P("seq", None)
    data = P("grp", "seq", None)
    params = (
        vec, mat, vec, mat, mat, mat, mat, vec, mat, vec, P(None, "seq"), vec, vec, mat, vec, mat,
        vec, mat, vec,
    )
    return jax.shard_map(
        per_device,
        mesh=mesh,
        in_specs=(data, P("grp", "seq"), data) + params,
        out_specs=(data, data) + params,
        check_vma=False,
    )
```

time: 884 us -> 305 us (0.35); the launches traced: 873 us -> 304 us
  other arithmetic: 226 us -> 1.78 us
  local copies, waits for them, and re-layouts: 222 us -> 32.6 us
  matrix products: 188 us -> 0 us
  Pallas kernels: 0 us -> 135 us
  blocking collectives: 157 us -> 26.1 us
  starting transfers between devices: 4.03 us -> 56.2 us
  between operations: 20.8 us -> 1.13 us
    dot_general x30 -> x0, matrix products: 174 us -> none  [the longest x3 42.6 us: smooth_local(): jnp.einsum('snk,snkc,kcj->sncj', tail, pieces, to_end, precision=HIGH)]
    pallas_call x0 -> x19, Pallas kernels: none -> 135 us  [the longest x1 30.2 us: per_device(): whole(partial(middle_kernel, devices=devices, depth=depth, dims=dims), [s...]
    scatter-add x2 -> x0, other arithmetic: 116 us -> none  [the longest x1 114 us: bias_table(): return jnp.where(offset >= 0, position[jnp.clip(offset, 0, size - 1)], 0.0)]
    gather x3 -> x0, local copies, waits for them, and re-layouts: 98.3 us -> none  [the longest x2 97.3 us: bias_table(): return jnp.where(offset >= 0, position[jnp.clip(offset, 0, size - 1)], 0.0)]
    all_gather x9 -> x1, blocking collectives: 89.3 us -> 26.1 us  [per_device(): small = lax.all_gather(placed, 'seq', axis=0, tiled=False)]
    ppermute x1 -> x45, starting transfers between devices: 2.87 us -> 56.2 us  [the longest x41 49.5 us: hop(): return lax.ppermute(x, axis, [(i, i ^ k) for i in range(length)])]
    ppermute x1 -> x45, waiting for transfers between devices: 0.01 us -> 51.5 us  [the longest x41 44.3 us: hop(): return lax.ppermute(x, axis, [(i, i ^ k) for i in range(length)])]
    unnamed x2 -> x0, blocking collectives: 48.2 us -> none
  transfers between devices with their start and end apart: 19 -> 45, of which waited for: 2 -> 12; matrix products, arithmetic and copies ran while one was open for 70% -> 7% of each run, Pallas kernels for 0% -> 34%
where the time goes in v1:
time: 305 us; the launch traced here: 304 us
  Pallas kernels  135 us (44%)
  starting transfers between devices  56.2 us (18%)
  waiting for transfers between devices  51.5 us (17%)
  local copies, waits for them, and re-layouts  32.6 us (11%)
  blocking collectives  26.1 us (9%)
    ppermute x41, starting transfers between devices, hop(): return lax.ppermute(x, axis, [(i, i ^ k) for i in range(length)])  49.5 us
    ppermute x41, waiting for transfers between devices, hop(): return lax.ppermute(x, axis, [(i, i ^ k) for i in range(length)])  44.3 us
    pallas_call x1, Pallas kernels, per_device(): whole(partial(middle_kernel, devices=devices, depth=depth, dims=dims), [s...  30.2 us
    all_gather x1, blocking collectives, per_device(): small = lax.all_gather(placed, 'seq', axis=0, tiled=False)  26.1 us
    pallas_call x1, Pallas kernels, per_device(): pl.pallas_call(partial(last_kernel, reach=reach, devices=devices, dims=di...  20.3 us
    unnamed x113, local copies, waits for them, and re-layouts  17.6 us
    pallas_call x1, Pallas kernels, per_device(): whole(partial(back_kernel, devices=devices, dims=dims), [struct((count, n...  16.3 us
    pallas_call x1, Pallas kernels, per_device(): whole(partial(front_kernel, devices=devices), [struct((count, nv), BF), s...  15 us
  transfers between devices with their start and end apart: 45, of which 12 were waited for; matrix products, arithmetic and copies ran while one was open for 7% of the time, Pallas kernels for 34%

profile of v1, /device:TPU:0, one launch (start us, length us, event | category | flops | bytes accessed | tf_op | source)
XLA Modules:
  0.0 304.0 jit_solution(687298296473968008)
XLA Ops:
  1.8 4.0 %collective-permute-start.5 = (bf16[192,1024]{1,0:T(8,128)(2,1)S(1)}, bf16[192,1024]{1,0:T(8,128)(2,1)S(1)}, u32[]{:S(2)}, u32[]{:S(2)}) collective-permute-start(bf16[192,1024]{1,0:T(8,128)(2,1)S(1)} %pad_maximum_fusion.refs_0_), channel_id=1, source_target_pairs={{0,6},{1,7},{2,4},{3,5},{4,2},{5,3},{6,0},{7,1},{8,14},{9,15},{10,... | collective-permute-start | bytes 1179656 | tf_op jit(solution)/shard_map/ppermute | solution.py:799
  8.2 1.6 collective-permute-start.12
  10.6 6.1 %concatenate.18 = bf16[896]{0:T(1024)(128)(2,1)S(1)} concatenate(bf16[128]{0:T(256)(128)(2,1)} %param.27, bf16[128]{0:T(256)(128)(2,1)} %param.41, bf16[272]{0:T(512)(128)(2,1)} %param.34, bf16[64]{0:T(256)(128)(2,1)} %param.25, bf16[64]{0:T(256)(128)(2,1)} %param.32, bf16[64]{0:T(256)(128)(2,1)} %param.39, bf16[64]{0:T(256)(128)(2,1)} %param.43, ...), dimensions={0} | concatenate | bytes 3584 | tf_op jit(solution)/shard_map/concatenate | solution.py:938
  19.1 1.6 place.1
  20.7 26.1 %all-gather = f32[704,128]{1,0:T(8,128)} all-gather(f32[88,128]{1,0:T(8,128)} %place.1), channel_id=2, replica_groups=mesh['grp'=4,'seq'=8] {'seq'}, dimensions={0}, use_global_device_ids=true | all-gather | bytes 405504 | tf_op jit(solution)/shard_map/all_gather | solution.py:943
  46.7 5.5 %head.1 = (f32[72,512]{1,0:T(8,128)}, f32[8,1024]{1,0:T(8,128)}, f32[8,128]{1,0:T(8,128)}, f32[8,2176]{1,0:T(8,128)}, f32[48,512]{1,0:T(8,128)}, /*index=5*/f32[...) custom-call(f32[8,88,128]{2,1,0:T(8,128)} %bitcast.28, ...), custom_call_target="tpu_custom_call" | custom-call | tf_op jit(solution)/shard_map/head/pallas_call | solution.py:955
  52.3 2.5 collective-permute-start.15
  54.8 2.5 collective-permute-done.15.refs_6_
  59.9 5.8 %collective-permute-start.8 = (bf16[64,3200]{1,0:T(8,128)(2,1)S(1)}, bf16[64,3200]{1,0:T(8,128)(2,1)S(1)}, u32[]{:S(2)}, u32[]{:S(2)}) collective-permute-start(bf16[64,3200]{1,0:T(8,128)(2,1)S(1)} %constant_dynamic-update-slice_fusion.refs_0_), channel_id=1, source_target_pairs={{0,2},{1,3},{2,0},{3,1},{4,6},{5,7},{6,4},{7,5},{8,10},{9,11},{10,... | collective-permute-start | bytes 1228808 | tf_op jit(solution)/shard_map/ppermute | solution.py:799
  66.5 9.3 %collective-permute-done.8.refs_2_ = bf16[64,3200]{1,0:T(8,128)(2,1)S(1)} collective-permute-done((bf16[64,3200]{1,0:T(8,128)(2,1)S(1)}, bf16[64,3200]{1,0:T(8,128)(2,1)S(1)}, u32[]{:S(2)}, u32[]{:S(2)}) %collective-permute-start.8) | collective-permute-done | bytes 409632 | tf_op jit(solution)/shard_map/ppermute | solution.py:799
  75.9 8.1 %collective-permute-done.1.refs_2_ = bf16[192,1024]{1,0:T(8,128)(2,1)S(1)} collective-permute-done((bf16[192,1024]{1,0:T(8,128)(2,1)S(1)}, bf16[192,1024]{1,0:T(8,128)(2,1)S(1)}, u32[]{:S(2)}, u32[]{:S(2)}) %collective-permute-start.1) | collective-permute-done | bytes 393248 | tf_op jit(solution)/shard_map/ppermute | solution.py:799
  85.0 10.1 %scan.1 = (f32[512,512]{1,0:T(8,128)}, bf16[512,512]{1,0:T(8,128)(2,1)}, f32[64,128,512]{2,1,0:T(8,128)}) custom-call(f32[4,512,128]{2,1,0:T(8,128)} %get-tuple-element.96.refs_0_.refs_18_.refs_1_, f32[512,128]{1,0:T(8,128)} %get-tuple-element.97.refs_1_.refs_13_.refs_22_.refs_4_, f32[48,512]{1,0:T(8,128)} %get-tuple-element.98.refs_2_.refs_21_.refs_5_, ...), custom_call_target="tpu_custom_call" | custom-call | tf_op jit(solution)/shard_map/scan/pallas_call | solution.py:982
  95.9 15.0 %front.1 = (bf16[512,1024]{1,0:T(8,128)(2,1)}, bf16[512,1024]{1,0:T(8,128)(2,1)}, f32[512,512]{1,0:T(8,128)}, f32[512,512]{1,0:T(8,128)}, f32[512,128]{1,0:T(8,1...) custom-call(bf16[64,3200]{1,0:T(8,128)(2,1)} %copy-done, ...), custom_call_target="tpu_custom_call" | custom-call | tf_op jit(solution)/shard_map/front/pallas_call | solution.py:1008
  112.1 30.2 %middle.1 = (f32[512,512]{1,0:T(8,128)}, f32[512,512]{1,0:T(8,128)}, bf16[512,1024]{1,0:T(8,128)(2,1)}, bf16[512,512]{1,0:T(8,128)(2,1)}, bf16[512,1536]{1,0:T(8...) custom-call(bf16[192,1024]{1,0:T(8,128)(2,1)} %copy-done.9, ...), custom_call_target="tpu_custom_call" | custom-call | tf_op jit(solution)/shard_map/middle/pallas_call | solution.py:1024
  142.6 16.3 %back.1 = (bf16[512,1024]{1,0:T(8,128)(2,1)}, bf16[512,128]{1,0:T(8,128)(2,1)}, f32[4,512,128]{2,1,0:T(8,128)}, f32[512,512]{1,0:T(8,128)}, f32[8,512]{1,0:T(8,1...) custom-call(bf16[64,3200]{1,0:T(8,128)(2,1)} %copy-done, ...), custom_call_target="tpu_custom_call" | custom-call | tf_op jit(solution)/shard_map/back/pallas_call | solution.py:1043
  158.9 11.5 %weights.1 = (bf16[4,4,16,3200]{3,2,1,0:T(8,128)(2,1)}, bf16[4,4,16,3200]{3,2,1,0:T(8,128)(2,1)}) custom-call(bf16[512,512]{1,0:T(8,128)(2,1)} %get-tuple-element.95.refs_8_.nlow, bf16[512,512]{1,0:T(8,128)(2,1)} %get-tuple-element.102.refs_9_.mlow, bf16[512,1024]{1,0:T(8,128)(2,1)} %get-tuple-element.141.vgl, ...), custom_call_target="tpu_custom_call" | custom-call | tf_op jit(solution)/shard_map/weights/pallas_call | solution.py:1065
  172.1 1.5 collective-permute-start.16
  173.6 3.6 %collective-permute-done.17.refs_9_ = bf16[80,512]{1,0:T(8,128)(2,1)S(1)} collective-permute-done((bf16[80,512]{1,0:T(8,128)(2,1)S(1)}, bf16[80,512]{1,0:T(8,128)(2,1)S(1)}, u32[]{:S(2)}, u32[]{:S(2)}) %collective-permute-start.17) | collective-permute-done | bytes 81952 | tf_op jit(solution)/shard_map/ppermute | solution.py:1060
  177.9 20.3 %last.1 = (f32[512,512]{1,0:T(8,128)}, f32[4,88,128]{2,1,0:T(8,128)}, f32[4,88,128]{2,1,0:T(8,128)}) custom-call(f32[64,128,512]{2,1,0:T(8,128)} %get-tuple-element.112.refs_0_, f32[4,512,128]{2,1,0:T(8,128)} %get-tuple-element.96.refs_0_.refs_18_.refs_1_, f32[4,512,128]{2,1,0:T(8,128)} %get-tuple-element.123.refs_2_, ...), custom_call_target="tpu_custom_call" | custom-call | tf_op jit(solution)/shard_map/last/pallas_call | solution.py:1075
  198.1 1.7 collective-permute-start.18
  201.0 3.3 %fold.5 = (f32[4,48,1024]{2,1,0:T(8,128)}, bf16[4,48,1024]{2,1,0:T(8,128)(2,1)}, bf16[4,48,1024]{2,1,0:T(8,128)(2,1)}, bf16[4,48,1024]{2,1,0:T(8,128)(2,1)}) custom-call(bf16[4,4,48,1024]{3,2,1,0:T(8,128)(2,1)} %get-tuple-element.156.own, bf16[4,4,48,1024]{3,2,1,0:T(8,128)(2,1)} %copy-done.10), custom_call_target="tpu_custom_call" | custom-call | tf_op jit(solution)/shard_map/fold/pallas_call | solution.py:810
  204.3 2.6 collective-permute-start.36
  207.6 1.7 fold.3
  209.3 2.0 collective-permute-start.20
  212.8 5.1 %collective-permute-done.19.refs_1_ = f32[88,128]{1,0:T(8,128)S(1)} collective-permute-done((f32[88,128]{1,0:T(8,128)}, f32[88,128]{1,0:T(8,128)S(1)}, u32[]{:S(2)}, u32[]{:S(2)}) %collective-permute-start.19) | collective-permute-done | bytes 45088 | tf_op jit(solution)/shard_map/ppermute | solution.py:799
  217.9 1.7 collective-permute-done.21.refs_3_
  220.2 1.5 total.1.refs_0_
  221.6 3.7 %collective-permute-start.24 = (f32[88,128]{1,0:T(8,128)}, f32[88,128]{1,0:T(8,128)S(1)}, u32[]{:S(2)}, u32[]{:S(2)}) collective-permute-start(f32[88,128]{1,0:T(8,128)} %total.1.refs_0_), channel_id=1, source_target_pairs={{0,24},{8,16},{16,8},{24,0},{1,25},{9,17},{17,9},{25,1},{2,26},{10... | collective-permute-start | bytes 135176 | tf_op jit(solution)/shard_map/ppermute | solution.py:799
  226.0 1.7 collective-permute-done.24.refs_3_
  227.7 2.8 collective-permute-done.23.refs_2_
  231.8 1.7 final.1
  233.7 1.5 collective-permute-start.38
  236.4 3.3 %fold.4 = (f32[4,16,3200]{2,1,0:T(8,128)}, bf16[4,16,3200]{2,1,0:T(8,128)(2,1)}, bf16[4,16,3200]{2,1,0:T(8,128)(2,1)}, bf16[4,16,3200]{2,1,0:T(8,128)(2,1)}) custom-call(bf16[4,4,16,3200]{3,2,1,0:T(8,128)(2,1)} %get-tuple-element.143.own, bf16[4,4,16,3200]{3,2,1,0:T(8,128)(2,1)} %copy-done.1), custom_call_target="tpu_custom_call" | custom-call | tf_op jit(solution)/shard_map/fold/pallas_call | solution.py:810
  239.7 1.7 collective-permute-start.26
  241.9 1.5 collective-permute-start.28
  244.7 9.5 %collective-permute-done.37.refs_2_ = bf16[4,48,1024]{2,1,0:T(8,128)(2,1)S(1)} collective-permute-done((bf16[4,48,1024]{2,1,0:T(8,128)(2,1)}, bf16[4,48,1024]{2,1,0:T(8,128)(2,1)S(1)}, u32[]{:S(2)}, u32[]{:S(2)}) %collective-permute-start.37) | collective-permute-done | bytes 393248 | tf_op jit(solution)/shard_map/ppermute | solution.py:799
  255.1 2.5 deal.3
  257.6 2.3 collective-permute-start.40
  260.0 2.1 collective-permute-start.41
  263.3 5.1 %collective-permute-done.27.refs_2_ = bf16[4,16,3200]{2,1,0:T(8,128)(2,1)S(1)} collective-permute-done((bf16[4,16,3200]{2,1,0:T(8,128)(2,1)}, bf16[4,16,3200]{2,1,0:T(8,128)(2,1)S(1)}, u32[]{:S(2)}, u32[]{:S(2)}) %collective-permute-start.27) | collective-permute-done | bytes 409632 | tf_op jit(solution)/shard_map/ppermute | solution.py:799
  269.3 2.6 deal.2
  273.4 2.9 collective-permute-start.31
  277.0 1.8 join.3.refs_0_
  284.8 3.5 %collective-permute-start.42 = (bf16[48,1024]{1,0:T(8,128)(2,1)}, bf16[48,1024]{1,0:T(8,128)(2,1)S(1)}, u32[]{:S(2)}, u32[]{:S(2)}) collective-permute-start(bf16[48,1024]{1,0:T(8,128)(2,1)} %join.3.refs_0_), channel_id=1, source_target_pairs={{0,8},{8,0},{16,24},{24,16},{1,9},{9,1},{17,25},{25,17},{2,10},{10... | collective-permute-start | bytes 294920 | tf_op jit(solution)/shard_map/ppermute | solution.py:799
  289.0 1.8 join.2.refs_0_
  292.5 2.7 collective-permute-start.32
  297.8 2.0 spread_a.1
  301.9 2.0 spread_b.1
  (188 shorter events, 42.9 us)
Async XLA Ops:
  1.8 93.4 %copy-start.9 = (bf16[192,1024]{1,0:T(8,128)(2,1)}, bf16[192,1024]{1,0:T(8,128)(2,1)S(1)}, u32[]{:S(2)}) copy-start(bf16[192,1024]{1,0:T(8,128)(2,1)S(1)} %pad_maximum_fusion.refs_0_) | copy-start | bytes 1179652
  1.8 63.9 %collective-permute-start.5 = (bf16[192,1024]{1,0:T(8,128)(2,1)S(1)}, bf16[192,1024]{1,0:T(8,128)(2,1)S(1)}, u32[]{:S(2)}, u32[]{:S(2)}) collective-permute-start(bf16[192,1024]{1,0:T(8,128)(2,1)S(1)} %pad_maximum_fusion.refs_0_), channel_id=1, source_target_pairs={{0,6},{1,7},{2,4},{3,5},{4,2},{5,3},{6,0},{7,1},{8,14},{9,15},{10,... | collective-permute-start | bytes 1179656 | tf_op jit(solution)/shard_map/ppermute | solution.py:799
  5.7 60.5 %collective-permute-start.3 = (bf16[192,1024]{1,0:T(8,128)(2,1)S(1)}, bf16[192,1024]{1,0:T(8,128)(2,1)S(1)}, u32[]{:S(2)}, u32[]{:S(2)}) collective-permute-start(bf16[192,1024]{1,0:T(8,128)(2,1)S(1)} %pad_maximum_fusion.refs_0_), channel_id=1, source_target_pairs={{0,4},{1,5},{2,6},{3,7},{4,0},{5,1},{6,2},{7,3},{8,12},{9,13},{10,... | collective-permute-start | bytes 1179656 | tf_op jit(solution)/shard_map/ppermute | solution.py:799
  8.2 87.0 %copy-start = (bf16[64,3200]{1,0:T(8,128)(2,1)}, bf16[64,3200]{1,0:T(8,128)(2,1)S(1)}, u32[]{:S(2)}) copy-start(bf16[64,3200]{1,0:T(8,128)(2,1)S(1)} %constant_dynamic-update-slice_fusion.refs_0_) | copy-start | bytes 1228804
  8.2 57.5 %collective-permute-start.12 = (bf16[64,3200]{1,0:T(8,128)(2,1)S(1)}, bf16[64,3200]{1,0:T(8,128)(2,1)S(1)}, u32[]{:S(2)}, u32[]{:S(2)}) collective-permute-start(bf16[64,3200]{1,0:T(8,128)(2,1)S(1)} %constant_dynamic-update-slice_fusion.refs_0_), channel_id=1, source_target_pairs={{0,6},{1,7},{2,4},{3,5},{4,2},{5,3},{6,0},{7,1},{8,14},{9,15},{10,... | collective-permute-start | bytes 1228808 | tf_op jit(solution)/shard_map/ppermute | solution.py:799
  9.7 56.4 %collective-permute-start.10 = (bf16[64,3200]{1,0:T(8,128)(2,1)S(1)}, bf16[64,3200]{1,0:T(8,128)(2,1)S(1)}, u32[]{:S(2)}, u32[]{:S(2)}) collective-permute-start(bf16[64,3200]{1,0:T(8,128)(2,1)S(1)} %constant_dynamic-update-slice_fusion.refs_0_), channel_id=1, source_target_pairs={{0,4},{1,5},{2,6},{3,7},{4,0},{5,1},{6,2},{7,3},{8,12},{9,13},{10,... | collective-permute-start | bytes 1228808 | tf_op jit(solution)/shard_map/ppermute | solution.py:799
  52.3 5.0 %collective-permute-start.15 = (bf16[80,512]{1,0:T(8,128)(2,1)}, bf16[80,512]{1,0:T(8,128)(2,1)S(1)}, u32[]{:S(2)}, u32[]{:S(2)}) collective-permute-start(bf16[80,512]{1,0:T(8,128)(2,1)} %get-tuple-element.101), channel_id=1, source_target_pairs={{0,2},{1,3},{2,4},{3,5},{4,6},{5,7},{8,10},{9,11},{10,12},{11,13},... | collective-permute-start | bytes 245768 | tf_op jit(solution)/shard_map/ppermute | solution.py:969
  57.3 2.6 collective-permute-start.14
  59.9 16.0 %collective-permute-start.8 = (bf16[64,3200]{1,0:T(8,128)(2,1)S(1)}, bf16[64,3200]{1,0:T(8,128)(2,1)S(1)}, u32[]{:S(2)}, u32[]{:S(2)}) collective-permute-start(bf16[64,3200]{1,0:T(8,128)(2,1)S(1)} %constant_dynamic-update-slice_fusion.refs_0_), channel_id=1, source_target_pairs={{0,2},{1,3},{2,0},{3,1},{4,6},{5,7},{6,4},{7,5},{8,10},{9,11},{10,... | collective-permute-start | bytes 1228808 | tf_op jit(solution)/shard_map/ppermute | solution.py:799
  65.6 45.4 %copy-start.15 = (bf16[192,1024]{1,0:T(8,128)(2,1)}, bf16[192,1024]{1,0:T(8,128)(2,1)S(1)}, u32[]{:S(2)}) copy-start(bf16[192,1024]{1,0:T(8,128)(2,1)S(1)} %collective-permute-done.5.refs_6_) | copy-start | bytes 1179652
  65.6 18.3 %collective-permute-start.7 = (bf16[64,3200]{1,0:T(8,128)(2,1)S(1)}, bf16[64,3200]{1,0:T(8,128)(2,1)S(1)}, u32[]{:S(2)}, u32[]{:S(2)}) collective-permute-start(bf16[64,3200]{1,0:T(8,128)(2,1)S(1)} %constant_dynamic-update-slice_fusion.refs_0_), channel_id=1, source_target_pairs={{0,1},{1,0},{2,3},{3,2},{4,5},{5,4},{6,7},{7,6},{8,9},{9,8},{10,11... | collective-permute-start | bytes 1228808 | tf_op jit(solution)/shard_map/ppermute | solution.py:799
  65.7 18.8 %collective-permute-start.13 = (bf16[64,3200]{1,0:T(8,128)(2,1)S(1)}, bf16[64,3200]{1,0:T(8,128)(2,1)S(1)}, u32[]{:S(2)}, u32[]{:S(2)}) collective-permute-start(bf16[64,3200]{1,0:T(8,128)(2,1)S(1)} %collective-permute-done.12.refs_6_), channel_id=1, source_target_pairs={{0,1},{1,0},{2,3},{3,2},{4,5},{5,4},{6,7},{7,6},{8,9},{9,8},{10,11... | collective-permute-start | bytes 1228808 | tf_op jit(solution)/shard_map/ppermute | solution.py:799
  66.2 18.4 %collective-permute-start.11 = (bf16[64,3200]{1,0:T(8,128)(2,1)S(1)}, bf16[64,3200]{1,0:T(8,128)(2,1)S(1)}, u32[]{:S(2)}, u32[]{:S(2)}) collective-permute-start(bf16[64,3200]{1,0:T(8,128)(2,1)S(1)} %collective-permute-done.10.refs_4_), channel_id=1, source_target_pairs={{0,1},{1,0},{2,3},{3,2},{4,5},{5,4},{6,7},{7,6},{8,9},{9,8},{10,11... | collective-permute-start | bytes 1228808 | tf_op jit(solution)/shard_map/ppermute | solution.py:799
  66.2 17.7 %collective-permute-start.1 = (bf16[192,1024]{1,0:T(8,128)(2,1)S(1)}, bf16[192,1024]{1,0:T(8,128)(2,1)S(1)}, u32[]{:S(2)}, u32[]{:S(2)}) collective-permute-start(bf16[192,1024]{1,0:T(8,128)(2,1)S(1)} %pad_maximum_fusion.refs_0_), channel_id=1, source_target_pairs={{0,2},{1,3},{2,0},{3,1},{4,6},{5,7},{6,4},{7,5},{8,10},{9,11},{10,... | collective-permute-start | bytes 1179656 | tf_op jit(solution)/shard_map/ppermute | solution.py:799
  75.9 19.3 %collective-permute-start.9 = (bf16[64,3200]{1,0:T(8,128)(2,1)S(1)}, bf16[64,3200]{1,0:T(8,128)(2,1)S(1)}, u32[]{:S(2)}, u32[]{:S(2)}) collective-permute-start(bf16[64,3200]{1,0:T(8,128)(2,1)S(1)} %collective-permute-done.8.refs_2_), channel_id=1, source_target_pairs={{0,1},{1,0},{2,3},{3,2},{4,5},{5,4},{6,7},{7,6},{8,9},{9,8},{10,11... | collective-permute-start | bytes 1228808 | tf_op jit(solution)/shard_map/ppermute | solution.py:799
  84.0 27.0 %collective-permute-start = (bf16[192,1024]{1,0:T(8,128)(2,1)S(1)}, bf16[192,1024]{1,0:T(8,128)(2,1)S(1)}, u32[]{:S(2)}, u32[]{:S(2)}) collective-permute-start(bf16[192,1024]{1,0:T(8,128)(2,1)S(1)} %pad_maximum_fusion.refs_0_), channel_id=1, source_target_pairs={{0,1},{1,0},{2,3},{3,2},{4,5},{5,4},{6,7},{7,6},{8,9},{9,8},{10,11... | collective-permute-start | bytes 1179656 | tf_op jit(solution)/shard_map/ppermute | solution.py:799
  84.0 27.0 %collective-permute-start.6 = (bf16[192,1024]{1,0:T(8,128)(2,1)S(1)}, bf16[192,1024]{1,0:T(8,128)(2,1)S(1)}, u32[]{:S(2)}, u32[]{:S(2)}) collective-permute-start(bf16[192,1024]{1,0:T(8,128)(2,1)S(1)} %collective-permute-done.5.refs_6_), channel_id=1, source_target_pairs={{0,1},{1,0},{2,3},{3,2},{4,5},{5,4},{6,7},{7,6},{8,9},{9,8},{10,11... | collective-permute-start | bytes 1179656 | tf_op jit(solution)/shard_map/ppermute | solution.py:799
  84.5 26.5 %collective-permute-start.4 = (bf16[192,1024]{1,0:T(8,128)(2,1)S(1)}, bf16[192,1024]{1,0:T(8,128)(2,1)S(1)}, u32[]{:S(2)}, u32[]{:S(2)}) collective-permute-start(bf16[192,1024]{1,0:T(8,128)(2,1)S(1)} %collective-permute-done.3.refs_4_), channel_id=1, source_target_pairs={{0,1},{1,0},{2,3},{3,2},{4,5},{5,4},{6,7},{7,6},{8,9},{9,8},{10,11... | collective-permute-start | bytes 1179656 | tf_op jit(solution)/shard_map/ppermute | solution.py:799
  84.6 26.4 %collective-permute-start.2 = (bf16[192,1024]{1,0:T(8,128)(2,1)S(1)}, bf16[192,1024]{1,0:T(8,128)(2,1)S(1)}, u32[]{:S(2)}, u32[]{:S(2)}) collective-permute-start(bf16[192,1024]{1,0:T(8,128)(2,1)S(1)} %collective-permute-done.1.refs_2_), channel_id=1, source_target_pairs={{0,1},{1,0},{2,3},{3,2},{4,5},{5,4},{6,7},{7,6},{8,9},{9,8},{10,11... | collective-permute-start | bytes 1179656 | tf_op jit(solution)/shard_map/ppermute | solution.py:799
  142.3 57.5 %collective-permute-start.35 = (bf16[4,4,48,1024]{3,2,1,0:T(8,128)(2,1)}, bf16[4,4,48,1024]{3,2,1,0:T(8,128)(2,1)S(1)}, u32[]{:S(2)}, u32[]{:S(2)}) collective-permute-start(bf16[4,4,48,1024]{3,2,1,0:T(8,128)(2,1)} %get-tuple-element.157), channel_id=1, source_target_pairs={{0,1},{1,0},{2,3},{3,2},{4,5},{5,4},{6,7},{7,6},{8,9},{9,8},{10,11... | collective-permute-start | bytes 4718600 | tf_op jit(solution)/shard_map/ppermute | solution.py:799
  170.4 64.8 %collective-permute-start.25 = (bf16[4,4,16,3200]{3,2,1,0:T(8,128)(2,1)}, bf16[4,4,16,3200]{3,2,1,0:T(8,128)(2,1)S(1)}, u32[]{:S(2)}, u32[]{:S(2)}) collective-permute-start(bf16[4,4,16,3200]{3,2,1,0:T(8,128)(2,1)} %get-tuple-element.144), channel_id=1, source_target_pairs={{0,1},{1,0},{2,3},{3,2},{4,5},{5,4},{6,7},{7,6},{8,9},{9,8},{10,11... | collective-permute-start | bytes 4915208 | tf_op jit(solution)/shard_map/ppermute | solution.py:799
  170.8 6.4 %collective-permute-start.17 = (bf16[80,512]{1,0:T(8,128)(2,1)S(1)}, bf16[80,512]{1,0:T(8,128)(2,1)S(1)}, u32[]{:S(2)}, u32[]{:S(2)}) collective-permute-start(bf16[80,512]{1,0:T(8,128)(2,1)S(1)} %copy-done.51), channel_id=1, source_target_pairs={{2,0},{3,1},{4,2},{5,3},{6,4},{7,5},{10,8},{11,9},{12,10},{13,11},... | collective-permute-start | bytes 245768 | tf_op jit(solution)/shard_map/ppermute | solution.py:1060
  172.1 5.1 %collective-permute-start.16 = (bf16[80,512]{1,0:T(8,128)(2,1)S(1)}, bf16[80,512]{1,0:T(8,128)(2,1)S(1)}, u32[]{:S(2)}, u32[]{:S(2)}) collective-permute-start(bf16[80,512]{1,0:T(8,128)(2,1)S(1)} %copy-done.51), channel_id=1, source_target_pairs={{1,0},{2,1},{3,2},{4,3},{5,4},{6,5},{7,6},{9,8},{10,9},{11,10},{12... | collective-permute-start | bytes 245768 | tf_op jit(solution)/shard_map/ppermute | solution.py:1060
  198.1 8.8 %collective-permute-start.18 = (f32[4,88,128]{2,1,0:T(8,128)}, f32[4,88,128]{2,1,0:T(8,128)S(1)}, u32[]{:S(2)}, u32[]{:S(2)}) collective-permute-start(f32[4,88,128]{2,1,0:T(8,128)} %get-tuple-element.135), channel_id=1, source_target_pairs={{0,1},{1,0},{2,3},{3,2},{4,5},{5,4},{6,7},{7,6},{8,9},{9,8},{10,11... | collective-permute-start | bytes 540680 | tf_op jit(solution)/shard_map/ppermute | solution.py:799
  204.3 37.6 %collective-permute-start.36 = (bf16[4,48,1024]{2,1,0:T(8,128)(2,1)}, bf16[4,48,1024]{2,1,0:T(8,128)(2,1)S(1)}, u32[]{:S(2)}, u32[]{:S(2)}) collective-permute-start(bf16[4,48,1024]{2,1,0:T(8,128)(2,1)} %get-tuple-element.159), channel_id=1, source_target_pairs={{0,2},{1,3},{2,0},{3,1},{4,6},{5,7},{6,4},{7,5},{8,10},{9,11},{10,... | collective-permute-start | bytes 1179656 | tf_op jit(solution)/shard_map/ppermute | solution.py:799
  209.3 8.6 %collective-permute-start.19 = (f32[88,128]{1,0:T(8,128)}, f32[88,128]{1,0:T(8,128)S(1)}, u32[]{:S(2)}, u32[]{:S(2)}) collective-permute-start(f32[88,128]{1,0:T(8,128)} %get-tuple-element.137), channel_id=1, source_target_pairs={{0,2},{1,3},{2,0},{3,1},{4,6},{5,7},{6,4},{7,5},{8,10},{9,11},{10,... | collective-permute-start | bytes 135176 | tf_op jit(solution)/shard_map/ppermute | solution.py:799
  209.3 8.6 %collective-permute-start.20 = (f32[88,128]{1,0:T(8,128)}, f32[88,128]{1,0:T(8,128)S(1)}, u32[]{:S(2)}, u32[]{:S(2)}) collective-permute-start(f32[88,128]{1,0:T(8,128)} %get-tuple-element.138), channel_id=1, source_target_pairs={{0,4},{1,5},{2,6},{3,7},{4,0},{5,1},{6,2},{7,3},{8,12},{9,13},{10,... | collective-permute-start | bytes 135176 | tf_op jit(solution)/shard_map/ppermute | solution.py:799
  211.3 8.2 %collective-permute-start.21 = (f32[88,128]{1,0:T(8,128)}, f32[88,128]{1,0:T(8,128)S(1)}, u32[]{:S(2)}, u32[]{:S(2)}) collective-permute-start(f32[88,128]{1,0:T(8,128)} %get-tuple-element.139), channel_id=1, source_target_pairs={{0,6},{1,7},{2,4},{3,5},{4,2},{5,3},{6,0},{7,1},{8,14},{9,15},{10,... | collective-permute-start | bytes 135176 | tf_op jit(solution)/shard_map/ppermute | solution.py:799
  221.6 6.1 %collective-permute-start.24 = (f32[88,128]{1,0:T(8,128)}, f32[88,128]{1,0:T(8,128)S(1)}, u32[]{:S(2)}, u32[]{:S(2)}) collective-permute-start(f32[88,128]{1,0:T(8,128)} %total.1.refs_0_), channel_id=1, source_target_pairs={{0,24},{8,16},{16,8},{24,0},{1,25},{9,17},{17,9},{25,1},{2,26},{10... | collective-permute-start | bytes 135176 | tf_op jit(solution)/shard_map/ppermute | solution.py:799
  225.4 5.2 %collective-permute-start.23 = (f32[88,128]{1,0:T(8,128)}, f32[88,128]{1,0:T(8,128)S(1)}, u32[]{:S(2)}, u32[]{:S(2)}) collective-permute-start(f32[88,128]{1,0:T(8,128)} %total.1.refs_0_), channel_id=1, source_target_pairs={{0,16},{8,24},{16,0},{24,8},{1,17},{9,25},{17,1},{25,9},{2,18},{10... | collective-permute-start | bytes 135176 | tf_op jit(solution)/shard_map/ppermute | solution.py:799
  225.4 5.2 %collective-permute-start.22 = (f32[88,128]{1,0:T(8,128)}, f32[88,128]{1,0:T(8,128)S(1)}, u32[]{:S(2)}, u32[]{:S(2)}) collective-permute-start(f32[88,128]{1,0:T(8,128)} %total.1.refs_0_), channel_id=1, source_target_pairs={{0,8},{8,0},{16,24},{24,16},{1,9},{9,1},{17,25},{25,17},{2,10},{10... | collective-permute-start | bytes 135176 | tf_op jit(solution)/shard_map/ppermute | solution.py:799
  233.4 20.8 %collective-permute-start.37 = (bf16[4,48,1024]{2,1,0:T(8,128)(2,1)}, bf16[4,48,1024]{2,1,0:T(8,128)(2,1)S(1)}, u32[]{:S(2)}, u32[]{:S(2)}) collective-permute-start(bf16[4,48,1024]{2,1,0:T(8,128)(2,1)} %get-tuple-element.160), channel_id=1, source_target_pairs={{0,4},{1,5},{2,6},{3,7},{4,0},{5,1},{6,2},{7,3},{8,12},{9,13},{10,... | collective-permute-start | bytes 1179656 | tf_op jit(solution)/shard_map/ppermute | solution.py:799
  233.7 20.5 %collective-permute-start.38 = (bf16[4,48,1024]{2,1,0:T(8,128)(2,1)}, bf16[4,48,1024]{2,1,0:T(8,128)(2,1)S(1)}, u32[]{:S(2)}, u32[]{:S(2)}) collective-permute-start(bf16[4,48,1024]{2,1,0:T(8,128)(2,1)} %get-tuple-element.161), channel_id=1, source_target_pairs={{0,6},{1,7},{2,4},{3,5},{4,2},{5,3},{6,0},{7,1},{8,14},{9,15},{10,... | collective-permute-start | bytes 1179656 | tf_op jit(solution)/shard_map/ppermute | solution.py:799
  239.7 20.2 %collective-permute-start.26 = (bf16[4,16,3200]{2,1,0:T(8,128)(2,1)}, bf16[4,16,3200]{2,1,0:T(8,128)(2,1)S(1)}, u32[]{:S(2)}, u32[]{:S(2)}) collective-permute-start(bf16[4,16,3200]{2,1,0:T(8,128)(2,1)} %get-tuple-element.146), channel_id=1, source_target_pairs={{0,2},{1,3},{2,0},{3,1},{4,6},{5,7},{6,4},{7,5},{8,10},{9,11},{10,... | collective-permute-start | bytes 1228808 | tf_op jit(solution)/shard_map/ppermute | solution.py:799
  241.5 26.9 %collective-permute-start.27 = (bf16[4,16,3200]{2,1,0:T(8,128)(2,1)}, bf16[4,16,3200]{2,1,0:T(8,128)(2,1)S(1)}, u32[]{:S(2)}, u32[]{:S(2)}) collective-permute-start(bf16[4,16,3200]{2,1,0:T(8,128)(2,1)} %get-tuple-element.147), channel_id=1, source_target_pairs={{0,4},{1,5},{2,6},{3,7},{4,0},{5,1},{6,2},{7,3},{8,12},{9,13},{10,... | collective-permute-start | bytes 1228808 | tf_op jit(solution)/shard_map/ppermute | solution.py:799
  241.9 26.6 %collective-permute-start.28 = (bf16[4,16,3200]{2,1,0:T(8,128)(2,1)}, bf16[4,16,3200]{2,1,0:T(8,128)(2,1)S(1)}, u32[]{:S(2)}, u32[]{:S(2)}) collective-permute-start(bf16[4,16,3200]{2,1,0:T(8,128)(2,1)} %get-tuple-element.148), channel_id=1, source_target_pairs={{0,6},{1,7},{2,4},{3,5},{4,2},{5,3},{6,0},{7,1},{8,14},{9,15},{10,... | collective-permute-start | bytes 1228808 | tf_op jit(solution)/shard_map/ppermute | solution.py:799
  257.6 15.7 %collective-permute-start.39 = (bf16[48,1024]{1,0:T(8,128)(2,1)}, bf16[48,1024]{1,0:T(8,128)(2,1)S(1)}, u32[]{:S(2)}, u32[]{:S(2)}) collective-permute-start(bf16[48,1024]{1,0:T(8,128)(2,1)} %get-tuple-element.163), channel_id=1, source_target_pairs={{0,8},{8,0},{16,24},{24,16},{1,9},{9,1},{17,25},{25,17},{2,10},{10... | collective-permute-start | bytes 294920 | tf_op jit(solution)/shard_map/ppermute | solution.py:799
  257.6 18.7 %collective-permute-start.40 = (bf16[48,1024]{1,0:T(8,128)(2,1)}, bf16[48,1024]{1,0:T(8,128)(2,1)S(1)}, u32[]{:S(2)}, u32[]{:S(2)}) collective-permute-start(bf16[48,1024]{1,0:T(8,128)(2,1)} %get-tuple-element.164), channel_id=1, source_target_pairs={{0,16},{8,24},{16,0},{24,8},{1,17},{9,25},{17,1},{25,9},{2,18},{10... | collective-permute-start | bytes 294920 | tf_op jit(solution)/shard_map/ppermute | solution.py:799
  260.0 16.3 %collective-permute-start.41 = (bf16[48,1024]{1,0:T(8,128)(2,1)}, bf16[48,1024]{1,0:T(8,128)(2,1)S(1)}, u32[]{:S(2)}, u32[]{:S(2)}) collective-permute-start(bf16[48,1024]{1,0:T(8,128)(2,1)} %get-tuple-element.165), channel_id=1, source_target_pairs={{0,24},{8,16},{16,8},{24,0},{1,25},{9,17},{17,9},{25,1},{2,26},{10... | collective-permute-start | bytes 294920 | tf_op jit(solution)/shard_map/ppermute | solution.py:799
  271.9 12.9 %collective-permute-start.29 = (bf16[16,3200]{1,0:T(8,128)(2,1)}, bf16[16,3200]{1,0:T(8,128)(2,1)S(1)}, u32[]{:S(2)}, u32[]{:S(2)}) collective-permute-start(bf16[16,3200]{1,0:T(8,128)(2,1)} %get-tuple-element.150), channel_id=1, source_target_pairs={{0,8},{8,0},{16,24},{24,16},{1,9},{9,1},{17,25},{25,17},{2,10},{10... | collective-permute-start | bytes 307208 | tf_op jit(solution)/shard_map/ppermute | solution.py:799
  271.9 16.4 %collective-permute-start.30 = (bf16[16,3200]{1,0:T(8,128)(2,1)}, bf16[16,3200]{1,0:T(8,128)(2,1)S(1)}, u32[]{:S(2)}, u32[]{:S(2)}) collective-permute-start(bf16[16,3200]{1,0:T(8,128)(2,1)} %get-tuple-element.151), channel_id=1, source_target_pairs={{0,16},{8,24},{16,0},{24,8},{1,17},{9,25},{17,1},{25,9},{2,18},{10... | collective-permute-start | bytes 307208 | tf_op jit(solution)/shard_map/ppermute | solution.py:799
  273.4 15.0 %collective-permute-start.31 = (bf16[16,3200]{1,0:T(8,128)(2,1)}, bf16[16,3200]{1,0:T(8,128)(2,1)S(1)}, u32[]{:S(2)}, u32[]{:S(2)}) collective-permute-start(bf16[16,3200]{1,0:T(8,128)(2,1)} %get-tuple-element.152), channel_id=1, source_target_pairs={{0,24},{8,16},{16,8},{24,0},{1,25},{9,17},{17,9},{25,1},{2,26},{10... | collective-permute-start | bytes 307208 | tf_op jit(solution)/shard_map/ppermute | solution.py:799
  278.7 13.7 %collective-permute-start.44 = (bf16[48,1024]{1,0:T(8,128)(2,1)}, bf16[48,1024]{1,0:T(8,128)(2,1)S(1)}, u32[]{:S(2)}, u32[]{:S(2)}) collective-permute-start(bf16[48,1024]{1,0:T(8,128)(2,1)} %join.3.refs_0_), channel_id=1, source_target_pairs={{0,24},{8,16},{16,8},{24,0},{1,25},{9,17},{17,9},{25,1},{2,26},{10... | collective-permute-start | bytes 294920 | tf_op jit(solution)/shard_map/ppermute | solution.py:799
  284.8 11.7 %collective-permute-start.43 = (bf16[48,1024]{1,0:T(8,128)(2,1)}, bf16[48,1024]{1,0:T(8,128)(2,1)S(1)}, u32[]{:S(2)}, u32[]{:S(2)}) collective-permute-start(bf16[48,1024]{1,0:T(8,128)(2,1)} %join.3.refs_0_), channel_id=1, source_target_pairs={{0,16},{8,24},{16,0},{24,8},{1,17},{9,25},{17,1},{25,9},{2,18},{10... | collective-permute-start | bytes 294920 | tf_op jit(solution)/shard_map/ppermute | solution.py:799
  284.8 11.6 %collective-permute-start.42 = (bf16[48,1024]{1,0:T(8,128)(2,1)}, bf16[48,1024]{1,0:T(8,128)(2,1)S(1)}, u32[]{:S(2)}, u32[]{:S(2)}) collective-permute-start(bf16[48,1024]{1,0:T(8,128)(2,1)} %join.3.refs_0_), channel_id=1, source_target_pairs={{0,8},{8,0},{16,24},{24,16},{1,9},{9,1},{17,25},{25,17},{2,10},{10... | collective-permute-start | bytes 294920 | tf_op jit(solution)/shard_map/ppermute | solution.py:799
  290.8 9.0 %collective-permute-start.34 = (bf16[16,3200]{1,0:T(8,128)(2,1)}, bf16[16,3200]{1,0:T(8,128)(2,1)S(1)}, u32[]{:S(2)}, u32[]{:S(2)}) collective-permute-start(bf16[16,3200]{1,0:T(8,128)(2,1)} %join.2.refs_0_), channel_id=1, source_target_pairs={{0,24},{8,16},{16,8},{24,0},{1,25},{9,17},{17,9},{25,1},{2,26},{10... | collective-permute-start | bytes 307208 | tf_op jit(solution)/shard_map/ppermute | solution.py:799
  291.7 9.0 %collective-permute-start.33 = (bf16[16,3200]{1,0:T(8,128)(2,1)}, bf16[16,3200]{1,0:T(8,128)(2,1)S(1)}, u32[]{:S(2)}, u32[]{:S(2)}) collective-permute-start(bf16[16,3200]{1,0:T(8,128)(2,1)} %join.2.refs_0_), channel_id=1, source_target_pairs={{0,16},{8,24},{16,0},{24,8},{1,17},{9,25},{17,1},{25,9},{2,18},{10... | collective-permute-start | bytes 307208 | tf_op jit(solution)/shard_map/ppermute | solution.py:799
  292.5 8.2 %collective-permute-start.32 = (bf16[16,3200]{1,0:T(8,128)(2,1)}, bf16[16,3200]{1,0:T(8,128)(2,1)S(1)}, u32[]{:S(2)}, u32[]{:S(2)}) collective-permute-start(bf16[16,3200]{1,0:T(8,128)(2,1)} %join.2.refs_0_), channel_id=1, source_target_pairs={{0,8},{8,0},{16,24},{24,16},{1,9},{9,1},{17,25},{25,17},{2,10},{10... | collective-permute-start | bytes 307208 | tf_op jit(solution)/shard_map/ppermute | solution.py:799
  (49 other events, 362.2 us)

commit v2 on v1

--- a/solution.py
+++ b/solution.py
@@ -32,29 +32,29 @@
 
 VM = pl.BlockSpec(memory_space=pltpu.VMEM)
 HB = pl.BlockSpec(memory_space=pl.ANY)
-PARAMS = pltpu.CompilerParams(vmem_limit_bytes=56 << 20)
-
-
-def whole(body, outs, scratch=(), in_specs=None, n_in=None, name=None):
+
+
+def cost(micros):
+    return pl.CostEstimate(flops=0, transcendentals=0, bytes_accessed=int(micros * 3.69e6))
+
+
+def whole(body, outs, scratch=(), in_specs=None, n_in=None, name=None, micros=2, vmem=26):
     return pl.pallas_call(
         body,
         out_shape=outs,
         in_specs=in_specs if in_specs is not None else [VM] * n_in,
         out_specs=jax.tree.map(lambda _: VM, outs),
         scratch_shapes=list(scratch),
-        compiler_params=PARAMS,
+        compiler_params=pltpu.CompilerParams(vmem_limit_bytes=vmem << 20),
+        cost_estimate=cost(micros),
         name=name,
     )
 
 
 def tiles(m_size, n_size, tm, tn, fn):
-    nm, nn = m_size // tm, n_size // tn
-
-    def body(i, _):
-        fn(pl.multiple_of((i % nm) * tm, tm), pl.multiple_of((i // nm) * tn, tn))
-        return 0
-
-    lax.fori_loop(0, nm * nn, body, 0)
+    for n in range(0, n_size, tn):
+        for m in range(0, m_size, tm):
+            fn(m, n)
 
 
 def rows_loop(total, step, fn):
@@ -73,23 +73,41 @@
     return max(ceil_div((d * n) % TILE + n, TILE) for d in range(devices))
 
 
-def place_kernel(flat_ref, dec_ref, out_ref, *, plan):
+def place_kernel(*refs, plan):
     me = lax.axis_index("seq")
+    decs, vectors, out_ref = refs[:4], refs[4:-1], refs[-1]
     out_ref[...] = jnp.zeros_like(out_ref)
-    held = dec_ref.shape[0]
-    row = lax.broadcasted_iota(jnp.int32, (held, TILE), 0)
-    lane = lax.broadcasted_iota(jnp.int32, (held, TILE), 1)
-    pick = jnp.where(lane == row + (me * held) % TILE, 1.0, 0.0).astype(BF)
-    out_ref[0 : dec_ref.shape[1], :] = dot(dec_ref[...], pick, TN)
-    for at, off, n, nt in plan:
-        low, high = off // TILE * TILE, ceil_div(off + n, TILE) * TILE
-        values = jnp.broadcast_to(flat_ref[:, low:high].astype(F32), (SUBS, high - low)).astype(BF)
-        row = lax.broadcasted_iota(jnp.int32, (high - low, nt * TILE), 0) - (off - low)
-        lane = lax.broadcasted_iota(jnp.int32, (high - low, nt * TILE), 1)
-        hit = (lane == row + (me * n) % TILE) & (row >= 0) & (row < n)
-        moved = dot(values, jnp.where(hit, 1.0, 0.0).astype(BF))
-        for j in range(nt):
-            out_ref[at + j : at + j + 1, :] = moved[0:1, j * TILE : (j + 1) * TILE]
+    dims, held = decs[0].shape
+    pick = pick_lanes(me, held, TILE)
+    for j, dec in enumerate(decs):
+        out_ref[j * dims : (j + 1) * dims, :] = dot(dec[...], pick.astype(BF))
+    source = 0
+    for at, count, n, nt in plan:
+        values = vectors[source][...].astype(F32)
+        source += 1
+        if count == 1:
+            values = values.reshape(1, n)
+        values = jnp.broadcast_to(values, (SUBS, n)) if count == 1 else values
+        moved = dot(values.astype(BF), pick_lanes(me, n, nt * TILE).astype(BF))
+        for i in range(count):
+            for j in range(nt):
+                out_ref[at + i + j : at + i + j + 1, :] = moved[i : i + 1, j * TILE : (j + 1) * TILE]
+
+
+def pick_lanes(me, n, lanes):
+    row = lax.broadcasted_iota(jnp.int32, (n, lanes), 0)
+    lane = lax.broadcasted_iota(jnp.int32, (n, lanes), 1)
+    return jnp.where(lane == row + (me * n) % TILE, 1.0, 0.0)
+
+
+def pack_kernel(value, mix, attend, down, up, w1, w2):
+    nv = value.shape[1]
+    w1[:, 0:nv] = value[...]
+    w1[:, nv:] = mix[...]
+    rows, width = attend.shape
+    w2[0:rows, 0:width] = attend[...]
+    w2[0:rows, width:] = down[...]
+    w2[rows:, :] = up[...]
 
 
 def assemble(src, low, high, n, total, devices):
@@ -136,10 +154,14 @@
     return lax.rsqrt(jnp.mean(x * x, axis=-1, keepdims=True) + EPSILON)
 
 
-def head_kernel(
-    small_ref, tok_ref, seg_ref, pd_ref, pv_ref, pz_ref, pm_ref, dk_ref, nrm_ref, low_ref, lab_ref,
-    fin_ref, msg_ref, scr_ref, *, devices, dims, nv, nm,
-):
+def head_kernel(*refs, devices, dims, nv, nm):
+    (
+        tok_ref, seg_ref, pd_ref, pv_ref, pz_ref, pm_ref, dk_ref, nrm_ref, low_ref, lab_ref,
+        fin_ref, msg_ref, scr_ref, small_ref,
+    ) = refs[devices:]
+    me = lax.axis_index("seq")
+    for k in range(devices):
+        small_ref[me ^ k] = refs[k][...]
     tokens, width = tok_ref.shape
     seqs, length = seg_ref.shape
     steps = tokens // SUBS
@@ -207,12 +229,12 @@
         msg_ref[dims * seqs : dims * seqs + 16, lanes] = tail.astype(BF)
 
 
-def entering(msgs, own_label, even, scr_refs, lab_scr, start, dims, seqs, power):
+def entering(msgs, lanes, own_label, even, scr_refs, lab_scr, start, dims, seqs, power):
     half = SUBS // seqs
     gates = []
     for m, scr in zip(msgs, scr_refs):
-        scr[pl.ds(start, dims * seqs, stride=half), :] = m[0 : dims * seqs, :].astype(F32)
-        tail = m[dims * seqs : dims * seqs + 16, :].astype(F32)
+        scr[pl.ds(start, dims * seqs, stride=half), :] = m[0 : dims * seqs, lanes].astype(F32)
+        tail = m[dims * seqs : dims * seqs + 16, lanes].astype(F32)
         lab_scr[pl.ds(start, seqs, stride=half), :] = tail[0:seqs, :]
         gates.append(even & (lab_scr[...] == own_label))
     result = []
@@ -235,53 +257,71 @@
     z_ref, mlow_ref, sp_ref = refs[5 + reach : 8 + reach]
     ent_ref, lab_scr, ys_ref = refs[8 + reach : 11 + reach]
     scr_refs = refs[11 + reach :]
-    tokens = nrm_ref.shape[0]
+    blocks, tokens, _ = nrm_ref.shape
     steps = tokens // SUBS
     half = SUBS // seqs
     first, last = chunk_labels(lab_ref, steps)
     place = lax.broadcasted_iota(jnp.int32, (SUBS, TILE), 0)
     even = place % half == 0
-    power = dk_ref[2 * dims : 3 * dims, :]
-    arrivals = entering(msgs, first, even, scr_refs, lab_scr, 0, dims, seqs, power)
     inside = first == last
     joined = first == pltpu.roll(last, 1, 0)
-    for h in range(dims):
-        e = arrivals[h]
-        own = fin_ref[h * SUBS : (h + 1) * SUBS, :]
-        onward = pltpu.roll(own + jnp.where(inside, e * power[h : h + 1, :], 0.0), 1, 0)
-        ent_ref[h * SUBS : (h + 1) * SUBS, :] = jnp.where(even, e, jnp.where(joined, onward, 0.0))
-    decay = [jnp.broadcast_to(dk_ref[h : h + 1, :], (SUBS, TILE)) for h in range(dims)]
-    weight = [jnp.broadcast_to(dk_ref[dims + h : dims + h + 1, :], (SUBS, TILE)) for h in range(dims)]
     unroll = 4
 
-    def step(i, carry):
-        before, state = carry[0], list(carry[1:])
-        for u in range(unroll):
-            t = i * unroll + u
-            x = nrm_ref[pl.ds(t, SUBS, stride=steps), :]
-            l = lab_ref[pl.ds(t, SUBS, stride=steps), :]
-            same = l == before
-            before = l
-            sums = [None] * 4
-            for h in range(dims):
-                kept = jnp.where(same, state[h], 0.0)
-                sp_ref[t, h * SUBS : (h + 1) * SUBS, :] = kept
-                state[h] = decay[h] * kept + x
-                term = weight[h] * state[h]
-                sums[h % 4] = term if sums[h % 4] is None else sums[h % 4] + term
-            ys_ref[pl.ds(t, SUBS, stride=steps), :] = (sums[0] + sums[1]) + (sums[2] + sums[3])
-        return (before,) + tuple(state)
-
-    start = tuple(ent_ref[h * SUBS : (h + 1) * SUBS, :] for h in range(dims))
-    lax.fori_loop(0, steps // unroll, step, (first,) + start)
+    def block(lt, _):
+        lanes = pl.ds(pl.multiple_of(lt * TILE, TILE), TILE)
+        power = dk_ref[2 * dims : 3 * dims, lanes]
+        arrivals = entering(msgs, lanes, first, even, scr_refs, lab_scr, 0, dims, seqs, power)
+        for h in range(dims):
+            e = arrivals[h]
+            own = fin_ref[h * SUBS : (h + 1) * SUBS, lanes]
+            onward = pltpu.roll(own + jnp.where(inside, e * power[h : h + 1, :], 0.0), 1, 0)
+            ent_ref[h * SUBS : (h + 1) * SUBS, :] = jnp.where(
+                even, e, jnp.where(joined, onward, 0.0)
+            )
+        decay = [jnp.broadcast_to(dk_ref[h : h + 1, lanes], (SUBS, TILE)) for h in range(dims)]
+        weight = [
+            jnp.broadcast_to(dk_ref[dims + h : dims + h + 1, lanes], (SUBS, TILE))
+            for h in range(dims)
+        ]
+
+        def step(i, carry):
+            before, state = carry[0], list(carry[1:])
+            for u in range(unroll):
+                t = i * unroll + u
+                x = nrm_ref[lt, pl.ds(t, SUBS, stride=steps), :]
+                l = lab_ref[pl.ds(t, SUBS, stride=steps), :]
+                same = l == before
+                before = l
+                sums = [None] * 4
+                for h in range(dims):
+                    kept = jnp.where(same, state[h], 0.0)
+                    if h % 2 == 0:
+                        held = kept
+                    else:
+                        pair = jnp.concatenate([held, kept], axis=0)
+                        sp_ref[lt, t, (h - 1) * SUBS : (h + 1) * SUBS, :] = pair.astype(BF)
+                    state[h] = decay[h] * kept + x
+                    term = weight[h] * state[h]
+                    sums[h % 4] = term if sums[h % 4] is None else sums[h % 4] + term
+                ys_ref[lt, pl.ds(t, SUBS, stride=steps), :] = (sums[0] + sums[1]) + (
+                    sums[2] + sums[3]
+                )
+            return (before,) + tuple(state)
+
+        start = tuple(ent_ref[h * SUBS : (h + 1) * SUBS, :] for h in range(dims))
+        lax.fori_loop(0, steps // unroll, step, (first,) + start)
+        return 0
+
+    lax.fori_loop(0, blocks, block, 0)
     omega = pd_ref[4 * dims + 1 : 4 * dims + 2, :]
 
     def gate(r):
-        v = ys_ref[pl.ds(r, 64), :] + omega * nrm_ref[pl.ds(r, 64), :]
-        z_ref[pl.ds(r, 64), :] = v
-        mlow_ref[pl.ds(r, 64), :] = (v * sig(v)).astype(BF)
-
-    rows_loop(tokens, 64, gate)
+        for t in range(blocks):
+            v = ys_ref[t, pl.ds(r, 128), :] + omega[:, lanes_of(t)] * nrm_ref[t, pl.ds(r, 128), :]
+            z_ref[pl.ds(r, 128), lanes_of(t)] = v
+            mlow_ref[pl.ds(r, 128), lanes_of(t)] = (v * sig(v)).astype(BF)
+
+    rows_loop(tokens, 128, gate)
 
 
 def load_weights(pieces, dst, sem, rows, start, cols, place):
@@ -320,42 +360,42 @@
         c.wait()
 
     def value(m, n):
-        v = dot(nlow[pl.ds(m, 256), :], w[:, pl.ds(n, 256)]) + pv[0:1, pl.ds(n, 256)]
+        v = dot(nlow[pl.ds(m, 512), :], w[:, pl.ds(n, 512)]) + pv[0:1, pl.ds(n, 512)]
         s = sig(v)
-        vlow[pl.ds(m, 256), pl.ds(n, 256)] = (v * s).astype(BF)
-        dval[pl.ds(m, 256), pl.ds(n, 256)] = (s * (1.0 + v * (1.0 - s))).astype(BF)
-
-    tiles(tokens, nv, 256, 256, value)
+        vlow[pl.ds(m, 512), pl.ds(n, 512)] = (v * s).astype(BF)
+        dval[pl.ds(m, 512), pl.ds(n, 512)] = (s * (1.0 + v * (1.0 - s))).astype(BF)
+
+    tiles(tokens, nv, 512, 512, value)
     at = split_sizes(width, zw, nv)
 
     def base(m, n, start, size):
-        cols = pl.multiple_of(start + n, TILE)
-        wcols = pl.multiple_of(nv + start + n, TILE)
-        return dot(mlow[pl.ds(m, 256), :], w[:, pl.ds(wcols, size)]) + pm[0:1, pl.ds(cols, size)]
+        cols = start + n
+        wcols = nv + start + n
+        return dot(mlow[pl.ds(m, 512), :], w[:, pl.ds(wcols, size)]) + pm[0:1, pl.ds(cols, size)]
 
     def update(m, n):
-        upd[pl.ds(m, 256), pl.ds(n, 256)] = sig(base(m, n, at["u"], 256))
-
-    tiles(tokens, width, 256, 256, update)
+        upd[pl.ds(m, 512), pl.ds(n, 512)] = sig(base(m, n, at["u"], 512))
+
+    tiles(tokens, width, 512, 512, update)
 
     def extra(m, n):
-        ext[pl.ds(m, 256), pl.ds(n, 256)] = base(m, n, at["e"], 256)
-
-    tiles(tokens, width, 256, 256, extra)
+        ext[pl.ds(m, 512), pl.ds(n, 512)] = base(m, n, at["e"], 512)
+
+    tiles(tokens, width, 512, 512, extra)
 
     def reset(m, n):
-        res[pl.ds(m, 256), pl.ds(n, 256)] = base(m, n, at["r"], 256)
-
-    tiles(tokens, nv, 256, 256, reset)
+        res[pl.ds(m, 512), pl.ds(n, 512)] = base(m, n, at["r"], 512)
+
+    tiles(tokens, nv, 512, 512, reset)
 
     def latent(m, n):
         v = base(m, n, at["l"], zw)
-        lat[pl.ds(m, 256), :] = v
+        lat[pl.ds(m, 512), :] = v
         y = v * sig(v)
-        qlow[pl.ds(m, 256), :] = ((y * pz[2:3, :] + pz[4:5, :]) * zw ** (-0.5)).astype(BF)
-        klow[pl.ds(m, 256), :] = (y * pz[3:4, :]).astype(BF)
-
-    tiles(tokens, zw, 256, zw, latent)
+        qlow[pl.ds(m, 512), :] = ((y * pz[2:3, :] + pz[4:5, :]) * zw ** (-0.5)).astype(BF)
+        klow[pl.ds(m, 512), :] = (y * pz[3:4, :]).astype(BF)
+
+    tiles(tokens, zw, 512, zw, latent)
 
     row = lax.broadcasted_iota(jnp.int32, (length, length), 0)
     col = lax.broadcasted_iota(jnp.int32, (length, length), 1)
@@ -389,6 +429,9 @@
 
 def column_sum(ref, row, cols, values, first):
     total = jnp.sum(values, axis=0, keepdims=True)
+    if isinstance(first, bool):
+        ref[row : row + 1, cols] = total if first else ref[row : row + 1, cols] + total
+        return
 
     @pl.when(first)
     def _():
@@ -430,9 +473,9 @@
     down = pl.ds(width, width)
 
     def project(m, n):
-        proj[pl.ds(m, 256), pl.ds(n, 256)] = dot(glow[pl.ds(m, 256), :], w2[:, pl.ds(n, 256)])
-
-    tiles(tokens, width, 256, 256, project)
+        proj[pl.ds(m, 512), pl.ds(n, 512)] = dot(glow[pl.ds(m, 512), :], w2[:, pl.ds(n, 512)])
+
+    tiles(tokens, width, 512, 512, project)
     gain = pd[4 * dims + 2 : 4 * dims + 3, :]
 
     def blend(r):
@@ -447,43 +490,42 @@
     rows_loop(tokens, 64, blend)
 
     def up(m, n):
-        v = dot(slow[pl.ds(m, 256), :], wup[:, pl.ds(n, 256)]) + pv[1:2, pl.ds(n, 256)]
+        v = dot(slow[pl.ds(m, 512), :], wup[:, pl.ds(n, 512)]) + pv[1:2, pl.ds(n, 512)]
         s = sig(v)
-        hlow[pl.ds(m, 256), pl.ds(n, 256)] = (v * s).astype(BF)
-        dup[pl.ds(m, 256), pl.ds(n, 256)] = s * (1.0 + v * (1.0 - s))
-
-    tiles(tokens, nf, 256, 256, up)
+        hlow[pl.ds(m, 512), pl.ds(n, 512)] = (v * s).astype(BF)
+        dup[pl.ds(m, 512), pl.ds(n, 512)] = s * (1.0 + v * (1.0 - s))
+
+    tiles(tokens, nf, 512, 512, up)
 
     def down_forward(m, n):
-        at, cols = pl.ds(m, 256), pl.ds(n, 256)
-        y = dot(hlow[at, :], w2[:, pl.ds(pl.multiple_of(width + n, 256), 256)])
+        at, cols = pl.ds(m, 512), pl.ds(n, 512)
+        y = dot(hlow[at, :], w2[:, pl.ds(width + n, 512)])
         out[at, cols] = mid[at, cols] + y + pd[4 * dims + 3 : 4 * dims + 4, cols]
         c = cot[at, cols]
         clow[at, cols] = c.astype(BF)
         column_sum(v512, 0, cols, c, m == 0)
 
-    tiles(tokens, width, 256, 256, down_forward)
+    tiles(tokens, width, 512, 512, down_forward)
 
     def up_back(m, n):
-        at, cols = pl.ds(m, 256), pl.ds(n, 256)
+        at, cols = pl.ds(m, 512), pl.ds(n, 512)
         g = dot(clow[at, :], w2[cols, down], NT) * dup[at, cols]
         ulow[at, cols] = g.astype(BF)
         column_sum(v1024, 0, cols, g, m == 0)
 
-    tiles(tokens, nf, 256, 256, up_back)
+    tiles(tokens, nf, 512, 512, up_back)
 
     def down_grad(m, n):
-        grad[pl.ds(m, 256), pl.ds(pl.multiple_of(width + n, 256), 256)] = dot(
-            hlow[:, pl.ds(m, 256)], clow[:, pl.ds(n, 256)], TN
+        grad[pl.ds(m, 512), pl.ds(width + n, 512)] = dot(
+            hlow[:, pl.ds(m, 512)], clow[:, pl.ds(n, 512)], TN
         ).astype(BF)
 
-    tiles(nf, width, 256, 256, down_grad)
+    tiles(nf, width, 512, 512, down_grad)
 
     def second_back(m, n):
-        proj[pl.ds(m, 256), pl.ds(n, 256)] += 0.0
-        gmid[pl.ds(m, 256), pl.ds(n, 256)] = dot(ulow[pl.ds(m, 256), :], wup[pl.ds(n, 256), :], NT)
-
-    tiles(tokens, width, 256, 256, second_back)
+        gmid[pl.ds(m, 512), pl.ds(n, 512)] = dot(ulow[pl.ds(m, 512), :], wup[pl.ds(n, 512), :], NT)
+
+    tiles(tokens, width, 512, 512, second_back)
     everything = slice(0, width)
 
     def middle_back(r):
@@ -513,30 +555,30 @@
     rows_loop(tokens, 64, middle_back)
 
     def gated_back(m, n):
-        at, cols = pl.ds(m, 256), pl.ds(n, 256)
+        at, cols = pl.ds(m, 512), pl.ds(n, 512)
         g = dot(elow[at, :], w2[cols, pl.ds(0, width)], NT)
         gr = g * ad[at, cols].astype(F32)
         blre[at, cols] = gr.astype(BF)
         attg[at, cols] = (g * rs[at, cols].astype(F32)).astype(BF)
         column_sum(v1024, 1, cols, gr, m == 0)
 
-    tiles(tokens, nv, 256, 256, gated_back)
+    tiles(tokens, nv, 512, 512, gated_back)
 
     def attend_grad(m, n):
-        grad[pl.ds(m, 256), pl.ds(n, 256)] = dot(
-            glow[:, pl.ds(m, 256)], elow[:, pl.ds(n, 256)], TN
+        grad[pl.ds(m, 512), pl.ds(n, 512)] = dot(
+            glow[:, pl.ds(m, 512)], elow[:, pl.ds(n, 512)], TN
         ).astype(BF)
 
-    tiles(nv, width, 256, 256, attend_grad)
+    tiles(nv, width, 512, 512, attend_grad)
     r2, r1 = rows2 // depth, rows1 // depth
     put_pieces(grad, own, sib, devices, depth, r2, 0, slice(0, 2 * width), slice(0, 2 * width))
 
     def up_grad(m, n):
-        grad[pl.ds(m, 256), pl.ds(n, 256)] = dot(
-            slow[:, pl.ds(m, 256)], ulow[:, pl.ds(n, 256)], TN
+        grad[pl.ds(m, 512), pl.ds(n, 512)] = dot(
+            slow[:, pl.ds(m, 512)], ulow[:, pl.ds(n, 512)], TN
         ).astype(BF)
 
-    tiles(width, nf, 256, 256, up_grad)
+    tiles(width, nf, 512, 512, up_grad)
     put_pieces(grad, own, sib, devices, depth, r1, r2, slice(0, nf), slice(0, nf))
 
 
@@ -605,7 +647,7 @@
     at = split_sizes(width, zw, nv)
 
     def mixed_back(m, n):
-        here, cols = pl.ds(m, 256), pl.ds(n, 256)
+        here, cols = pl.ds(m, 512), pl.ds(n, 512)
         g = dot(blu[here, :], w[cols, nv : nv + width], NT)
         g = g + dot(bll[here, :], w[cols, nv + at["l"] : nv + at["r"]], NT)
         g = g + dot(blre[here, :], w[cols, nv + at["r"] :], NT)
@@ -613,11 +655,11 @@
         s = sig(v)
         g = g * (s * (1.0 + v * (1.0 - s)))
         t = n // TILE
-        for j in range(256 // TILE):
+        for j in range(512 // TILE):
             gs[t + j, here, :] = g[:, lanes_of(j)]
         column_sum(w512, 0, cols, g * two(nrm, t, here), m == 0)
 
-    tiles(tokens, width, 256, 256, mixed_back)
+    tiles(tokens, width, 512, 512, mixed_back)
     first, last = chunk_labels(lab, steps)
     one_way(gs, lab, first, dk, ach, dims, steps, width, True)
     power = dk[2 * dims : 3 * dims, :]
@@ -635,15 +677,17 @@
         msg[dims * seqs : dims * seqs + 16, lanes] = tail.astype(BF)
 
     def normed_back(m, n):
-        here, cols = pl.ds(m, 256), pl.ds(n, 256)
+        here, cols = pl.ds(m, 512), pl.ds(n, 512)
         omega = pd[4 * dims + 1 : 4 * dims + 2, cols]
-        gnp[here, cols] = two(gs, n // TILE, here) * omega + dot(vgl[here, :], w[cols, 0:nv], NT)
-
-    tiles(tokens, width, 256, 256, normed_back)
+        g = two(gs, n // TILE, here) * omega + dot(vgl[here, :], w[cols, 0:nv], NT)
+        for j in range(512 // TILE):
+            gnp[n // TILE + j, here, :] = g[:, lanes_of(j)]
+
+    tiles(tokens, width, 512, 512, normed_back)
 
 
 def two(ref, t, here):
-    return jnp.concatenate([ref[t + j, here, :] for j in range(256 // TILE)], axis=1)
+    return jnp.concatenate([ref[t + j, here, :] for j in range(512 // TILE)], axis=1)
 
 
 def weight_kernel(
@@ -656,142 +700,148 @@
 
     def piece(lhs, rhs, start, cols):
         def fn(m, n):
-            grad[pl.ds(m, 256), pl.ds(pl.multiple_of(start + n, TILE), cols)] = dot(
-                lhs[:, pl.ds(m, 256)], rhs[:, pl.ds(n, cols)], TN
+            grad[pl.ds(m, 512), pl.ds(start + n, cols)] = dot(
+                lhs[:, pl.ds(m, 512)], rhs[:, pl.ds(n, cols)], TN
             ).astype(BF)
 
-        tiles(width, rhs.shape[1], 256, cols, fn)
-
-    piece(nlow, vgl, 0, 256)
-    piece(mlow, blu, nv, 256)
+        tiles(width, rhs.shape[1], 512, cols, fn)
+
+    piece(nlow, vgl, 0, 512)
+    piece(mlow, blu, nv, 512)
     piece(mlow, bll, nv + at["l"], zw)
-    piece(mlow, blre, nv + at["r"], 256)
+    piece(mlow, blre, nv + at["r"], 512)
     full = slice(0, grad.shape[1])
     put_pieces(grad, own, sib, devices, depth, width // devices // depth, 0, full, full)
 
 
 def last_kernel(*refs, reach, devices, dims, seqs, nm):
-    sp, nrm, gs, gnp, lab, dk, pdb, ach = refs[:8]
-    msgs = refs[8 : 8 + reach]
-    tok, gin, pd, v512, v1024, w512, w1024, w128 = refs[8 + reach : 16 + reach]
-    tg, own, sib = refs[16 + reach : 19 + reach]
-    ent, lab_scr, gnb, gnf, sd, sv, sm = refs[19 + reach : 26 + reach]
-    scr_refs = refs[26 + reach :]
-    tokens = nrm.shape[0]
+    sp, nrm, gs, gnp, lab, dk, ach = refs[:7]
+    msgs = refs[7 : 7 + reach]
+    tok, gin, pd, v512, v1024, w512, w1024, w128 = refs[7 + reach : 15 + reach]
+    tg, own, sib = refs[15 + reach : 18 + reach]
+    ent, lab_scr, gnb, sd, sv, sm, sums_ref = refs[18 + reach : 25 + reach]
+    scr_refs = refs[25 + reach :]
+    blocks, tokens, _ = nrm.shape
     width = tok.shape[1]
     steps = tokens // SUBS
     half = SUBS // seqs
-    lt = pl.program_id(0)
     first, last = chunk_labels(lab, steps)
     place = lax.broadcasted_iota(jnp.int32, (SUBS, TILE), 0)
     odd = place % half == half - 1
-    power = dk[2 * dims : 3 * dims, :]
-    arrivals = entering(msgs, last, odd, scr_refs, lab_scr, half - 1, dims, seqs, power)
     inside = first == last
     joined = last == pltpu.roll(first, SUBS - 1, 0)
-    for h in range(dims):
-        e = arrivals[h]
-        here = slice(h * SUBS, (h + 1) * SUBS)
-        onward = pltpu.roll(
-            ach[here, :] + jnp.where(inside, e * power[h : h + 1, :], 0.0), SUBS - 1, 0
-        )
-        ent[here, :] = jnp.where(odd, e, jnp.where(joined, onward, 0.0))
     unroll = 4
     group = 8
     zero = jnp.zeros((SUBS, TILE), F32)
-    cols = pl.ds(pl.multiple_of(lt * TILE, TILE), TILE)
-    for base in range(0, dims, group):
-        span = range(base, base + group)
-        decay = [jnp.broadcast_to(dk[h : h + 1, :], (SUBS, TILE)) for h in span]
-        weight = [jnp.broadcast_to(dk[dims + h : dims + h + 1, :], (SUBS, TILE)) for h in span]
-
-        def step(i, carry, base=base, decay=decay, weight=weight):
-            after = carry[0]
-            a, g0, g1 = (list(carry[1 + j * group : 1 + (j + 1) * group]) for j in range(3))
-            for u in range(unroll):
-                t = steps - 1 - (i * unroll + u)
-                here = pl.ds(t, SUBS, stride=steps)
-                x = nrm[here, :]
-                g = gs[here, :]
-                l = lab[here, :]
-                same = l == after
-                after = l
-                sums = [gnp[here, :] if base == 0 else gnb[here, :], zero]
-                for j in range(group):
-                    h = base + j
-                    a[j] = decay[j] * jnp.where(same, a[j], 0.0) + g
-                    g0[j] = g0[j] + a[j] * x
-                    g1[j] = g1[j] + a[j] * sp[t, h * SUBS : (h + 1) * SUBS, :]
-                    sums[j % 2] = sums[j % 2] + weight[j] * a[j]
-                gnb[here, :] = sums[0] + sums[1]
-            return (after,) + tuple(a) + tuple(g0) + tuple(g1)
-
-        start = tuple(ent[h * SUBS : (h + 1) * SUBS, :] for h in span)
-        done = lax.fori_loop(0, steps // unroll, step, (last,) + start + (zero,) * (2 * group))
-        for j in range(group):
-            h = base + j
-            g0 = jnp.sum(done[1 + group + j], axis=0, keepdims=True)
-            g1 = jnp.sum(done[1 + 2 * group + j], axis=0, keepdims=True)
-            rate = 1.0 / (1.0 + jnp.exp(-pdb[h : h + 1, :]))
-            damping = 1.0 / (1.0 + jnp.exp(-pdb[dims + h : dims + h + 1, :]))
-            beta = pdb[2 * dims + h : 2 * dims + h + 1, :]
-            eta = pdb[3 * dims + h : 3 * dims + h + 1, :]
-            grad_decay = g1 * eta * rate * beta
-            grad_rate = g0 * eta * beta - damping * grad_decay
-            sd[h : h + 1, cols] = grad_rate * rate * (1.0 - rate)
-            sd[dims + h : dims + h + 1, cols] = -grad_decay * rate * damping * (1.0 - damping)
-            sd[2 * dims + h : 2 * dims + h + 1, cols] = g0 * rate * eta
-            sd[3 * dims + h : 3 * dims + h + 1, cols] = g0 * rate * beta
-    gnf[:, cols] = gnb[...]
-
-    @pl.when(lt == pl.num_programs(0) - 1)
-    def _():
-        top = 4 * dims
-        gain = pd[top : top + 1, :]
-        sd[top : top + 8, :] = jnp.zeros((8, width), F32)
-
-        def norm(r):
-            here = pl.ds(r, 64)
-            x = tok[here, :].astype(F32)
-            q = norm_scale(x)
-            m = x * q
-            gn = gnf[here, :]
-            sd[top : top + 1, :] += jnp.sum(gn * m, axis=0, keepdims=True)
-            gn = gn * gain
-            tg[here, :] = gin[here, :] + q * (gn - m * jnp.mean(gn * m, axis=-1, keepdims=True))
-
-        rows_loop(tokens, 64, norm)
-        sd[top + 1 : top + 2, :] = w512[0:1, :]
-        sd[top + 2 : top + 3, :] = v512[1:2, :]
-        sd[top + 3 : top + 4, :] = v512[0:1, :]
-        nv = v1024.shape[1]
-        zw = w128.shape[1]
-        sv[...] = jnp.zeros_like(sv)
-        sv[0:1, :] = w1024[0:1, :]
-        sv[1:2, :] = v1024[0:1, :]
-        at = split_sizes(width, zw, nv)
-        sm[...] = jnp.zeros_like(sm)
-        sm[0:1, 0:width] = v512[2:3, :]
-        sm[0:1, at["l"] : at["r"]] = w128[0:1, :]
-        sm[0:1, at["r"] : at["e"]] = v1024[1:2, :]
-        sm[0:1, at["e"] : nm] = v512[3:4, :]
-        me = lax.axis_index("seq")
-        zrow = lax.broadcasted_iota(jnp.int32, (8, TILE), 0)
-        zpart = jnp.where(zrow >= 2, w128[...], 0.0)
-        for p in range(devices):
-            k = me ^ p
-            kc = k // 2
-
-            def put(dst, p=p, kc=kc):
-                dst[kc, 0:72, :] = sd[:, lanes_of(p * (width // devices) // TILE)]
-                dst[kc, 72:80, :] = sv[:, lanes_of(p * (nv // devices) // TILE)] + zpart
-                begin = p * (nm // devices) // TILE
-                dst[kc, 80:88, :] = jnp.zeros((8, TILE), F32)
-                for j in range(spread(nm // devices, devices)):
-                    dst[kc, 80 + j : 81 + j, :] = sm[0:1, lanes_of(begin + j)]
-
-            pl.when(k % 2 == 0)(partial(put, own))
-            pl.when(k % 2 == 1)(partial(put, sib))
+
+    def block(lt, _):
+        lanes = pl.ds(pl.multiple_of(lt * TILE, TILE), TILE)
+        power = dk[2 * dims : 3 * dims, lanes]
+        arrivals = entering(msgs, lanes, last, odd, scr_refs, lab_scr, half - 1, dims, seqs, power)
+        for h in range(dims):
+            e = arrivals[h]
+            here = slice(h * SUBS, (h + 1) * SUBS)
+            onward = pltpu.roll(
+                ach[here, lanes] + jnp.where(inside, e * power[h : h + 1, :], 0.0), SUBS - 1, 0
+            )
+            ent[here, :] = jnp.where(odd, e, jnp.where(joined, onward, 0.0))
+        for base in range(0, dims, group):
+            span = range(base, base + group)
+            decay = [jnp.broadcast_to(dk[h : h + 1, lanes], (SUBS, TILE)) for h in span]
+            weight = [
+                jnp.broadcast_to(dk[dims + h : dims + h + 1, lanes], (SUBS, TILE)) for h in span
+            ]
+
+            def step(i, carry, base=base, decay=decay, weight=weight):
+                after = carry[0]
+                a, g0, g1 = (list(carry[1 + j * group : 1 + (j + 1) * group]) for j in range(3))
+                for u in range(unroll):
+                    t = steps - 1 - (i * unroll + u)
+                    here = pl.ds(t, SUBS, stride=steps)
+                    x = nrm[lt, here, :]
+                    g = gs[lt, here, :]
+                    l = lab[here, :]
+                    same = l == after
+                    after = l
+                    sums = [gnp[lt, here, :] if base == 0 else gnb[lt, here, :], zero]
+                    for j in range(group):
+                        h = base + j
+                        if j % 2 == 0:
+                            pair = sp[lt, t, h * SUBS : (h + 2) * SUBS, :].astype(F32)
+                        a[j] = decay[j] * jnp.where(same, a[j], 0.0) + g
+                        g0[j] = g0[j] + a[j] * x
+                        g1[j] = g1[j] + a[j] * pair[j % 2 * SUBS : (j % 2 + 1) * SUBS, :]
+                        sums[j % 2] = sums[j % 2] + weight[j] * a[j]
+                    gnb[lt, here, :] = sums[0] + sums[1]
+                return (after,) + tuple(a) + tuple(g0) + tuple(g1)
+
+            start = tuple(ent[h * SUBS : (h + 1) * SUBS, :] for h in span)
+            done = lax.fori_loop(0, steps // unroll, step, (last,) + start + (zero,) * (2 * group))
+            for j in range(group):
+                h = base + j
+                sums_ref[h : h + 1, lanes] = jnp.sum(done[1 + group + j], axis=0, keepdims=True)
+                sums_ref[dims + h : dims + h + 1, lanes] = jnp.sum(
+                    done[1 + 2 * group + j], axis=0, keepdims=True
+                )
+        return 0
+
+    lax.fori_loop(0, blocks, block, 0)
+    rate = 1.0 / (1.0 + jnp.exp(-pd[0:dims, :]))
+    damping = 1.0 / (1.0 + jnp.exp(-pd[dims : 2 * dims, :]))
+    beta, eta = pd[2 * dims : 3 * dims, :], pd[3 * dims : 4 * dims, :]
+    g0 = sums_ref[0:dims, :]
+    grad_decay = sums_ref[dims : 2 * dims, :] * eta * rate * beta
+    grad_rate = g0 * eta * beta - damping * grad_decay
+    sd[0:dims, :] = grad_rate * rate * (1.0 - rate)
+    sd[dims : 2 * dims, :] = -grad_decay * rate * damping * (1.0 - damping)
+    sd[2 * dims : 3 * dims, :] = g0 * rate * eta
+    sd[3 * dims : 4 * dims, :] = g0 * rate * beta
+    top = 4 * dims
+    gain = pd[top : top + 1, :]
+    sd[top : top + 8, :] = jnp.zeros((8, width), F32)
+
+    def norm(r):
+        here = pl.ds(r, 64)
+        x = tok[here, :].astype(F32)
+        q = norm_scale(x)
+        m = x * q
+        gn = jnp.concatenate([gnb[t, here, :] for t in range(blocks)], axis=1)
+        sd[top : top + 1, :] += jnp.sum(gn * m, axis=0, keepdims=True)
+        gn = gn * gain
+        tg[here, :] = gin[here, :] + q * (gn - m * jnp.mean(gn * m, axis=-1, keepdims=True))
+
+    rows_loop(tokens, 64, norm)
+    sd[top + 1 : top + 2, :] = w512[0:1, :]
+    sd[top + 2 : top + 3, :] = v512[1:2, :]
+    sd[top + 3 : top + 4, :] = v512[0:1, :]
+    nv = v1024.shape[1]
+    zw = w128.shape[1]
+    sv[...] = jnp.zeros_like(sv)
+    sv[0:1, :] = w1024[0:1, :]
+    sv[1:2, :] = v1024[0:1, :]
+    at = split_sizes(width, zw, nv)
+    sm[...] = jnp.zeros_like(sm)
+    sm[0:1, 0:width] = v512[2:3, :]
+    sm[0:1, at["l"] : at["r"]] = w128[0:1, :]
+    sm[0:1, at["r"] : at["e"]] = v1024[1:2, :]
+    sm[0:1, at["e"] : nm] = v512[3:4, :]
+    me = lax.axis_index("seq")
+    zrow = lax.broadcasted_iota(jnp.int32, (8, TILE), 0)
+    zpart = jnp.where(zrow >= 2, w128[...], 0.0)
+    for p in range(devices):
+        k = me ^ p
+        kc = k // 2
+
+        def put(dst, p=p, kc=kc):
+            dst[kc, 0:72, :] = sd[:, lanes_of(p * (width // devices) // TILE)]
+            dst[kc, 72:80, :] = sv[:, lanes_of(p * (nv // devices) // TILE)] + zpart
+            begin = p * (nm // devices) // TILE
+            dst[kc, 80:88, :] = jnp.zeros((8, TILE), F32)
+            for j in range(spread(nm // devices, devices)):
+                dst[kc, 80 + j : 81 + j, :] = sm[0:1, lanes_of(begin + j)]
+
+        pl.when(k % 2 == 0)(partial(put, own))
+        pl.when(k % 2 == 1)(partial(put, sib))
 
 
 def hop(x, axis, k):
@@ -871,27 +921,31 @@
 
 
 def final_kernel(*refs, depth, plan, held, dims):
-    ins, dec, flat, scr = refs[:depth], refs[depth], refs[depth + 1], refs[depth + 2]
+    ins, decs = refs[:depth], refs[depth : depth + 4]
+    vectors, scr = refs[depth + 4 : -1], refs[-1]
     grp, me = lax.axis_index("grp"), lax.axis_index("seq")
     for k in range(depth):
         scr[grp ^ k] = ins[k][...]
     total = scr[0]
     for z in range(1, depth):
         total = total + scr[z]
-    row = lax.broadcasted_iota(jnp.int32, (held, TILE), 0)
-    lane = lax.broadcasted_iota(jnp.int32, (held, TILE), 1)
-    pick = jnp.where(lane == row + (me * held) % TILE, 1.0, 0.0)
-    dec[...] = lax.dot_general(
-        pick, total[0 : 4 * dims, :], NT, precision=lax.Precision.HIGHEST, preferred_element_type=F32
-    )
-    flat[...] = jnp.zeros_like(flat)
-    for j, (at, _, n, nt) in enumerate(plan):
-        values = [total[at + i : at + i + 1, :] for i in range(nt)]
-        values = values[0] if nt == 1 else jnp.concatenate(values, axis=1)
-        values = jnp.broadcast_to(values, (SUBS, nt * TILE))
+    pick = pick_lanes(me, held, TILE)
+    for j, dec in enumerate(decs):
+        dec[...] = lax.dot_general(
+            total[j * dims : (j + 1) * dims, :], pick, NT,
+            precision=lax.Precision.HIGHEST, preferred_element_type=F32,
+        )
+    for out, (at, count, n, nt) in zip(vectors, plan):
         lanes = nt * TILE
-        moved = pltpu.roll(values, (lanes - (me * n) % TILE) % lanes, 1)
-        flat[j : j + 1, 0:lanes] = moved[0:1, :]
+        for i in range(count):
+            values = [total[at + i + j : at + i + j + 1, :] for j in range(nt)]
+            values = values[0] if nt == 1 else jnp.concatenate(values, axis=1)
+            values = jnp.broadcast_to(values, (SUBS, lanes))
+            moved = pltpu.roll(values, (lanes - (me * n) % TILE) % lanes, 1)
+            if count == 1:
+                out[...] = moved[0:1, 0:n].reshape(n)
+            else:
+                out[i : i + 1, :] = moved[0:1, 0:n]
 
 
 def total_kernel(*refs):
@@ -901,10 +955,25 @@
     refs[-1][...] = total
 
 
+def near_pieces(x, devices):
+    return [x] + [hop(x, "seq", 2 * k) for k in range(1, devices // 2)]
+
+
+def far_pieces(near):
+    return [hop(part, "seq", 1) for part in near]
+
+
+def woven(near, far):
+    return [part for pair in zip(near, far) for part in pair]
+
+
 def gather_pieces(x, devices):
-    near = [x] + [hop(x, "seq", 2 * k) for k in range(1, devices // 2)]
-    far = [hop(part, "seq", 1) for part in near]
-    return [part for pair in zip(near, far) for part in pair]
+    near = near_pieces(x, devices)
+    return woven(near, far_pieces(near))
+
+
+def after(x, *first):
+    return lax.optimization_barrier((x, first))[0]
 
 
 def per_device(
@@ -927,26 +996,30 @@
 
     vectors = [
         (72, value_bias), (73, up_bias), (80, mix_bias), (64, first_gain), (65, skip_omega),
-        (66, second_gain), (67, down_bias), (74, latent_gains[0]), (75, latent_gains[1]),
-        (76, query_offset), (77, position_bias),
+        (66, second_gain), (67, down_bias), (74, latent_gains), (76, query_offset),
+        (77, position_bias),
     ]
-    plan, off = [], 0
+    plan = []
     for at, v in vectors:
-        plan.append((at, off, v.shape[0], spread(v.shape[0], devices)))
-        off += v.shape[0]
-    padded = ceil_div(off, TILE) * TILE
-    flat = jnp.concatenate([v for _, v in vectors] + [jnp.zeros((padded - off,), BF)])[None]
-    decs = jnp.concatenate([decay_alpha, decay_delta, decay_beta, decay_eta], axis=1)
+        n = v.shape[-1]
+        plan.append((at, v.ndim, n, spread(n, devices)))
+    decs = [d.T for d in (decay_alpha, decay_delta, decay_beta, decay_eta)]
     placed = whole(
-        partial(place_kernel, plan=plan), struct((ROWS_SMALL, TILE), F32), n_in=2, name="place"
-    )(flat, decs)
-    small = lax.all_gather(placed, "seq", axis=0, tiled=False)
-
-    w1 = gather_pieces(jnp.concatenate([value_weight, mix_weight], axis=1), devices)
-    w2 = gather_pieces(
-        jnp.concatenate([jnp.concatenate([attend_weight, down_weight], axis=1), up_weight], axis=0),
-        devices,
-    )
+        partial(place_kernel, plan=plan), struct((ROWS_SMALL, TILE), F32),
+        n_in=4 + len(vectors), name="place", vmem=60,
+    )(*decs, *[v for _, v in vectors])
+    small = gather_pieces(placed, devices)
+
+    w1, w2 = whole(
+        pack_kernel,
+        [struct((held, nv + nm), BF), struct((nv // devices + held, 2 * width), BF)],
+        n_in=5,
+        name="pack",
+        vmem=60,
+    )(*lax.optimization_barrier(
+        (value_weight, mix_weight, attend_weight, down_weight, up_weight, small)
+    )[:5])
+    w1 = near_pieces(w1, devices)
 
     tok = tokens.reshape(count, width)
     cot = cotangent.reshape(count, width)
@@ -960,47 +1033,36 @@
             struct((count, width), BF), struct((count, TILE), F32),
             struct((dims * SUBS, width), F32), struct((msg_rows, width), BF),
         ],
-        [pltpu.VMEM((dims * SUBS, TILE), F32)],
-        n_in=3,
+        [pltpu.VMEM((dims * SUBS, TILE), F32), pltpu.VMEM((devices, ROWS_SMALL, TILE), F32)],
+        n_in=devices + 2,
         name="head",
-    )(small, tok, segments)
-
+        micros=6,
+    )(*small, tok, segments)
+
+    w2 = near_pieces(after(w2, msg), devices)
     onward = [
         lax.ppermute(msg, "seq", [(i, i + k) for i in range(devices - k)])
         for k in range(1, reach + 1)
     ]
 
-    def lane_block(rows):
-        return pl.BlockSpec((rows, TILE), lambda i: (0, i))
-
-    tile_block = pl.BlockSpec((None, count, TILE), lambda i: (i, 0, 0))
-
-    def fixed(shape):
-        return pl.BlockSpec(shape, lambda i: (0,) * len(shape))
-
     arrivals = [pltpu.VMEM((dims * SUBS, TILE), F32)] * reach
-    z, mlow, sp = pl.pallas_call(
+    z, mlow, sp = whole(
         partial(scan_kernel, reach=reach, dims=dims, seqs=seqs),
-        grid=(blocks,),
-        in_specs=[
-            tile_block, fixed((count, TILE)), lane_block(3 * dims), lane_block(72),
-            lane_block(dims * SUBS),
-        ] + [lane_block(msg_rows)] * reach,
-        out_specs=[
-            lane_block(count), lane_block(count),
-            pl.BlockSpec((steps, dims * SUBS, TILE), lambda i: (0, 0, i)),
+        [
+            struct((count, width), F32), struct((count, width), BF),
+            struct((blocks, steps, dims * SUBS, TILE), BF),
         ],
-        out_shape=[
-            struct((count, width), F32), struct((count, width), BF),
-            struct((steps, dims * SUBS, width), F32),
-        ],
-        scratch_shapes=[
+        [
             pltpu.VMEM((dims * SUBS, TILE), F32), pltpu.VMEM((SUBS, TILE), F32),
-            pltpu.VMEM((count, TILE), F32),
+            pltpu.VMEM((blocks, count, TILE), F32),
         ] + arrivals,
-        compiler_params=PARAMS,
+        n_in=5 + reach,
         name="scan",
+        micros=8,
     )(nrm, lab, dk, pd, fin, *onward)
+
+    early, late = w1[:-1], w1[-1:]
+    w1 = woven(w1, far_pieces(after(early, onward)) + far_pieces(after(late, z)))
 
     def sems(n):
         return pltpu.SemaphoreType.DMA((n, devices))
@@ -1016,8 +1078,10 @@
         [pltpu.VMEM((width, nv + nm), BF), pltpu.VMEM((count, nv), F32), sems(1)],
         in_specs=[HB] * devices + [VM] * 7,
         name="front",
+        micros=11,
     )(*w1, nlow, mlow, pv, pm, pz, lab, segments)
 
+    w2 = woven(w2, far_pieces(after(w2, glow)))
     half = devices // 2
     rows2, rows1 = nv // devices // depth, held // depth
     piece_a = struct((half, depth, rows2 + rows1, 2 * width), BF)
@@ -1038,13 +1102,14 @@
         ],
         in_specs=[HB] * devices + [VM] * 9,
         name="middle",
+        micros=19,
     )(*w2, tok, cot, upd, ext, rs, ad, glow, pd, pv)
 
     vgl, bll, gs, gnp, w512, w1024, w128, back_msg, ach = whole(
         partial(back_kernel, devices=devices, dims=dims),
         [
             struct((count, nv), BF), struct((count, zw), BF), struct((blocks, count, TILE), F32),
-            struct((count, width), F32), struct((8, width), F32), struct((8, nv), F32),
+            struct((blocks, count, TILE), F32), struct((8, width), F32), struct((8, nv), F32),
             struct((8, TILE), F32), struct((msg_rows, width), BF),
             struct((dims * SUBS, width), F32),
         ],
@@ -1054,6 +1119,7 @@
         ],
         in_specs=[HB] * devices + [VM] * 15,
         name="back",
+        micros=15,
     )(*w1, probs, attg, vlow, dval, qlow, klow, lat, blu, blre, z, nrm, pd, pz, dk, lab)
 
     backward = [
@@ -1068,36 +1134,24 @@
         [pltpu.VMEM((width, nv + nm), BF)],
         n_in=6,
         name="weights",
+        micros=6,
     )(nlow, mlow, vgl, blu, bll, blre)
 
     piece_c = struct((half, ROWS_SMALL, TILE), F32)
     wide = ceil_div(nm, TILE) + 2
-    tokens_grad, own_c, sib_c = pl.pallas_call(
+    tokens_grad, own_c, sib_c = whole(
         partial(last_kernel, reach=reach, devices=devices, dims=dims, seqs=seqs, nm=nm),
-        grid=(blocks,),
-        in_specs=[
-            pl.BlockSpec((steps, dims * SUBS, TILE), lambda i: (0, 0, i)), tile_block,
-            tile_block, lane_block(count), fixed((count, TILE)), lane_block(3 * dims),
-            lane_block(72), lane_block(dims * SUBS),
-        ] + [lane_block(msg_rows)] * reach + [
-            fixed((count, width)), fixed((count, width)), fixed((72, width)), fixed((8, width)),
-            fixed((8, nv)), fixed((8, width)), fixed((8, nv)), fixed((8, TILE)),
-        ],
-        out_specs=[
-            fixed((count, width)), fixed(piece_c.shape), fixed(piece_c.shape),
-        ],
-        out_shape=[struct((count, width), F32), piece_c, piece_c],
-        scratch_shapes=[
+        [struct((count, width), F32), piece_c, piece_c],
+        [
             pltpu.VMEM((dims * SUBS, TILE), F32), pltpu.VMEM((SUBS, TILE), F32),
-            pltpu.VMEM((count, TILE), F32), pltpu.VMEM((count, width), F32),
-            pltpu.VMEM((72, width), F32), pltpu.VMEM((8, nv), F32),
-            pltpu.VMEM((8, wide * TILE), F32),
+            pltpu.VMEM((blocks, count, TILE), F32), pltpu.VMEM((72, width), F32),
+            pltpu.VMEM((8, nv), F32), pltpu.VMEM((8, wide * TILE), F32),
+            pltpu.VMEM((2 * dims, width), F32),
         ] + arrivals,
-        compiler_params=PARAMS,
+        n_in=15 + reach,
         name="last",
-    )(
-        sp, nrm, gs, gnp, lab, dk, pd, ach, *backward, tok, gin, pd, v512, v1024, w512, w1024, w128
-    )
+        micros=12,
+    )(sp, nrm, gs, gnp, lab, dk, ach, *backward, tok, gin, pd, v512, v1024, w512, w1024, w128)
 
     sum_a = join(deal(across(fold(own_a, sib_a, BF)), depth))
     attend_grad, down_grad, up_grad = whole(
@@ -1121,30 +1175,27 @@
     parts_c = across(fold(own_c, sib_c, F32))
     shard_c = whole(total_kernel, struct(piece_c.shape[1:], F32), n_in=half, name="total")(*parts_c)
     all_c = [shard_c] + [hop(shard_c, "grp", k) for k in range(1, depth)]
-    most = max(nt for _, _, _, nt in plan)
-    dec_grad, flat_grad = whole(
+    alpha_g, delta_g, beta_g, eta_g, value_b, up_b, mix_b, first_g, omega, second_g, down_b, gains_g, qoff, posb = whole(
         partial(final_kernel, depth=depth, plan=plan, held=held, dims=dims),
-        [struct((held, 4 * dims), F32), struct((16, most * TILE), F32)],
+        [struct((dims, held), F32)] * 4 + [struct(v.shape, F32) for _, v in vectors],
         [pltpu.VMEM((depth,) + piece_c.shape[1:], F32)],
         n_in=depth,
         name="final",
     )(*all_c)
-    grads = [flat_grad[j, :n] for j, (_, _, n, _) in enumerate(plan)]
-    value_b, up_b, mix_b, first_g, omega, second_g, down_b, g0, g1, qoff, posb = grads
     return (
         out.reshape(tokens.shape),
         tokens_grad.reshape(tokens.shape),
         first_g,
         value_grad,
         value_b,
-        dec_grad[:, 0:dims],
-        dec_grad[:, dims : 2 * dims],
-        dec_grad[:, 2 * dims : 3 * dims],
-        dec_grad[:, 3 * dims :],
+        alpha_g.T,
+        delta_g.T,
+        beta_g.T,
+        eta_g.T,
         omega,
         mix_grad,
         mix_b,
-        jnp.stack([g0, g1]),
+        gains_g,
         qoff,
         posb,
         attend_grad,

time: 305 us -> 177 us (0.58)
  Pallas kernels: 135 us -> 67.1 us
  local copies, waits for them, and re-layouts: 32.6 us -> 2.53 us
  blocking collectives: 26.1 us -> 0 us
  waiting for transfers between devices: 51.5 us -> 47.8 us
    all_gather x1 -> x0, blocking collectives: 26.1 us -> none  [per_device(): small = lax.all_gather(placed, 'seq', axis=0, tiled=False)]
    pallas_call x1, Pallas kernels: 30.2 us -> 13.3 us  [per_device(): whole(partial(middle_kernel, devices=devices, depth=depth, dims=dims), [s...]
    unnamed x113 -> x16, local copies, waits for them, and re-layouts: 17.6 us -> 2.53 us
    pallas_call x1, Pallas kernels: 11.5 us -> 2.32 us  [per_device(): whole(partial(weight_kernel, devices=devices, depth=depth), [piece_b, pie...]
    pallas_call x1, Pallas kernels: 15 us -> 6.78 us  [per_device(): whole(partial(front_kernel, devices=devices), [struct((count, nv), BF), s...]
    pallas_call x3, Pallas kernels: 8.28 us -> 0.73 us  [fold(): return whole(fold_kernel, outs, n_in=2, name='fold')(own, got)]
    concatenate x2 -> x0, local copies, waits for them, and re-layouts: 7.09 us -> none  [the longest x1 6.11 us: per_device(): jnp.concatenate([v for _, v in vectors] + [jnp.zeros((padded - off,), BF)])]
    pallas_call x2 -> x3, Pallas kernels: 30.4 us -> 23.5 us  [the longest x1 16 us: per_device(): whole(partial(last_kernel, reach=reach, devices=devices, dims=dims, seqs=...]
  transfers between devices with their start and end apart: 45 -> 52, of which waited for: 12 -> 23; matrix products, arithmetic and copies ran while one was open for 7% -> 0% of each run, Pallas kernels for 34% -> 28%
where the time goes in v2:
time: 177 us
  Pallas kernels  67.1 us (38%)
  starting transfers between devices  58.3 us (33%)
  waiting for transfers between devices  47.8 us (27%)
  local copies, waits for them, and re-layouts  2.53 us (1%)
    ppermute x48, starting transfers between devices, hop(): return lax.ppermute(x, axis, [(i, i ^ k) for i in range(length)])  51 us
    ppermute x48, waiting for transfers between devices, hop(): return lax.ppermute(x, axis, [(i, i ^ k) for i in range(length)])  40.6 us
    pallas_call x1, Pallas kernels, per_device(): whole(partial(last_kernel, reach=reach, devices=devices, dims=dims, seqs=...  16 us
    pallas_call x1, Pallas kernels, per_device(): whole(partial(middle_kernel, devices=devices, depth=depth, dims=dims), [s...  13.3 us
    pallas_call x1, Pallas kernels, per_device(): whole(partial(back_kernel, devices=devices, dims=dims), [struct((count, n...  12 us
    pallas_call x1, Pallas kernels, per_device(): whole(partial(front_kernel, devices=devices), [struct((count, nv), BF), s...  6.78 us
    ppermute x2, waiting for transfers between devices, per_device(): lax.ppermute(back_msg, 'seq', [(i + k, i) for i in range(devices - k)])  6.3 us
    pallas_call x1, Pallas kernels, per_device(): whole(partial(scan_kernel, reach=reach, dims=dims, seqs=seqs), [struct((c...  5.38 us
  transfers between devices with their start and end apart: 52, of which 23 were waited for; matrix products, arithmetic and copies ran while one was open for 0% of the time, Pallas kernels for 28%

profile of v2, /device:TPU:0, one launch (start us, length us, event | category | flops | bytes accessed | tf_op | source)
XLA Modules:
  0.0 176.6 jit_solution(265988379493260886)
XLA Ops:
  0.7 1.7 place.1.refs_0_
  2.3 3.9 %collective-permute-start.5 = (f32[88,128]{1,0:T(8,128)}, f32[88,128]{1,0:T(8,128)S(1)}, u32[]{:S(2)}, u32[]{:S(2)}) collective-permute-start(f32[88,128]{1,0:T(8,128)} %place.1.refs_0_), channel_id=1, source_target_pairs={{0,6},{1,7},{2,4},{3,5},{4,2},{5,3},{6,0},{7,1},{8,14},{9,15},{10,... | collective-permute-start | bytes 135176 | tf_op jit(solution)/shard_map/ppermute | solution.py:849
  6.8 1.7 collective-permute-done.5.refs_6_
  8.5 2.0 %collective-permute-done.3.refs_4_ = f32[88,128]{1,0:T(8,128)S(1)} collective-permute-done((f32[88,128]{1,0:T(8,128)}, f32[88,128]{1,0:T(8,128)S(1)}, u32[]{:S(2)}, u32[]{:S(2)}) %collective-permute-start.3) | collective-permute-done | bytes 45088 | tf_op jit(solution)/shard_map/ppermute | solution.py:849
  12.2 2.1 %pack.1 = (bf16[64,3200]{1,0:T(8,128)(2,1)}, bf16[192,1024]{1,0:T(8,128)(2,1)}) custom-call(bf16[64,1024]{1,0:T(8,128)(2,1)} %value, bf16[64,2176]{1,0:T(8,128)(2,1)} %mix, bf16[128,512]{1,0:T(8,128)(2,1)} %attend, bf16[128,512]{1,0:T(8,128)(2,1)} %down, bf16[64,1024]{1,0:T(8,128)(2,1)} %up), custom_call_target="tpu_custom_call" | custom-call | bytes 7380000 | tf_op jit(solution)/shard_map/pack/pallas_call | solution.py:1013
  14.3 1.5 collective-permute-start.11
  16.3 1.0 copy-done
  17.4 0.8 copy-done.5
  18.9 3.1 %head.1 = (f32[72,512]{1,0:T(8,128)S(1)}, f32[8,1024]{1,0:T(8,128)S(1)}, f32[8,128]{1,0:T(8,128)S(1)}, f32[8,2176]{1,0:T(8,128)S(1)}, f32[48,512]{1,0:T(8,128)S(...) custom-call(f32[88,128]{1,0:T(8,128)S(1)} %copy-done.5, ...), custom_call_target="tpu_custom_call" | custom-call | bytes 22140000 | tf_op jit(solution)/shard_map/head/pallas_call | solution.py:1028
  22.0 3.4 %collective-permute-start.13 = (bf16[80,512]{1,0:T(8,128)(2,1)S(1)}, bf16[80,512]{1,0:T(8,128)(2,1)S(1)}, u32[]{:S(2)}, u32[]{:S(2)}) collective-permute-start(bf16[80,512]{1,0:T(8,128)(2,1)S(1)} %get-tuple-element.129), channel_id=1, source_target_pairs={{0,2},{1,3},{2,4},{3,5},{4,6},{5,7},{8,10},{9,11},{10,12},{11,13},... | collective-permute-start | bytes 245768 | tf_op jit(solution)/shard_map/ppermute | solution.py:1044
  25.4 1.3 collective-permute-start.12
  28.1 1.6 collective-permute-start.14
  29.8 5.4 %scan.1 = (f32[512,512]{1,0:T(8,128)S(1)}, bf16[512,512]{1,0:T(8,128)(2,1)S(1)}, bf16[4,64,128,128]{3,2,1,0:T(8,128)(2,1)S(1)}) custom-call(f32[4,512,128]{2,1,0:T(8,128)S(1)} %get-tuple-element.135.refs_0_.refs_18_.refs_1_, f32[512,128]{1,0:T(8,128)S(1)} %get-tuple-element.136.refs_1_.refs_13_.refs_22_.refs_4_, ...), custom_call_target="tpu_custom_call" | custom-call | bytes 29520000 | tf_op jit(solution)/shard_map/scan/pallas_call | solution.py:1049
  35.7 4.4 %collective-permute-done.17.refs_6_ = bf16[64,3200]{1,0:T(8,128)(2,1)S(1)} collective-permute-done((bf16[64,3200]{1,0:T(8,128)(2,1)}, bf16[64,3200]{1,0:T(8,128)(2,1)S(1)}, u32[]{:S(2)}, u32[]{:S(2)}) %collective-permute-start.17) | collective-permute-done | bytes 409632 | tf_op jit(solution)/shard_map/ppermute | solution.py:849
  40.8 1.5 collective-permute-start.8
  42.3 1.4 collective-permute-start.7
  43.7 6.8 %front.1 = (bf16[512,1024]{1,0:T(8,128)(2,1)S(1)}, bf16[512,1024]{1,0:T(8,128)(2,1)S(1)}, f32[512,512]{1,0:T(8,128)S(1)}, f32[512,512]{1,0:T(8,128)S(1)}, f32[51...) custom-call(bf16[64,3200]{1,0:T(8,128)(2,1)S(1)} %copy-done.2, ...), custom_call_target="tpu_custom_call" | custom-call | bytes 40590000 | tf_op jit(solution)/shard_map/front/pallas_call | solution.py:1070
  50.5 2.5 %collective-permute-done.9.refs_6_ = bf16[192,1024]{1,0:T(8,128)(2,1)S(1)} collective-permute-done((bf16[192,1024]{1,0:T(8,128)(2,1)S(1)}, bf16[192,1024]{1,0:T(8,128)(2,1)S(1)}, u32[]{:S(2)}, u32[]{:S(2)}) %collective-permute-start.9) | collective-permute-done | bytes 393248 | tf_op jit(solution)/shard_map/ppermute | solution.py:849
  53.1 7.1 %collective-permute-done.8.refs_4_ = bf16[192,1024]{1,0:T(8,128)(2,1)S(1)} collective-permute-done((bf16[192,1024]{1,0:T(8,128)(2,1)S(1)}, bf16[192,1024]{1,0:T(8,128)(2,1)S(1)}, u32[]{:S(2)}, u32[]{:S(2)}) %collective-permute-start.8) | collective-permute-done | bytes 393248 | tf_op jit(solution)/shard_map/ppermute | solution.py:849
  64.2 13.3 %middle.1 = (f32[512,512]{1,0:T(8,128)}, f32[512,512]{1,0:T(8,128)S(1)}, bf16[512,1024]{1,0:T(8,128)(2,1)S(1)}, bf16[512,512]{1,0:T(8,128)(2,1)S(1)}, bf16[512,1...) custom-call(bf16[192,1024]{1,0:T(8,128)(2,1)S(1)} %copy-done.4, ...), custom_call_target="tpu_custom_call" | custom-call | bytes 70110000 | tf_op jit(solution)/shard_map/middle/pallas_call | solution.py:1088
  77.7 12.0 %back.1 = (bf16[512,1024]{1,0:T(8,128)(2,1)S(1)}, bf16[512,128]{1,0:T(8,128)(2,1)S(1)}, f32[4,512,128]{2,1,0:T(8,128)S(1)}, f32[4,512,128]{2,1,0:T(8,128)S(1)}, ...) custom-call(bf16[64,3200]{1,0:T(8,128)(2,1)S(1)} %copy-done.2, ...), custom_call_target="tpu_custom_call" | custom-call | bytes 55350000 | tf_op jit(solution)/shard_map/back/pallas_call | solution.py:1108
  89.8 2.3 %weights.1 = (bf16[4,4,16,3200]{3,2,1,0:T(8,128)(2,1)S(1)}, bf16[4,4,16,3200]{3,2,1,0:T(8,128)(2,1)S(1)}) custom-call(bf16[512,512]{1,0:T(8,128)(2,1)S(1)} %get-tuple-element.142.refs_8_.nlow, bf16[512,512]{1,0:T(8,128)(2,1)S(1)} %get-tuple-element.143.refs_9_.mlow, bf16[512,1024]{1,0:T(8,128)(2,1)S(1)} %get-tuple-element.185.vgl, ...), custom_call_target="tpu_custom_call" | custom-call | bytes 22140000 | tf_op jit(solution)/shard_map/weights/pallas_call | solution.py:1131
  94.1 1.3 collective-permute-start.24
  95.4 1.3 collective-permute-start.23
  97.0 3.3 %collective-permute-start.33 = (bf16[4,16,3200]{2,1,0:T(8,128)(2,1)S(1)}, bf16[4,16,3200]{2,1,0:T(8,128)(2,1)S(1)}, u32[]{:S(2)}, u32[]{:S(2)}) collective-permute-start(bf16[4,16,3200]{2,1,0:T(8,128)(2,1)S(1)} %get-tuple-element.190), channel_id=1, source_target_pairs={{0,2},{1,3},{2,0},{3,1},{4,6},{5,7},{6,4},{7,5},{8,10},{9,11},{10,... | collective-permute-start | bytes 1228808 | tf_op jit(solution)/shard_map/ppermute | solution.py:849
  100.4 6.3 %collective-permute-done.24.refs_8_ = bf16[80,512]{1,0:T(8,128)(2,1)S(1)} collective-permute-done((bf16[80,512]{1,0:T(8,128)(2,1)S(1)}, bf16[80,512]{1,0:T(8,128)(2,1)S(1)}, u32[]{:S(2)}, u32[]{:S(2)}) %collective-permute-start.24) | collective-permute-done | bytes 81952 | tf_op jit(solution)/shard_map/ppermute | solution.py:1126
  106.7 2.0 %collective-permute-start.34 = (bf16[4,16,3200]{2,1,0:T(8,128)(2,1)S(1)}, bf16[4,16,3200]{2,1,0:T(8,128)(2,1)S(1)}, u32[]{:S(2)}, u32[]{:S(2)}) collective-permute-start(bf16[4,16,3200]{2,1,0:T(8,128)(2,1)S(1)} %get-tuple-element.191), channel_id=1, source_target_pairs={{0,4},{1,5},{2,6},{3,7},{4,0},{5,1},{6,2},{7,3},{8,12},{9,13},{10,... | collective-permute-start | bytes 1228808 | tf_op jit(solution)/shard_map/ppermute | solution.py:849
  108.7 1.8 %collective-permute-start.35 = (bf16[4,16,3200]{2,1,0:T(8,128)(2,1)S(1)}, bf16[4,16,3200]{2,1,0:T(8,128)(2,1)S(1)}, u32[]{:S(2)}, u32[]{:S(2)}) collective-permute-start(bf16[4,16,3200]{2,1,0:T(8,128)(2,1)S(1)} %get-tuple-element.192), channel_id=1, source_target_pairs={{0,6},{1,7},{2,4},{3,5},{4,2},{5,3},{6,0},{7,1},{8,14},{9,15},{10,... | collective-permute-start | bytes 1228808 | tf_op jit(solution)/shard_map/ppermute | solution.py:849
  110.5 16.0 %last.1 = (f32[512,512]{1,0:T(8,128)}, f32[4,88,128]{2,1,0:T(8,128)S(1)}, f32[4,88,128]{2,1,0:T(8,128)S(1)}) custom-call(bf16[4,64,128,128]{3,2,1,0:T(8,128)(2,1)S(1)} %get-tuple-element.157.refs_0_, f32[4,512,128]{2,1,0:T(8,128)S(1)} %get-tuple-element.135.refs_0_.refs_18_.refs_1_, f32[4,512,128]{2,1,0:T(8,128)S(1)} %get-tuple-element.167.refs_2_, ...), custom_call_target="tpu_custom_call" | custom-call | bytes 44280000 | tf_op jit(solution)/shard_map/last/pallas_call | solution.py:1142
  126.8 1.9 %collective-permute-start.46 = (bf16[48,1024]{1,0:T(8,128)(2,1)S(1)}, bf16[48,1024]{1,0:T(8,128)(2,1)S(1)}, u32[]{:S(2)}, u32[]{:S(2)}) collective-permute-start(bf16[48,1024]{1,0:T(8,128)(2,1)S(1)} %get-tuple-element.216), channel_id=1, source_target_pairs={{0,8},{8,0},{16,24},{24,16},{1,9},{9,1},{17,25},{25,17},{2,10},{10... | collective-permute-start | bytes 294920 | tf_op jit(solution)/shard_map/ppermute | solution.py:849
  128.7 2.6 %collective-permute-start.47 = (bf16[48,1024]{1,0:T(8,128)(2,1)S(1)}, bf16[48,1024]{1,0:T(8,128)(2,1)S(1)}, u32[]{:S(2)}, u32[]{:S(2)}) collective-permute-start(bf16[48,1024]{1,0:T(8,128)(2,1)S(1)} %get-tuple-element.217), channel_id=1, source_target_pairs={{0,16},{8,24},{16,0},{24,8},{1,17},{9,25},{17,1},{25,9},{2,18},{10... | collective-permute-start | bytes 294920 | tf_op jit(solution)/shard_map/ppermute | solution.py:849
  131.3 4.4 %collective-permute-done.34.refs_2_ = bf16[4,16,3200]{2,1,0:T(8,128)(2,1)S(1)} collective-permute-done((bf16[4,16,3200]{2,1,0:T(8,128)(2,1)S(1)}, bf16[4,16,3200]{2,1,0:T(8,128)(2,1)S(1)}, u32[]{:S(2)}, u32[]{:S(2)}) %collective-permute-start.34) | collective-permute-done | bytes 409632 | tf_op jit(solution)/shard_map/ppermute | solution.py:849
  135.7 4.2 %collective-permute-start.48 = (bf16[48,1024]{1,0:T(8,128)(2,1)S(1)}, bf16[48,1024]{1,0:T(8,128)(2,1)S(1)}, u32[]{:S(2)}, u32[]{:S(2)}) collective-permute-start(bf16[48,1024]{1,0:T(8,128)(2,1)S(1)} %get-tuple-element.218), channel_id=1, source_target_pairs={{0,24},{8,16},{16,8},{24,0},{1,25},{9,17},{17,9},{25,1},{2,26},{10... | collective-permute-start | bytes 294920 | tf_op jit(solution)/shard_map/ppermute | solution.py:849
  140.9 1.5 collective-permute-start.26
  143.5 3.9 %collective-permute-start.38 = (bf16[16,3200]{1,0:T(8,128)(2,1)S(1)}, bf16[16,3200]{1,0:T(8,128)(2,1)S(1)}, u32[]{:S(2)}, u32[]{:S(2)}) collective-permute-start(bf16[16,3200]{1,0:T(8,128)(2,1)S(1)} %get-tuple-element.196), channel_id=1, source_target_pairs={{0,24},{8,16},{16,8},{24,0},{1,25},{9,17},{17,9},{25,1},{2,26},{10... | collective-permute-start | bytes 307208 | tf_op jit(solution)/shard_map/ppermute | solution.py:849
  147.5 1.4 collective-permute-start.51
  148.8 1.2 collective-permute-start.28
  150.0 3.8 %collective-permute-done.28.refs_3_ = f32[88,128]{1,0:T(8,128)S(1)} collective-permute-done((f32[88,128]{1,0:T(8,128)S(1)}, f32[88,128]{1,0:T(8,128)S(1)}, u32[]{:S(2)}, u32[]{:S(2)}) %collective-permute-start.28) | collective-permute-done | bytes 45088 | tf_op jit(solution)/shard_map/ppermute | solution.py:849
  153.8 2.6 %collective-permute-start.31 = (f32[88,128]{1,0:T(8,128)S(1)}, f32[88,128]{1,0:T(8,128)S(1)}, u32[]{:S(2)}, u32[]{:S(2)}) collective-permute-start(f32[88,128]{1,0:T(8,128)S(1)} %total.1.refs_0_), channel_id=1, source_target_pairs={{0,24},{8,16},{16,8},{24,0},{1,25},{9,17},{17,9},{25,1},{2,26},{10... | collective-permute-start | bytes 135176 | tf_op jit(solution)/shard_map/ppermute | solution.py:849
  156.4 1.8 %collective-permute-start.29 = (f32[88,128]{1,0:T(8,128)S(1)}, f32[88,128]{1,0:T(8,128)S(1)}, u32[]{:S(2)}, u32[]{:S(2)}) collective-permute-start(f32[88,128]{1,0:T(8,128)S(1)} %total.1.refs_0_), channel_id=1, source_target_pairs={{0,8},{8,0},{16,24},{24,16},{1,9},{9,1},{17,25},{25,17},{2,10},{10... | collective-permute-start | bytes 135176 | tf_op jit(solution)/shard_map/ppermute | solution.py:849
  158.3 2.6 %collective-permute-start.41 = (bf16[16,3200]{1,0:T(8,128)(2,1)S(1)}, bf16[16,3200]{1,0:T(8,128)(2,1)S(1)}, u32[]{:S(2)}, u32[]{:S(2)}) collective-permute-start(bf16[16,3200]{1,0:T(8,128)(2,1)S(1)} %join.2.refs_0_), channel_id=1, source_target_pairs={{0,24},{8,16},{16,8},{24,0},{1,25},{9,17},{17,9},{25,1},{2,26},{10... | collective-permute-start | bytes 307208 | tf_op jit(solution)/shard_map/ppermute | solution.py:849
  160.9 1.9 %collective-permute-start.40 = (bf16[16,3200]{1,0:T(8,128)(2,1)S(1)}, bf16[16,3200]{1,0:T(8,128)(2,1)S(1)}, u32[]{:S(2)}, u32[]{:S(2)}) collective-permute-start(bf16[16,3200]{1,0:T(8,128)(2,1)S(1)} %join.2.refs_0_), channel_id=1, source_target_pairs={{0,16},{8,24},{16,0},{24,8},{1,17},{9,25},{17,1},{25,9},{2,18},{10... | collective-permute-start | bytes 307208 | tf_op jit(solution)/shard_map/ppermute | solution.py:849
  162.9 2.1 %collective-permute-done.30.refs_2_ = f32[88,128]{1,0:T(8,128)S(1)} collective-permute-done((f32[88,128]{1,0:T(8,128)S(1)}, f32[88,128]{1,0:T(8,128)S(1)}, u32[]{:S(2)}, u32[]{:S(2)}) %collective-permute-start.30) | collective-permute-done | bytes 45088 | tf_op jit(solution)/shard_map/ppermute | solution.py:849
  165.3 1.7 collective-permute-start.49
  167.1 0.9 final.1
  168.0 6.1 %collective-permute-done.50.refs_2_ = bf16[48,1024]{1,0:T(8,128)(2,1)S(1)} collective-permute-done((bf16[48,1024]{1,0:T(8,128)(2,1)S(1)}, bf16[48,1024]{1,0:T(8,128)(2,1)S(1)}, u32[]{:S(2)}, u32[]{:S(2)}) %collective-permute-start.50) | collective-permute-done | bytes 98336 | tf_op jit(solution)/shard_map/ppermute | solution.py:849
  174.6 1.0 spread_a.1
  175.6 1.0 spread_b.1
  (92 shorter events, 16.2 us)
Async XLA Ops:
  2.3 6.1 %collective-permute-start.5 = (f32[88,128]{1,0:T(8,128)}, f32[88,128]{1,0:T(8,128)S(1)}, u32[]{:S(2)}, u32[]{:S(2)}) collective-permute-start(f32[88,128]{1,0:T(8,128)} %place.1.refs_0_), channel_id=1, source_target_pairs={{0,6},{1,7},{2,4},{3,5},{4,2},{5,3},{6,0},{7,1},{8,14},{9,15},{10,... | collective-permute-start | bytes 135176 | tf_op jit(solution)/shard_map/ppermute | solution.py:849
  6.2 4.3 %collective-permute-start.3 = (f32[88,128]{1,0:T(8,128)}, f32[88,128]{1,0:T(8,128)S(1)}, u32[]{:S(2)}, u32[]{:S(2)}) collective-permute-start(f32[88,128]{1,0:T(8,128)} %place.1.refs_0_), channel_id=1, source_target_pairs={{0,4},{1,5},{2,6},{3,7},{4,0},{5,1},{6,2},{7,3},{8,12},{9,13},{10,... | collective-permute-start | bytes 135176 | tf_op jit(solution)/shard_map/ppermute | solution.py:849
  6.7 4.3 %collective-permute-start.1 = (f32[88,128]{1,0:T(8,128)}, f32[88,128]{1,0:T(8,128)S(1)}, u32[]{:S(2)}, u32[]{:S(2)}) collective-permute-start(f32[88,128]{1,0:T(8,128)} %place.1.refs_0_), channel_id=1, source_target_pairs={{0,2},{1,3},{2,0},{3,1},{4,6},{5,7},{6,4},{7,5},{8,10},{9,11},{10,... | collective-permute-start | bytes 135176 | tf_op jit(solution)/shard_map/ppermute | solution.py:849
  6.8 4.2 %collective-permute-start = (f32[88,128]{1,0:T(8,128)}, f32[88,128]{1,0:T(8,128)S(1)}, u32[]{:S(2)}, u32[]{:S(2)}) collective-permute-start(f32[88,128]{1,0:T(8,128)} %place.1.refs_0_), channel_id=1, source_target_pairs={{0,1},{1,0},{2,3},{3,2},{4,5},{5,4},{6,7},{7,6},{8,9},{9,8},{10,11... | collective-permute-start | bytes 135176 | tf_op jit(solution)/shard_map/ppermute | solution.py:849
  8.5 2.5 %collective-permute-start.6 = (f32[88,128]{1,0:T(8,128)S(1)}, f32[88,128]{1,0:T(8,128)S(1)}, u32[]{:S(2)}, u32[]{:S(2)}) collective-permute-start(f32[88,128]{1,0:T(8,128)S(1)} %collective-permute-done.5.refs_6_), channel_id=1, source_target_pairs={{0,1},{1,0},{2,3},{3,2},{4,5},{5,4},{6,7},{7,6},{8,9},{9,8},{10,11... | collective-permute-start | bytes 135176 | tf_op jit(solution)/shard_map/ppermute | solution.py:849
  14.3 13.3 %collective-permute-start.11 = (bf16[64,3200]{1,0:T(8,128)(2,1)}, bf16[64,3200]{1,0:T(8,128)(2,1)S(1)}, u32[]{:S(2)}, u32[]{:S(2)}) collective-permute-start(bf16[64,3200]{1,0:T(8,128)(2,1)} %get-tuple-element.132.refs_0_), channel_id=1, source_target_pairs={{0,4},{1,5},{2,6},{3,7},{4,0},{5,1},{6,2},{7,3},{8,12},{9,13},{10,... | collective-permute-start | bytes 1228808 | tf_op jit(solution)/shard_map/ppermute | solution.py:849
  15.8 12.3 %collective-permute-start.10 = (bf16[64,3200]{1,0:T(8,128)(2,1)}, bf16[64,3200]{1,0:T(8,128)(2,1)S(1)}, u32[]{:S(2)}, u32[]{:S(2)}) collective-permute-start(bf16[64,3200]{1,0:T(8,128)(2,1)} %get-tuple-element.132.refs_0_), channel_id=1, source_target_pairs={{0,2},{1,3},{2,0},{3,1},{4,6},{5,7},{6,4},{7,5},{8,10},{9,11},{10,... | collective-permute-start | bytes 1228808 | tf_op jit(solution)/shard_map/ppermute | solution.py:849
  22.0 5.4 %collective-permute-start.13 = (bf16[80,512]{1,0:T(8,128)(2,1)S(1)}, bf16[80,512]{1,0:T(8,128)(2,1)S(1)}, u32[]{:S(2)}, u32[]{:S(2)}) collective-permute-start(bf16[80,512]{1,0:T(8,128)(2,1)S(1)} %get-tuple-element.129), channel_id=1, source_target_pairs={{0,2},{1,3},{2,4},{3,5},{4,6},{5,7},{8,10},{9,11},{10,12},{11,13},... | collective-permute-start | bytes 245768 | tf_op jit(solution)/shard_map/ppermute | solution.py:1044
  26.7 13.5 %collective-permute-start.17 = (bf16[64,3200]{1,0:T(8,128)(2,1)}, bf16[64,3200]{1,0:T(8,128)(2,1)S(1)}, u32[]{:S(2)}, u32[]{:S(2)}) collective-permute-start(bf16[64,3200]{1,0:T(8,128)(2,1)} %get-tuple-element.132.refs_0_), channel_id=1, source_target_pairs={{0,6},{1,7},{2,4},{3,5},{4,2},{5,3},{6,0},{7,1},{8,14},{9,15},{10,... | collective-permute-start | bytes 1228808 | tf_op jit(solution)/shard_map/ppermute | solution.py:849
  28.1 12.7 %collective-permute-start.14 = (bf16[64,3200]{1,0:T(8,128)(2,1)}, bf16[64,3200]{1,0:T(8,128)(2,1)S(1)}, u32[]{:S(2)}, u32[]{:S(2)}) collective-permute-start(bf16[64,3200]{1,0:T(8,128)(2,1)} %get-tuple-element.132.refs_0_), channel_id=1, source_target_pairs={{0,1},{1,0},{2,3},{3,2},{4,5},{5,4},{6,7},{7,6},{8,9},{9,8},{10,11... | collective-permute-start | bytes 1228808 | tf_op jit(solution)/shard_map/ppermute | solution.py:849
  29.8 12.5 %collective-permute-start.15 = (bf16[64,3200]{1,0:T(8,128)(2,1)S(1)}, bf16[64,3200]{1,0:T(8,128)(2,1)S(1)}, u32[]{:S(2)}, u32[]{:S(2)}) collective-permute-start(bf16[64,3200]{1,0:T(8,128)(2,1)S(1)} %collective-permute-done.10.refs_2_), channel_id=1, source_target_pairs={{0,1},{1,0},{2,3},{3,2},{4,5},{5,4},{6,7},{7,6},{8,9},{9,8},{10,11... | collective-permute-start | bytes 1228808 | tf_op jit(solution)/shard_map/ppermute | solution.py:849
  35.2 8.5 %collective-permute-start.16 = (bf16[64,3200]{1,0:T(8,128)(2,1)S(1)}, bf16[64,3200]{1,0:T(8,128)(2,1)S(1)}, u32[]{:S(2)}, u32[]{:S(2)}) collective-permute-start(bf16[64,3200]{1,0:T(8,128)(2,1)S(1)} %collective-permute-done.11.refs_4_), channel_id=1, source_target_pairs={{0,1},{1,0},{2,3},{3,2},{4,5},{5,4},{6,7},{7,6},{8,9},{9,8},{10,11... | collective-permute-start | bytes 1228808 | tf_op jit(solution)/shard_map/ppermute | solution.py:849
  40.1 3.6 %collective-permute-start.18 = (bf16[64,3200]{1,0:T(8,128)(2,1)S(1)}, bf16[64,3200]{1,0:T(8,128)(2,1)S(1)}, u32[]{:S(2)}, u32[]{:S(2)}) collective-permute-start(bf16[64,3200]{1,0:T(8,128)(2,1)S(1)} %collective-permute-done.17.refs_6_), channel_id=1, source_target_pairs={{0,1},{1,0},{2,3},{3,2},{4,5},{5,4},{6,7},{7,6},{8,9},{9,8},{10,11... | collective-permute-start | bytes 1228808 | tf_op jit(solution)/shard_map/ppermute | solution.py:849
  40.2 12.9 %collective-permute-start.9 = (bf16[192,1024]{1,0:T(8,128)(2,1)S(1)}, bf16[192,1024]{1,0:T(8,128)(2,1)S(1)}, u32[]{:S(2)}, u32[]{:S(2)}) collective-permute-start(bf16[192,1024]{1,0:T(8,128)(2,1)S(1)} %copy-done.4), channel_id=1, source_target_pairs={{0,6},{1,7},{2,4},{3,5},{4,2},{5,3},{6,0},{7,1},{8,14},{9,15},{10,... | collective-permute-start | bytes 1179656 | tf_op jit(solution)/shard_map/ppermute | solution.py:849
  40.8 19.3 %collective-permute-start.8 = (bf16[192,1024]{1,0:T(8,128)(2,1)S(1)}, bf16[192,1024]{1,0:T(8,128)(2,1)S(1)}, u32[]{:S(2)}, u32[]{:S(2)}) collective-permute-start(bf16[192,1024]{1,0:T(8,128)(2,1)S(1)} %copy-done.4), channel_id=1, source_target_pairs={{0,4},{1,5},{2,6},{3,7},{4,0},{5,1},{6,2},{7,3},{8,12},{9,13},{10,... | collective-permute-start | bytes 1179656 | tf_op jit(solution)/shard_map/ppermute | solution.py:849
  42.3 18.4 %collective-permute-start.7 = (bf16[192,1024]{1,0:T(8,128)(2,1)S(1)}, bf16[192,1024]{1,0:T(8,128)(2,1)S(1)}, u32[]{:S(2)}, u32[]{:S(2)}) collective-permute-start(bf16[192,1024]{1,0:T(8,128)(2,1)S(1)} %copy-done.4), channel_id=1, source_target_pairs={{0,2},{1,3},{2,0},{3,1},{4,6},{5,7},{6,4},{7,5},{8,10},{9,11},{10,... | collective-permute-start | bytes 1179656 | tf_op jit(solution)/shard_map/ppermute | solution.py:849
  60.7 2.3 %collective-permute-start.20 = (bf16[192,1024]{1,0:T(8,128)(2,1)S(1)}, bf16[192,1024]{1,0:T(8,128)(2,1)S(1)}, u32[]{:S(2)}, u32[]{:S(2)}) collective-permute-start(bf16[192,1024]{1,0:T(8,128)(2,1)S(1)} %collective-permute-done.7.refs_2_), channel_id=1, source_target_pairs={{0,1},{1,0},{2,3},{3,2},{4,5},{5,4},{6,7},{7,6},{8,9},{9,8},{10,11... | collective-permute-start | bytes 1179656 | tf_op jit(solution)/shard_map/ppermute | solution.py:849
  61.3 2.3 %collective-permute-start.21 = (bf16[192,1024]{1,0:T(8,128)(2,1)S(1)}, bf16[192,1024]{1,0:T(8,128)(2,1)S(1)}, u32[]{:S(2)}, u32[]{:S(2)}) collective-permute-start(bf16[192,1024]{1,0:T(8,128)(2,1)S(1)} %collective-permute-done.8.refs_4_), channel_id=1, source_target_pairs={{0,1},{1,0},{2,3},{3,2},{4,5},{5,4},{6,7},{7,6},{8,9},{9,8},{10,11... | collective-permute-start | bytes 1179656 | tf_op jit(solution)/shard_map/ppermute | solution.py:849
  61.3 2.9 %collective-permute-start.22 = (bf16[192,1024]{1,0:T(8,128)(2,1)S(1)}, bf16[192,1024]{1,0:T(8,128)(2,1)S(1)}, u32[]{:S(2)}, u32[]{:S(2)}) collective-permute-start(bf16[192,1024]{1,0:T(8,128)(2,1)S(1)} %collective-permute-done.9.refs_6_), channel_id=1, source_target_pairs={{0,1},{1,0},{2,3},{3,2},{4,5},{5,4},{6,7},{7,6},{8,9},{9,8},{10,11... | collective-permute-start | bytes 1179656 | tf_op jit(solution)/shard_map/ppermute | solution.py:849
  77.5 15.0 %collective-permute-start.42 = (bf16[4,4,48,1024]{3,2,1,0:T(8,128)(2,1)S(1)}, bf16[4,4,48,1024]{3,2,1,0:T(8,128)(2,1)S(1)}, u32[]{:S(2)}, u32[]{:S(2)}) collective-permute-start(bf16[4,4,48,1024]{3,2,1,0:T(8,128)(2,1)S(1)} %get-tuple-element.210), channel_id=1, source_target_pairs={{0,1},{1,0},{2,3},{3,2},{4,5},{5,4},{6,7},{7,6},{8,9},{9,8},{10,11... | collective-permute-start | bytes 4718600 | tf_op jit(solution)/shard_map/ppermute | solution.py:849
  92.1 4.5 %collective-permute-start.32 = (bf16[4,4,16,3200]{3,2,1,0:T(8,128)(2,1)S(1)}, bf16[4,4,16,3200]{3,2,1,0:T(8,128)(2,1)S(1)}, u32[]{:S(2)}, u32[]{:S(2)}) collective-permute-start(bf16[4,4,16,3200]{3,2,1,0:T(8,128)(2,1)S(1)} %get-tuple-element.188), channel_id=1, source_target_pairs={{0,1},{1,0},{2,3},{3,2},{4,5},{5,4},{6,7},{7,6},{8,9},{9,8},{10,11... | collective-permute-start | bytes 4915208 | tf_op jit(solution)/shard_map/ppermute | solution.py:849
  92.9 15.8 %collective-permute-start.43 = (bf16[4,48,1024]{2,1,0:T(8,128)(2,1)S(1)}, bf16[4,48,1024]{2,1,0:T(8,128)(2,1)S(1)}, u32[]{:S(2)}, u32[]{:S(2)}) collective-permute-start(bf16[4,48,1024]{2,1,0:T(8,128)(2,1)S(1)} %get-tuple-element.212), channel_id=1, source_target_pairs={{0,2},{1,3},{2,0},{3,1},{4,6},{5,7},{6,4},{7,5},{8,10},{9,11},{10,... | collective-permute-start | bytes 1179656 | tf_op jit(solution)/shard_map/ppermute | solution.py:849
  93.4 33.1 %collective-permute-start.44 = (bf16[4,48,1024]{2,1,0:T(8,128)(2,1)S(1)}, bf16[4,48,1024]{2,1,0:T(8,128)(2,1)S(1)}, u32[]{:S(2)}, u32[]{:S(2)}) collective-permute-start(bf16[4,48,1024]{2,1,0:T(8,128)(2,1)S(1)} %get-tuple-element.213), channel_id=1, source_target_pairs={{0,4},{1,5},{2,6},{3,7},{4,0},{5,1},{6,2},{7,3},{8,12},{9,13},{10,... | collective-permute-start | bytes 1179656 | tf_op jit(solution)/shard_map/ppermute | solution.py:849
  94.1 12.6 %collective-permute-start.24 = (bf16[80,512]{1,0:T(8,128)(2,1)S(1)}, bf16[80,512]{1,0:T(8,128)(2,1)S(1)}, u32[]{:S(2)}, u32[]{:S(2)}) collective-permute-start(bf16[80,512]{1,0:T(8,128)(2,1)S(1)} %get-tuple-element.170), channel_id=1, source_target_pairs={{2,0},{3,1},{4,2},{5,3},{6,4},{7,5},{10,8},{11,9},{12,10},{13,11},... | collective-permute-start | bytes 245768 | tf_op jit(solution)/shard_map/ppermute | solution.py:1126
  95.4 11.3 %collective-permute-start.23 = (bf16[80,512]{1,0:T(8,128)(2,1)S(1)}, bf16[80,512]{1,0:T(8,128)(2,1)S(1)}, u32[]{:S(2)}, u32[]{:S(2)}) collective-permute-start(bf16[80,512]{1,0:T(8,128)(2,1)S(1)} %get-tuple-element.170), channel_id=1, source_target_pairs={{1,0},{2,1},{3,2},{4,3},{5,4},{6,5},{7,6},{9,8},{10,9},{11,10},{12... | collective-permute-start | bytes 245768 | tf_op jit(solution)/shard_map/ppermute | solution.py:1126
  97.0 31.7 %collective-permute-start.33 = (bf16[4,16,3200]{2,1,0:T(8,128)(2,1)S(1)}, bf16[4,16,3200]{2,1,0:T(8,128)(2,1)S(1)}, u32[]{:S(2)}, u32[]{:S(2)}) collective-permute-start(bf16[4,16,3200]{2,1,0:T(8,128)(2,1)S(1)} %get-tuple-element.190), channel_id=1, source_target_pairs={{0,2},{1,3},{2,0},{3,1},{4,6},{5,7},{6,4},{7,5},{8,10},{9,11},{10,... | collective-permute-start | bytes 1228808 | tf_op jit(solution)/shard_map/ppermute | solution.py:849
  106.7 19.8 %collective-permute-start.45 = (bf16[4,48,1024]{2,1,0:T(8,128)(2,1)S(1)}, bf16[4,48,1024]{2,1,0:T(8,128)(2,1)S(1)}, u32[]{:S(2)}, u32[]{:S(2)}) collective-permute-start(bf16[4,48,1024]{2,1,0:T(8,128)(2,1)S(1)} %get-tuple-element.214), channel_id=1, source_target_pairs={{0,6},{1,7},{2,4},{3,5},{4,2},{5,3},{6,0},{7,1},{8,14},{9,15},{10,... | collective-permute-start | bytes 1179656 | tf_op jit(solution)/shard_map/ppermute | solution.py:849
  106.7 29.0 %collective-permute-start.34 = (bf16[4,16,3200]{2,1,0:T(8,128)(2,1)S(1)}, bf16[4,16,3200]{2,1,0:T(8,128)(2,1)S(1)}, u32[]{:S(2)}, u32[]{:S(2)}) collective-permute-start(bf16[4,16,3200]{2,1,0:T(8,128)(2,1)S(1)} %get-tuple-element.191), channel_id=1, source_target_pairs={{0,4},{1,5},{2,6},{3,7},{4,0},{5,1},{6,2},{7,3},{8,12},{9,13},{10,... | collective-permute-start | bytes 1228808 | tf_op jit(solution)/shard_map/ppermute | solution.py:849
  108.7 31.2 %collective-permute-start.35 = (bf16[4,16,3200]{2,1,0:T(8,128)(2,1)S(1)}, bf16[4,16,3200]{2,1,0:T(8,128)(2,1)S(1)}, u32[]{:S(2)}, u32[]{:S(2)}) collective-permute-start(bf16[4,16,3200]{2,1,0:T(8,128)(2,1)S(1)} %get-tuple-element.192), channel_id=1, source_target_pairs={{0,6},{1,7},{2,4},{3,5},{4,2},{5,3},{6,0},{7,1},{8,14},{9,15},{10,... | collective-permute-start | bytes 1228808 | tf_op jit(solution)/shard_map/ppermute | solution.py:849
  126.5 13.8 %collective-permute-start.25 = (f32[4,88,128]{2,1,0:T(8,128)S(1)}, f32[4,88,128]{2,1,0:T(8,128)S(1)}, u32[]{:S(2)}, u32[]{:S(2)}) collective-permute-start(f32[4,88,128]{2,1,0:T(8,128)S(1)} %get-tuple-element.179), channel_id=1, source_target_pairs={{0,1},{1,0},{2,3},{3,2},{4,5},{5,4},{6,7},{7,6},{8,9},{9,8},{10,11... | collective-permute-start | bytes 540680 | tf_op jit(solution)/shard_map/ppermute | solution.py:849
  126.8 14.0 %collective-permute-start.46 = (bf16[48,1024]{1,0:T(8,128)(2,1)S(1)}, bf16[48,1024]{1,0:T(8,128)(2,1)S(1)}, u32[]{:S(2)}, u32[]{:S(2)}) collective-permute-start(bf16[48,1024]{1,0:T(8,128)(2,1)S(1)} %get-tuple-element.216), channel_id=1, source_target_pairs={{0,8},{8,0},{16,24},{24,16},{1,9},{9,1},{17,25},{25,17},{2,10},{10... | collective-permute-start | bytes 294920 | tf_op jit(solution)/shard_map/ppermute | solution.py:849
  128.7 13.7 %collective-permute-start.47 = (bf16[48,1024]{1,0:T(8,128)(2,1)S(1)}, bf16[48,1024]{1,0:T(8,128)(2,1)S(1)}, u32[]{:S(2)}, u32[]{:S(2)}) collective-permute-start(bf16[48,1024]{1,0:T(8,128)(2,1)S(1)} %get-tuple-element.217), channel_id=1, source_target_pairs={{0,16},{8,24},{16,0},{24,8},{1,17},{9,25},{17,1},{25,9},{2,18},{10... | collective-permute-start | bytes 294920 | tf_op jit(solution)/shard_map/ppermute | solution.py:849
  135.7 7.8 %collective-permute-start.48 = (bf16[48,1024]{1,0:T(8,128)(2,1)S(1)}, bf16[48,1024]{1,0:T(8,128)(2,1)S(1)}, u32[]{:S(2)}, u32[]{:S(2)}) collective-permute-start(bf16[48,1024]{1,0:T(8,128)(2,1)S(1)} %get-tuple-element.218), channel_id=1, source_target_pairs={{0,24},{8,16},{16,8},{24,0},{1,25},{9,17},{17,9},{25,1},{2,26},{10... | collective-permute-start | bytes 294920 | tf_op jit(solution)/shard_map/ppermute | solution.py:849
  140.2 16.2 %collective-permute-start.36 = (bf16[16,3200]{1,0:T(8,128)(2,1)S(1)}, bf16[16,3200]{1,0:T(8,128)(2,1)S(1)}, u32[]{:S(2)}, u32[]{:S(2)}) collective-permute-start(bf16[16,3200]{1,0:T(8,128)(2,1)S(1)} %get-tuple-element.194), channel_id=1, source_target_pairs={{0,8},{8,0},{16,24},{24,16},{1,9},{9,1},{17,25},{25,17},{2,10},{10... | collective-permute-start | bytes 307208 | tf_op jit(solution)/shard_map/ppermute | solution.py:849
  140.3 16.1 %collective-permute-start.37 = (bf16[16,3200]{1,0:T(8,128)(2,1)S(1)}, bf16[16,3200]{1,0:T(8,128)(2,1)S(1)}, u32[]{:S(2)}, u32[]{:S(2)}) collective-permute-start(bf16[16,3200]{1,0:T(8,128)(2,1)S(1)} %get-tuple-element.195), channel_id=1, source_target_pairs={{0,16},{8,24},{16,0},{24,8},{1,17},{9,25},{17,1},{25,9},{2,18},{10... | collective-permute-start | bytes 307208 | tf_op jit(solution)/shard_map/ppermute | solution.py:849
  140.9 6.6 %collective-permute-start.26 = (f32[88,128]{1,0:T(8,128)S(1)}, f32[88,128]{1,0:T(8,128)S(1)}, u32[]{:S(2)}, u32[]{:S(2)}) collective-permute-start(f32[88,128]{1,0:T(8,128)S(1)} %get-tuple-element.181), channel_id=1, source_target_pairs={{0,2},{1,3},{2,0},{3,1},{4,6},{5,7},{6,4},{7,5},{8,10},{9,11},{10,... | collective-permute-start | bytes 135176 | tf_op jit(solution)/shard_map/ppermute | solution.py:849
  142.4 6.4 %collective-permute-start.27 = (f32[88,128]{1,0:T(8,128)S(1)}, f32[88,128]{1,0:T(8,128)S(1)}, u32[]{:S(2)}, u32[]{:S(2)}) collective-permute-start(f32[88,128]{1,0:T(8,128)S(1)} %get-tuple-element.182), channel_id=1, source_target_pairs={{0,4},{1,5},{2,6},{3,7},{4,0},{5,1},{6,2},{7,3},{8,12},{9,13},{10,... | collective-permute-start | bytes 135176 | tf_op jit(solution)/shard_map/ppermute | solution.py:849
  143.5 14.8 %collective-permute-start.38 = (bf16[16,3200]{1,0:T(8,128)(2,1)S(1)}, bf16[16,3200]{1,0:T(8,128)(2,1)S(1)}, u32[]{:S(2)}, u32[]{:S(2)}) collective-permute-start(bf16[16,3200]{1,0:T(8,128)(2,1)S(1)} %get-tuple-element.196), channel_id=1, source_target_pairs={{0,24},{8,16},{16,8},{24,0},{1,25},{9,17},{17,9},{25,1},{2,26},{10... | collective-permute-start | bytes 307208 | tf_op jit(solution)/shard_map/ppermute | solution.py:849
  147.5 17.9 %collective-permute-start.51 = (bf16[48,1024]{1,0:T(8,128)(2,1)S(1)}, bf16[48,1024]{1,0:T(8,128)(2,1)S(1)}, u32[]{:S(2)}, u32[]{:S(2)}) collective-permute-start(bf16[48,1024]{1,0:T(8,128)(2,1)S(1)} %join.3.refs_0_), channel_id=1, source_target_pairs={{0,24},{8,16},{16,8},{24,0},{1,25},{9,17},{17,9},{25,1},{2,26},{10... | collective-permute-start | bytes 294920 | tf_op jit(solution)/shard_map/ppermute | solution.py:849
  148.8 4.9 %collective-permute-start.28 = (f32[88,128]{1,0:T(8,128)S(1)}, f32[88,128]{1,0:T(8,128)S(1)}, u32[]{:S(2)}, u32[]{:S(2)}) collective-permute-start(f32[88,128]{1,0:T(8,128)S(1)} %get-tuple-element.183), channel_id=1, source_target_pairs={{0,6},{1,7},{2,4},{3,5},{4,2},{5,3},{6,0},{7,1},{8,14},{9,15},{10,... | collective-permute-start | bytes 135176 | tf_op jit(solution)/shard_map/ppermute | solution.py:849
  153.8 7.2 %collective-permute-start.31 = (f32[88,128]{1,0:T(8,128)S(1)}, f32[88,128]{1,0:T(8,128)S(1)}, u32[]{:S(2)}, u32[]{:S(2)}) collective-permute-start(f32[88,128]{1,0:T(8,128)S(1)} %total.1.refs_0_), channel_id=1, source_target_pairs={{0,24},{8,16},{16,8},{24,0},{1,25},{9,17},{17,9},{25,1},{2,26},{10... | collective-permute-start | bytes 135176 | tf_op jit(solution)/shard_map/ppermute | solution.py:849
  156.4 8.6 %collective-permute-start.30 = (f32[88,128]{1,0:T(8,128)S(1)}, f32[88,128]{1,0:T(8,128)S(1)}, u32[]{:S(2)}, u32[]{:S(2)}) collective-permute-start(f32[88,128]{1,0:T(8,128)S(1)} %total.1.refs_0_), channel_id=1, source_target_pairs={{0,16},{8,24},{16,0},{24,8},{1,17},{9,25},{17,1},{25,9},{2,18},{10... | collective-permute-start | bytes 135176 | tf_op jit(solution)/shard_map/ppermute | solution.py:849
  156.4 8.6 %collective-permute-start.29 = (f32[88,128]{1,0:T(8,128)S(1)}, f32[88,128]{1,0:T(8,128)S(1)}, u32[]{:S(2)}, u32[]{:S(2)}) collective-permute-start(f32[88,128]{1,0:T(8,128)S(1)} %total.1.refs_0_), channel_id=1, source_target_pairs={{0,8},{8,0},{16,24},{24,16},{1,9},{9,1},{17,25},{25,17},{2,10},{10... | collective-permute-start | bytes 135176 | tf_op jit(solution)/shard_map/ppermute | solution.py:849
  158.3 17.3 %collective-permute-start.41 = (bf16[16,3200]{1,0:T(8,128)(2,1)S(1)}, bf16[16,3200]{1,0:T(8,128)(2,1)S(1)}, u32[]{:S(2)}, u32[]{:S(2)}) collective-permute-start(bf16[16,3200]{1,0:T(8,128)(2,1)S(1)} %join.2.refs_0_), channel_id=1, source_target_pairs={{0,24},{8,16},{16,8},{24,0},{1,25},{9,17},{17,9},{25,1},{2,26},{10... | collective-permute-start | bytes 307208 | tf_op jit(solution)/shard_map/ppermute | solution.py:849
  160.9 14.6 %collective-permute-start.40 = (bf16[16,3200]{1,0:T(8,128)(2,1)S(1)}, bf16[16,3200]{1,0:T(8,128)(2,1)S(1)}, u32[]{:S(2)}, u32[]{:S(2)}) collective-permute-start(bf16[16,3200]{1,0:T(8,128)(2,1)S(1)} %join.2.refs_0_), channel_id=1, source_target_pairs={{0,16},{8,24},{16,0},{24,8},{1,17},{9,25},{17,1},{25,9},{2,18},{10... | collective-permute-start | bytes 307208 | tf_op jit(solution)/shard_map/ppermute | solution.py:849
  165.0 10.6 %collective-permute-start.39 = (bf16[16,3200]{1,0:T(8,128)(2,1)S(1)}, bf16[16,3200]{1,0:T(8,128)(2,1)S(1)}, u32[]{:S(2)}, u32[]{:S(2)}) collective-permute-start(bf16[16,3200]{1,0:T(8,128)(2,1)S(1)} %join.2.refs_0_), channel_id=1, source_target_pairs={{0,8},{8,0},{16,24},{24,16},{1,9},{9,1},{17,25},{25,17},{2,10},{10... | collective-permute-start | bytes 307208 | tf_op jit(solution)/shard_map/ppermute | solution.py:849
  165.0 9.2 %collective-permute-start.50 = (bf16[48,1024]{1,0:T(8,128)(2,1)S(1)}, bf16[48,1024]{1,0:T(8,128)(2,1)S(1)}, u32[]{:S(2)}, u32[]{:S(2)}) collective-permute-start(bf16[48,1024]{1,0:T(8,128)(2,1)S(1)} %join.3.refs_0_), channel_id=1, source_target_pairs={{0,16},{8,24},{16,0},{24,8},{1,17},{9,25},{17,1},{25,9},{2,18},{10... | collective-permute-start | bytes 294920 | tf_op jit(solution)/shard_map/ppermute | solution.py:849
  165.3 9.3 %collective-permute-start.49 = (bf16[48,1024]{1,0:T(8,128)(2,1)S(1)}, bf16[48,1024]{1,0:T(8,128)(2,1)S(1)}, u32[]{:S(2)}, u32[]{:S(2)}) collective-permute-start(bf16[48,1024]{1,0:T(8,128)(2,1)S(1)} %join.3.refs_0_), channel_id=1, source_target_pairs={{0,8},{8,0},{16,24},{24,16},{1,9},{9,1},{17,25},{25,17},{2,10},{10... | collective-permute-start | bytes 294920 | tf_op jit(solution)/shard_map/ppermute | solution.py:849
  (12 other events, 125.4 us)

commit v3 on v2

--- a/solution.py
+++ b/solution.py
@@ -127,19 +127,43 @@
     return slice(t * TILE, (t + 1) * TILE)
 
 
-def one_way(src_ref, lab_ref, ref_label, dk_ref, out_ref, dims, steps, width, reverse, unroll=8):
+def padded(steps):
+    return pltpu.VMEM((SUBS * (steps + 1), TILE), F32)
+
+
+def stage(src, dst, steps):
+    for c in range(SUBS):
+        dst[c * (steps + 1) : c * (steps + 1) + steps, :] = src[pl.ds(c * steps, steps), :]
+
+
+def unstage(src, dst, steps):
+    for c in range(SUBS):
+        dst[pl.ds(c * steps, steps), :] = src[c * (steps + 1) : c * (steps + 1) + steps, :]
+
+
+def rows_at(t, steps):
+    return pl.ds(t, SUBS, stride=steps + 1)
+
+
+def one_way(
+    src_ref, lab_ref, ref_label, dk_ref, out_ref, pads, dims, steps, width, reverse, unroll=8
+):
+    src_pad, lab_pad = pads
+    stage(lab_ref, lab_pad, steps)
     for lt in range(width // TILE):
         lanes = lanes_of(lt)
         decay = [jnp.broadcast_to(dk_ref[h : h + 1, lanes], (SUBS, TILE)) for h in range(dims)]
 
-        def step(i, state, lt=lt, decay=decay):
+        stage(src_ref.at[lt], src_pad, steps)
+
+        def step(i, state, decay=decay):
             state = list(state)
             for u in range(unroll):
                 t = i * unroll + u
                 if reverse:
                     t = steps - 1 - t
-                x = src_ref[lt, pl.ds(t, SUBS, stride=steps), :]
-                l = lab_ref[pl.ds(t, SUBS, stride=steps), :]
+                x = src_pad[rows_at(t, steps), :]
+                l = lab_pad[rows_at(t, steps), :]
                 x = jnp.where(l == ref_label, x, 0.0)
                 state = [decay[h] * state[h] + x for h in range(dims)]
             return tuple(state)
@@ -157,11 +181,11 @@
 def head_kernel(*refs, devices, dims, nv, nm):
     (
         tok_ref, seg_ref, pd_ref, pv_ref, pz_ref, pm_ref, dk_ref, nrm_ref, low_ref, lab_ref,
-        fin_ref, msg_ref, scr_ref, small_ref,
-    ) = refs[devices:]
+        fin_ref, msg_ref, scr_ref, small_ref, *pads
+    ) = refs[2:]
     me = lax.axis_index("seq")
     for k in range(devices):
-        small_ref[me ^ k] = refs[k][...]
+        small_ref[me ^ k] = refs[k % 2][k // 2]
     tokens, width = tok_ref.shape
     seqs, length = seg_ref.shape
     steps = tokens // SUBS
@@ -212,7 +236,7 @@
         lab_ref[s * length : (s + 1) * length, :] = dot(diagonal, jnp.ones((length, TILE), BF))
 
     first, last = chunk_labels(lab_ref, steps)
-    one_way(nrm_ref, lab_ref, last, dk_ref, fin_ref, dims, steps, width, False)
+    one_way(nrm_ref, lab_ref, last, dk_ref, fin_ref, pads, dims, steps, width, False)
     through = (first == last) & (first == pltpu.roll(last, 1, 0))
     for lt in range(width // TILE):
         lanes = lanes_of(lt)
@@ -255,8 +279,8 @@
     nrm_ref, lab_ref, dk_ref, pd_ref, fin_ref = refs[:5]
     msgs = refs[5 : 5 + reach]
     z_ref, mlow_ref, sp_ref = refs[5 + reach : 8 + reach]
-    ent_ref, lab_scr, ys_ref = refs[8 + reach : 11 + reach]
-    scr_refs = refs[11 + reach :]
+    ent_ref, lab_scr, ys_ref, x_pad, lab_pad, y_pad = refs[8 + reach : 14 + reach]
+    scr_refs = refs[14 + reach :]
     blocks, tokens, _ = nrm_ref.shape
     steps = tokens // SUBS
     half = SUBS // seqs
@@ -266,8 +290,10 @@
     inside = first == last
     joined = first == pltpu.roll(last, 1, 0)
     unroll = 4
+    stage(lab_ref, lab_pad, steps)
 
     def block(lt, _):
+        stage(nrm_ref.at[lt], x_pad, steps)
         lanes = pl.ds(pl.multiple_of(lt * TILE, TILE), TILE)
         power = dk_ref[2 * dims : 3 * dims, lanes]
         arrivals = entering(msgs, lanes, first, even, scr_refs, lab_scr, 0, dims, seqs, power)
@@ -288,8 +314,8 @@
             before, state = carry[0], list(carry[1:])
             for u in range(unroll):
                 t = i * unroll + u
-                x = nrm_ref[lt, pl.ds(t, SUBS, stride=steps), :]
-                l = lab_ref[pl.ds(t, SUBS, stride=steps), :]
+                x = x_pad[rows_at(t, steps), :]
+                l = lab_pad[rows_at(t, steps), :]
                 same = l == before
                 before = l
                 sums = [None] * 4
@@ -303,13 +329,14 @@
                     state[h] = decay[h] * kept + x
                     term = weight[h] * state[h]
                     sums[h % 4] = term if sums[h % 4] is None else sums[h % 4] + term
-                ys_ref[lt, pl.ds(t, SUBS, stride=steps), :] = (sums[0] + sums[1]) + (
+                y_pad[rows_at(t, steps), :] = (sums[0] + sums[1]) + (
                     sums[2] + sums[3]
                 )
             return (before,) + tuple(state)
 
         start = tuple(ent_ref[h * SUBS : (h + 1) * SUBS, :] for h in range(dims))
         lax.fori_loop(0, steps // unroll, step, (first,) + start)
+        unstage(y_pad, ys_ref.at[lt], steps)
         return 0
 
     lax.fori_loop(0, blocks, block, 0)
@@ -327,8 +354,9 @@
 def load_weights(pieces, dst, sem, rows, start, cols, place):
     me = lax.axis_index("seq")
     copies = []
-    for k, piece in enumerate(pieces):
+    for k in range(2 * pieces[0].shape[0]):
         p = me ^ k
+        piece = pieces[k % 2].at[k // 2]
         copies.append(
             pltpu.make_async_copy(
                 piece.at[pl.ds(start, rows), pl.ds(0, cols)],
@@ -346,10 +374,11 @@
 
 
 def front_kernel(*refs, devices):
-    pieces = refs[:devices]
-    nlow, mlow, pv, pm, pz, lab, seg = refs[devices : devices + 7]
-    vlow, dval, upd, ext, lat, rs, ad, glow, probs, qlow, klow = refs[devices + 7 : devices + 18]
-    w, res, sem = refs[devices + 18 :]
+    n = 2
+    pieces = refs[:n]
+    nlow, mlow, pv, pm, pz, lab, seg = refs[n : n + 7]
+    vlow, dval, upd, ext, lat, rs, ad, glow, probs, qlow, klow = refs[n + 7 : n + 18]
+    w, res, sem = refs[n + 18 :]
     tokens, width = nlow.shape
     nv = vlow.shape[1]
     zw = lat.shape[1]
@@ -458,10 +487,11 @@
 
 
 def middle_kernel(*refs, devices, depth, dims):
-    pieces = refs[:devices]
-    tok, cot, upd, ext, rs, ad, glow, pd, pv = refs[devices : devices + 9]
-    out, gin, attg, blu, blre, v512, v1024, own, sib = refs[devices + 9 : devices + 18]
-    w2, wup, proj, mid, slow, dup, hlow, clow, ulow, elow, gmid, grad, sem = refs[devices + 18 :]
+    n = 2
+    pieces = refs[:n]
+    tok, cot, upd, ext, rs, ad, glow, pd, pv = refs[n : n + 9]
+    out, gin, attg, blu, blre, v512, v1024, own, sib = refs[n + 9 : n + 18]
+    w2, wup, proj, mid, slow, dup, hlow, clow, ulow, elow, gmid, grad, sem = refs[n + 18 :]
     tokens, width = tok.shape
     nv = rs.shape[1]
     nf = dup.shape[1]
@@ -583,12 +613,13 @@
 
 
 def back_kernel(*refs, devices, dims):
-    pieces = refs[:devices]
+    n = 2
+    pieces = refs[:n]
     probs, attg, vlow, dval, qlow, klow, lat, blu, blre, z, nrm, pd, pz, dk, lab = refs[
-        devices : devices + 15
+        n : n + 15
     ]
-    vgl, bll, gs, gnp, w512, w1024, w128, msg, ach = refs[devices + 15 : devices + 24]
-    w, gq, gk, scr, sem = refs[devices + 24 :]
+    vgl, bll, gs, gnp, w512, w1024, w128, msg, ach = refs[n + 15 : n + 24]
+    w, gq, gk, scr, sem, *pads = refs[n + 24 :]
     tokens, width = z.shape
     nv = vlow.shape[1]
     zw = lat.shape[1]
@@ -661,7 +692,7 @@
 
     tiles(tokens, width, 512, 512, mixed_back)
     first, last = chunk_labels(lab, steps)
-    one_way(gs, lab, first, dk, ach, dims, steps, width, True)
+    one_way(gs, lab, first, dk, ach, pads, dims, steps, width, True)
     power = dk[2 * dims : 3 * dims, :]
     through = (first == last) & (last == pltpu.roll(first, SUBS - 1, 0))
     for lt in range(width // TILE):
@@ -720,7 +751,8 @@
     tok, gin, pd, v512, v1024, w512, w1024, w128 = refs[7 + reach : 15 + reach]
     tg, own, sib = refs[15 + reach : 18 + reach]
     ent, lab_scr, gnb, sd, sv, sm, sums_ref = refs[18 + reach : 25 + reach]
-    scr_refs = refs[25 + reach :]
+    lab_pad, x_pad, g_pad, n_pad = refs[25 + reach : 29 + reach]
+    scr_refs = refs[29 + reach :]
     blocks, tokens, _ = nrm.shape
     width = tok.shape[1]
     steps = tokens // SUBS
@@ -733,8 +765,12 @@
     unroll = 4
     group = 8
     zero = jnp.zeros((SUBS, TILE), F32)
+    stage(lab, lab_pad, steps)
 
     def block(lt, _):
+        stage(nrm.at[lt], x_pad, steps)
+        stage(gs.at[lt], g_pad, steps)
+        stage(gnp.at[lt], n_pad, steps)
         lanes = pl.ds(pl.multiple_of(lt * TILE, TILE), TILE)
         power = dk[2 * dims : 3 * dims, lanes]
         arrivals = entering(msgs, lanes, last, odd, scr_refs, lab_scr, half - 1, dims, seqs, power)
@@ -757,13 +793,13 @@
                 a, g0, g1 = (list(carry[1 + j * group : 1 + (j + 1) * group]) for j in range(3))
                 for u in range(unroll):
                     t = steps - 1 - (i * unroll + u)
-                    here = pl.ds(t, SUBS, stride=steps)
-                    x = nrm[lt, here, :]
-                    g = gs[lt, here, :]
-                    l = lab[here, :]
+                    here = rows_at(t, steps)
+                    x = x_pad[here, :]
+                    g = g_pad[here, :]
+                    l = lab_pad[here, :]
                     same = l == after
                     after = l
-                    sums = [gnp[lt, here, :] if base == 0 else gnb[lt, here, :], zero]
+                    sums = [n_pad[here, :], zero]
                     for j in range(group):
                         h = base + j
                         if j % 2 == 0:
@@ -772,7 +808,7 @@
                         g0[j] = g0[j] + a[j] * x
                         g1[j] = g1[j] + a[j] * pair[j % 2 * SUBS : (j % 2 + 1) * SUBS, :]
                         sums[j % 2] = sums[j % 2] + weight[j] * a[j]
-                    gnb[lt, here, :] = sums[0] + sums[1]
+                    n_pad[here, :] = sums[0] + sums[1]
                 return (after,) + tuple(a) + tuple(g0) + tuple(g1)
 
             start = tuple(ent[h * SUBS : (h + 1) * SUBS, :] for h in span)
@@ -783,6 +819,7 @@
                 sums_ref[dims + h : dims + h + 1, lanes] = jnp.sum(
                     done[1 + 2 * group + j], axis=0, keepdims=True
                 )
+        unstage(n_pad, gnb.at[lt], steps)
         return 0
 
     lax.fori_loop(0, blocks, block, 0)
@@ -864,71 +901,143 @@
     return [parts[0]] + [hop(part, "seq", 2 * k) for k, part in enumerate(parts) if k]
 
 
-def deal_kernel(*refs, count, depth):
+def split_kernel(own, got, kept, to_x, to_y, later_x, later_y):
+    h = own.shape[1] // 2
+    top, low = slice(0, h), slice(h, None)
+
+    def piece(k, part):
+        return own[k, part].astype(F32) + got[k, part].astype(F32)
+
+    kept[...] = own[0].astype(F32) + got[0].astype(F32)
+    to_x[top] = piece(1, top).astype(BF)
+    to_x[low] = piece(3, top).astype(BF)
+    to_y[top] = piece(2, low).astype(BF)
+    to_y[low] = piece(3, low).astype(BF)
+    later_x[...] = piece(1, low)
+    later_y[...] = piece(2, top)
+
+
+def split(own, sib):
+    got = hop(sib, "seq", 1)
+    shape = own.shape[1:]
+    half = (shape[0] // 2,) + shape[1:]
+    return whole(
+        split_kernel,
+        [struct(shape, F32), struct(shape, BF), struct(shape, BF), struct(half, F32), struct(half, F32)],
+        n_in=2,
+        name="split",
+    )(own, got)
+
+
+def turn_kernel(from_x, from_y, later_x, later_y, to_x, to_y):
+    h = later_x.shape[0]
+    to_x[...] = (later_x[...] + from_y[h:].astype(F32)).astype(BF)
+    to_y[...] = (later_y[...] + from_x[h:].astype(F32)).astype(BF)
+
+
+def spread_sums(own, sib, devices, tie):
+    if devices != 8:
+        parts = across(fold(own, sib, BF))
+        return parts[:1], parts[:1], lambda *first: parts
+    kept, to_x, to_y, later_x, later_y = split(own, sib)
+    from_x, from_y = hop(to_x, "seq", 2), hop(to_y, "seq", 4)
+
+    def finish(*first):
+        fx, fy = after((from_x, from_y), *first)
+        half = struct(later_x.shape, BF)
+        qx, qy = whole(turn_kernel, [half, half], n_in=4, name="turn")(fx, fy, later_x, later_y)
+        return [kept, fx, fy, hop(qx, "seq", 2), hop(qy, "seq", 4)]
+
+    return [kept], [from_x, from_y], finish
+
+
+def deal_kernel(*refs, count, depth, halves):
     ins, outs, scr = refs[:count], refs[count:-1], refs[-1]
     me = lax.axis_index("grp")
-    total = ins[0][...]
-    for other in ins[1:]:
-        total = total + other[...].astype(F32)
-    scr[...] = total
+    if halves:
+        kept, from_x, from_y, last_x, last_y = ins
+        h = depth // 2
+        scr[0:h] = kept[0:h] + from_x[0:h].astype(F32) + last_y[...].astype(F32)
+        scr[h:] = kept[h:] + from_y[0:h].astype(F32) + last_x[...].astype(F32)
+    else:
+        total = ins[0][...]
+        for other in ins[1:]:
+            total = total + other[...].astype(F32)
+        scr[...] = total
     for k in range(depth):
         outs[k][...] = scr[me ^ k].astype(outs[k].dtype)
 
 
-def deal(parts, depth):
+def deal(parts, depth, devices):
     shape = parts[0].shape
     outs = [struct(shape[1:], F32)] + [struct(shape[1:], BF)] * (depth - 1)
-    body = partial(deal_kernel, count=len(parts), depth=depth)
+    body = partial(deal_kernel, count=len(parts), depth=depth, halves=devices == 8)
     mine = whole(body, outs, [pltpu.VMEM(shape, F32)], n_in=len(parts), name="deal")(*parts)
     return [mine[0]] + [hop(part, "grp", k) for k, part in enumerate(mine) if k]
 
 
-def join_kernel(*refs):
-    total = refs[0][...]
-    for other in refs[1:-1]:
-        total = total + other[...].astype(F32)
-    refs[-1][...] = total.astype(BF)
-
-
-def join(parts):
-    depth = len(parts)
-    mine = whole(join_kernel, struct(parts[0].shape, BF), n_in=depth, name="join")(*parts)
+def join_kernel(*refs, depth, half):
+    part_a, part_b = refs[:depth], refs[depth : 2 * depth]
+    part_c, out, c_scr = refs[2 * depth : 2 * depth + half], refs[-2], refs[-1]
+    a, b = part_a[0][...], part_b[0][...]
+    for k in range(1, depth):
+        a, b = a + part_a[k][...].astype(F32), b + part_b[k][...].astype(F32)
+    c = part_c[0][...]
+    for other in part_c[1:]:
+        c = c + other[...]
+    rows, lanes = out.shape[0], a.shape[1]
+    for j in range(a.shape[0] // rows):
+        out[:, j * lanes : (j + 1) * lanes] = a[j * rows : (j + 1) * rows, :].astype(BF)
+    at = a.shape[0] // rows * lanes
+    out[:, at : at + b.shape[1]] = b.astype(BF)
+    at += b.shape[1]
+    c_scr[...] = jnp.zeros_like(c_scr)
+    c_scr[0 : c.shape[0], :] = c
+    for j in range(c_scr.shape[0] // rows):
+        out[:, at + j * TILE : at + (j + 1) * TILE] = c_scr[j * rows : (j + 1) * rows, :].astype(BF)
+
+
+def join(sum_a, sum_b, parts_c):
+    depth, rows = len(sum_a), sum_b[0].shape[0]
+    blocks_c = ceil_div(ROWS_SMALL, rows)
+    wide = sum_a[0].shape[0] // rows * sum_a[0].shape[1] + sum_b[0].shape[1] + blocks_c * TILE
+    mine = whole(
+        partial(join_kernel, depth=depth, half=len(parts_c)), struct((rows, wide), BF),
+        [pltpu.VMEM((blocks_c * rows, TILE), F32)],
+        n_in=2 * depth + len(parts_c), name="join",
+    )(*sum_a, *sum_b, *parts_c)
     return [mine] + [hop(mine, "grp", k) for k in range(1, depth)]
 
 
-def spread_a_kernel(*refs, depth, r2, width):
-    ins, (attend, down, up, scr) = refs[:depth], refs[depth:]
-    me = lax.axis_index("grp")
-    for k in range(depth):
-        scr[me ^ k] = ins[k][...].astype(F32)
-    r1 = up.shape[0] // depth
-    for z in range(depth):
-        attend[z * r2 : (z + 1) * r2, :] = scr[z, 0:r2, 0:width]
-        down[z * r2 : (z + 1) * r2, :] = scr[z, 0:r2, width:]
-        up[z * r1 : (z + 1) * r1, :] = scr[z, r2:, :]
-
-
-def spread_b_kernel(*refs, depth):
-    ins, (value, mix, scr) = refs[:depth], refs[depth:]
-    me = lax.axis_index("grp")
-    for k in range(depth):
-        scr[me ^ k] = ins[k][...].astype(F32)
-    r = value.shape[0] // depth
-    nv = value.shape[1]
-    for z in range(depth):
-        value[z * r : (z + 1) * r, :] = scr[z, :, 0:nv]
-        mix[z * r : (z + 1) * r, :] = scr[z, :, nv:]
-
-
 def final_kernel(*refs, depth, plan, held, dims):
-    ins, decs = refs[:depth], refs[depth : depth + 4]
-    vectors, scr = refs[depth + 4 : -1], refs[-1]
+    ins, (attend, down, up, value, mix) = refs[:depth], refs[depth : depth + 5]
+    decs, vectors = refs[depth + 5 : depth + 9], refs[depth + 9 : -2]
+    scr, c_scr = refs[-2:]
     grp, me = lax.axis_index("grp"), lax.axis_index("seq")
     for k in range(depth):
-        scr[grp ^ k] = ins[k][...]
-    total = scr[0]
-    for z in range(1, depth):
-        total = total + scr[z]
+        scr[grp ^ k] = ins[k][...].astype(F32)
+    rows, width = scr.shape[1], attend.shape[1]
+    wide, nv = 2 * width, value.shape[1]
+    folds = attend.shape[0] // depth // rows
+    for z in range(depth):
+        for j in range(folds):
+            at = (z * folds + j) * rows
+            attend[at : at + rows, :] = scr[z, :, j * wide : j * wide + width]
+            down[at : at + rows, :] = scr[z, :, j * wide + width : (j + 1) * wide]
+        at = folds * wide
+        here = slice(z * rows, (z + 1) * rows)
+        up[here, :] = scr[z, :, at : at + wide]
+        at += wide
+        value[here, :] = scr[z, :, at : at + nv]
+        mix[here, :] = scr[z, :, at + nv : at + nv + mix.shape[1]]
+    at = (folds + 1) * wide + nv + mix.shape[1]
+    for j in range(c_scr.shape[0] // rows):
+        cols = slice(at + j * TILE, at + (j + 1) * TILE)
+        block = scr[0, :, cols]
+        for z in range(1, depth):
+            block = block + scr[z, :, cols]
+        c_scr[j * rows : (j + 1) * rows, :] = block
+    total = c_scr[...]
     pick = pick_lanes(me, held, TILE)
     for j, dec in enumerate(decs):
         dec[...] = lax.dot_general(
@@ -948,28 +1057,54 @@
                 out[i : i + 1, :] = moved[0:1, 0:n]
 
 
-def total_kernel(*refs):
-    total = refs[0][...]
-    for other in refs[1:-1]:
-        total = total + other[...]
-    refs[-1][...] = total
-
-
 def near_pieces(x, devices):
     return [x] + [hop(x, "seq", 2 * k) for k in range(1, devices // 2)]
 
 
-def far_pieces(near):
-    return [hop(part, "seq", 1) for part in near]
-
-
-def woven(near, far):
-    return [part for pair in zip(near, far) for part in pair]
-
-
-def gather_pieces(x, devices):
-    near = near_pieces(x, devices)
-    return woven(near, far_pieces(near))
+def bundle_kernel(*refs, halves):
+    ins, out = refs[:-1], refs[-1]
+    for k, ref in enumerate(ins[: out.shape[0] - halves]):
+        out[k] = ref[...]
+    if halves:
+        rows = out.shape[1] // 2
+        out[out.shape[0] - 1, 0:rows, :] = ins[-2][...]
+        out[out.shape[0] - 1, rows:, :] = ins[-1][...]
+
+
+def bundle(parts, halves=0):
+    shape = (len(parts) - halves,) + parts[0].shape
+    return whole(
+        partial(bundle_kernel, halves=halves), struct(shape, parts[0].dtype), n_in=len(parts),
+        name="bundle",
+    )(*parts)
+
+
+def with_far(both):
+    return [both, hop(both, "seq", 1)]
+
+
+def relay_kernel(x, y, top, bottom):
+    rows = top.shape[0]
+    top[...] = x[0:rows, :]
+    bottom[...] = y[rows:, :]
+
+
+def relay(x, y):
+    half = struct((x.shape[0] // 2, x.shape[1]), x.dtype)
+    top, bottom = whole(relay_kernel, [half, half], n_in=2, name="relay")(x, y)
+    return [hop(top, "seq", 4), hop(bottom, "seq", 2)]
+
+
+def first_pieces(x, devices):
+    near = 3 if devices == 8 else devices // 2
+    return [x] + [hop(x, "seq", 2 * k) for k in range(1, near)]
+
+
+def more_pieces(parts, devices, *first):
+    if devices != 8:
+        return parts
+    x, y = after(parts[1:3], *first)
+    return parts + relay(x, y)
 
 
 def after(x, *first):
@@ -1008,7 +1143,8 @@
         partial(place_kernel, plan=plan), struct((ROWS_SMALL, TILE), F32),
         n_in=4 + len(vectors), name="place", vmem=60,
     )(*decs, *[v for _, v in vectors])
-    small = gather_pieces(placed, devices)
+    near = near_pieces(placed, devices)
+    small = with_far(bundle(near))
 
     w1, w2 = whole(
         pack_kernel,
@@ -1017,9 +1153,9 @@
         name="pack",
         vmem=60,
     )(*lax.optimization_barrier(
-        (value_weight, mix_weight, attend_weight, down_weight, up_weight, small)
+        (value_weight, mix_weight, attend_weight, down_weight, up_weight, placed)
     )[:5])
-    w1 = near_pieces(w1, devices)
+    w1 = first_pieces(after(w1, near[1:]), devices)
 
     tok = tokens.reshape(count, width)
     cot = cotangent.reshape(count, width)
@@ -1033,18 +1169,23 @@
             struct((count, width), BF), struct((count, TILE), F32),
             struct((dims * SUBS, width), F32), struct((msg_rows, width), BF),
         ],
-        [pltpu.VMEM((dims * SUBS, TILE), F32), pltpu.VMEM((devices, ROWS_SMALL, TILE), F32)],
-        n_in=devices + 2,
+        [pltpu.VMEM((dims * SUBS, TILE), F32), pltpu.VMEM((devices, ROWS_SMALL, TILE), F32)]
+        + [padded(steps)] * 2,
+        n_in=4,
         name="head",
         micros=6,
     )(*small, tok, segments)
 
-    w2 = near_pieces(after(w2, msg), devices)
     onward = [
         lax.ppermute(msg, "seq", [(i, i + k) for i in range(devices - k)])
         for k in range(1, reach + 1)
     ]
 
+    halves = 1 if devices == 8 else 0
+    w1 = more_pieces(w1, devices, msg)
+    w1 = with_far(bundle(after(w1, onward), halves))
+    w2 = first_pieces(after(w2, w1[0]), devices)
+    nrm = after(nrm, w1[0])
     arrivals = [pltpu.VMEM((dims * SUBS, TILE), F32)] * reach
     z, mlow, sp = whole(
         partial(scan_kernel, reach=reach, dims=dims, seqs=seqs),
@@ -1055,14 +1196,13 @@
         [
             pltpu.VMEM((dims * SUBS, TILE), F32), pltpu.VMEM((SUBS, TILE), F32),
             pltpu.VMEM((blocks, count, TILE), F32),
-        ] + arrivals,
+        ] + [padded(steps)] * 3 + arrivals,
         n_in=5 + reach,
         name="scan",
         micros=8,
     )(nrm, lab, dk, pd, fin, *onward)
 
-    early, late = w1[:-1], w1[-1:]
-    w1 = woven(w1, far_pieces(after(early, onward)) + far_pieces(after(late, z)))
+    w2 = more_pieces(w2, devices, z)
 
     def sems(n):
         return pltpu.SemaphoreType.DMA((n, devices))
@@ -1076,12 +1216,12 @@
             struct((count, zw), BF), struct((count, zw), BF),
         ],
         [pltpu.VMEM((width, nv + nm), BF), pltpu.VMEM((count, nv), F32), sems(1)],
-        in_specs=[HB] * devices + [VM] * 7,
+        in_specs=[HB] * 2 + [VM] * 7,
         name="front",
         micros=11,
     )(*w1, nlow, mlow, pv, pm, pz, lab, segments)
 
-    w2 = woven(w2, far_pieces(after(w2, glow)))
+    w2 = with_far(bundle(after(w2, glow), halves))
     half = devices // 2
     rows2, rows1 = nv // devices // depth, held // depth
     piece_a = struct((half, depth, rows2 + rows1, 2 * width), BF)
@@ -1100,7 +1240,7 @@
             pltpu.VMEM((count, nf), BF), pltpu.VMEM((count, width), BF),
             pltpu.VMEM((count, width), F32), pltpu.VMEM((nv, 2 * width), BF), sems(2),
         ],
-        in_specs=[HB] * devices + [VM] * 9,
+        in_specs=[HB] * 2 + [VM] * 9,
         name="middle",
         micros=19,
     )(*w2, tok, cot, upd, ext, rs, ad, glow, pd, pv)
@@ -1116,8 +1256,9 @@
         [
             pltpu.VMEM((width, nv + nm), BF), pltpu.VMEM((count, zw), F32),
             pltpu.VMEM((count, zw), F32), pltpu.VMEM((dims * SUBS, TILE), F32), sems(1),
+            padded(steps), padded(steps),
         ],
-        in_specs=[HB] * devices + [VM] * 15,
+        in_specs=[HB] * 2 + [VM] * 15,
         name="back",
         micros=15,
     )(*w1, probs, attg, vlow, dval, qlow, klow, lat, blu, blre, z, nrm, pd, pz, dk, lab)
@@ -1137,6 +1278,9 @@
         micros=6,
     )(nlow, mlow, vgl, blu, bll, blre)
 
+    _, _, finish_a = spread_sums(after(own_a, backward), sib_a, devices, None)
+    tie_b, _, finish_b = spread_sums(own_b, sib_b, devices, None)
+    nrm = after(nrm, tie_b)
     piece_c = struct((half, ROWS_SMALL, TILE), F32)
     wide = ceil_div(nm, TILE) + 2
     tokens_grad, own_c, sib_c = whole(
@@ -1147,41 +1291,32 @@
             pltpu.VMEM((blocks, count, TILE), F32), pltpu.VMEM((72, width), F32),
             pltpu.VMEM((8, nv), F32), pltpu.VMEM((8, wide * TILE), F32),
             pltpu.VMEM((2 * dims, width), F32),
-        ] + arrivals,
+        ] + [padded(steps)] * 4 + arrivals,
         n_in=15 + reach,
         name="last",
         micros=12,
     )(sp, nrm, gs, gnp, lab, dk, ach, *backward, tok, gin, pd, v512, v1024, w512, w1024, w128)
 
-    sum_a = join(deal(across(fold(own_a, sib_a, BF)), depth))
-    attend_grad, down_grad, up_grad = whole(
-        partial(spread_a_kernel, depth=depth, r2=rows2, width=width),
+    sum_a = deal(finish_a(own_c), depth, devices)
+    sum_b = deal(finish_b(own_c), depth, devices)
+    parts_c = across(fold(own_c, sib_c, F32))
+    everything = join(sum_a, sum_b, parts_c)
+    grads = whole(
+        partial(final_kernel, depth=depth, plan=plan, held=held, dims=dims),
         [
             struct((nv // devices, width), F32), struct((nf // devices, width), F32),
-            struct((held, nf), F32),
+            struct((held, nf), F32), struct((held, nv), F32), struct((held, nm), F32),
+        ] + [struct((dims, held), F32)] * 4 + [struct(v.shape, F32) for _, v in vectors],
+        [
+            pltpu.VMEM((depth,) + everything[0].shape, F32),
+            pltpu.VMEM((ceil_div(ROWS_SMALL, rows1) * rows1, TILE), F32),
         ],
-        [pltpu.VMEM((depth,) + piece_a.shape[2:], F32)],
-        n_in=depth,
-        name="spread_a",
-    )(*sum_a)
-    sum_b = join(deal(across(fold(own_b, sib_b, BF)), depth))
-    value_grad, mix_grad = whole(
-        partial(spread_b_kernel, depth=depth),
-        [struct((held, nv), F32), struct((held, nm), F32)],
-        [pltpu.VMEM((depth,) + piece_b.shape[2:], F32)],
-        n_in=depth,
-        name="spread_b",
-    )(*sum_b)
-    parts_c = across(fold(own_c, sib_c, F32))
-    shard_c = whole(total_kernel, struct(piece_c.shape[1:], F32), n_in=half, name="total")(*parts_c)
-    all_c = [shard_c] + [hop(shard_c, "grp", k) for k in range(1, depth)]
-    alpha_g, delta_g, beta_g, eta_g, value_b, up_b, mix_b, first_g, omega, second_g, down_b, gains_g, qoff, posb = whole(
-        partial(final_kernel, depth=depth, plan=plan, held=held, dims=dims),
-        [struct((dims, held), F32)] * 4 + [struct(v.shape, F32) for _, v in vectors],
-        [pltpu.VMEM((depth,) + piece_c.shape[1:], F32)],
         n_in=depth,
         name="final",
-    )(*all_c)
+    )(*everything)
+    attend_grad, down_grad, up_grad, value_grad, mix_grad = grads[:5]
+    alpha_g, delta_g, beta_g, eta_g = grads[5:9]
+    value_b, up_b, mix_b, first_g, omega, second_g, down_b, gains_g, qoff, posb = grads[9:]
     return (
         out.reshape(tokens.shape),
         tokens_grad.reshape(tokens.shape),

time: 177 us -> 168 us (0.949)
  Pallas kernels: 67.1 us -> 56.9 us
  waiting for transfers between devices: 47.8 us -> 55.6 us
  starting transfers between devices: 58.3 us -> 51.7 us
    ppermute x48 -> x37, waiting for transfers between devices: 40.6 us -> 50.9 us  [hop(): return lax.ppermute(x, axis, [(i, i ^ k) for i in range(length)])]
    ppermute x48 -> x37, starting transfers between devices: 51 us -> 44.5 us  [hop(): return lax.ppermute(x, axis, [(i, i ^ k) for i in range(length)])]
    pallas_call x1, Pallas kernels: 16 us -> 9.81 us  [per_device(): whole(partial(last_kernel, reach=reach, devices=devices, dims=dims, seqs=...]
    ppermute x2, waiting for transfers between devices: 6.3 us -> 3.81 us  [per_device(): lax.ppermute(back_msg, 'seq', [(i + k, i) for i in range(devices - k)])]
  transfers between devices with their start and end apart: 52 -> 41, of which waited for: 23 -> 18; matrix products, arithmetic and copies ran while one was open for 0% -> 0% of each run, Pallas kernels for 28% -> 16%
where the time goes in v3:
time: 168 us
  Pallas kernels  56.9 us (34%)
  waiting for transfers between devices  55.6 us (33%)
  starting transfers between devices  51.7 us (31%)
  local copies, waits for them, and re-layouts  2.54 us (2%)
    ppermute x37, waiting for transfers between devices, hop(): return lax.ppermute(x, axis, [(i, i ^ k) for i in range(length)])  50.9 us
    ppermute x37, starting transfers between devices, hop(): return lax.ppermute(x, axis, [(i, i ^ k) for i in range(length)])  44.5 us
    pallas_call x1, Pallas kernels, per_device(): whole(partial(middle_kernel, devices=devices, depth=depth, dims=dims), [s...  13.3 us
    pallas_call x1, Pallas kernels, per_device(): whole(partial(back_kernel, devices=devices, dims=dims), [struct((count, n...  11.2 us
    pallas_call x1, Pallas kernels, per_device(): whole(partial(last_kernel, reach=reach, devices=devices, dims=dims, seqs=...  9.81 us
    pallas_call x1, Pallas kernels, per_device(): whole(partial(front_kernel, devices=devices), [struct((count, nv), BF), s...  6.76 us
    ppermute x2, starting transfers between devices, per_device(): lax.ppermute(msg, 'seq', [(i, i + k) for i in range(devices - k)])  4.61 us
    pallas_call x1, Pallas kernels, per_device(): whole(partial(scan_kernel, reach=reach, dims=dims, seqs=seqs), [struct((c...  4.16 us
  transfers between devices with their start and end apart: 41, of which 18 were waited for; matrix products, arithmetic and copies ran while one was open for 0% of the time, Pallas kernels for 16%

profile of v3, /device:TPU:0, one launch (start us, length us, event | category | flops | bytes accessed | tf_op | source)
XLA Modules:
  0.0 167.8 jit_solution(11204803537852586001)
XLA Ops:
  0.7 1.7 place.1.refs_0_
  2.3 3.9 %collective-permute-start.2 = (f32[88,128]{1,0:T(8,128)}, f32[88,128]{1,0:T(8,128)S(1)}, u32[]{:S(2)}, u32[]{:S(2)}) collective-permute-start(f32[88,128]{1,0:T(8,128)} %place.1.refs_0_), channel_id=1, source_target_pairs={{0,6},{1,7},{2,4},{3,5},{4,2},{5,3},{6,0},{7,1},{8,14},{9,15},{10,... | collective-permute-start | bytes 135176 | tf_op jit(solution)/shard_map/ppermute | solution.py:886
  6.8 2.1 %pack.1 = (bf16[64,3200]{1,0:T(8,128)(2,1)}, bf16[192,1024]{1,0:T(8,128)(2,1)}) custom-call(bf16[64,1024]{1,0:T(8,128)(2,1)} %value, bf16[64,2176]{1,0:T(8,128)(2,1)} %mix, bf16[128,512]{1,0:T(8,128)(2,1)} %attend, bf16[128,512]{1,0:T(8,128)(2,1)} %down, bf16[64,1024]{1,0:T(8,128)(2,1)} %up), custom_call_target="tpu_custom_call" | custom-call | bytes 7380000 | tf_op jit(solution)/shard_map/pack/pallas_call | solution.py:1149
  8.9 1.6 collective-permute-done.1.refs_2_
  11.0 1.5 collective-permute-start.4
  13.9 1.4 collective-permute-done.5.refs_1_
  15.3 1.0 copy-done
  17.1 2.5 %head.1 = (f32[72,512]{1,0:T(8,128)S(1)}, f32[8,1024]{1,0:T(8,128)S(1)}, f32[8,128]{1,0:T(8,128)S(1)}, f32[8,2176]{1,0:T(8,128)S(1)}, f32[48,512]{1,0:T(8,128)S(...) custom-call(f32[4,88,128]{2,1,0:T(8,128)S(1)} %bundle.3.refs_0_, ...), custom_call_target="tpu_custom_call" | custom-call | bytes 22140000 | tf_op jit(solution)/shard_map/head/pallas_call | solution.py:1164
  19.6 1.3 collective-permute-done.4.y.refs_2_
  20.9 1.4 collective-permute-done.3.x.refs_1_
  23.3 3.3 %collective-permute-start.9 = (bf16[80,512]{1,0:T(8,128)(2,1)S(1)}, bf16[80,512]{1,0:T(8,128)(2,1)S(1)}, u32[]{:S(2)}, u32[]{:S(2)}) collective-permute-start(bf16[80,512]{1,0:T(8,128)(2,1)S(1)} %get-tuple-element.155), channel_id=1, source_target_pairs={{0,2},{1,3},{2,4},{3,5},{4,6},{5,7},{8,10},{9,11},{10,12},{11,13},... | collective-permute-start | bytes 245768 | tf_op jit(solution)/shard_map/ppermute | solution.py:1180
  26.7 1.3 collective-permute-start.8
  29.5 2.6 %collective-permute-start.14 = (bf16[4,64,3200]{2,1,0:T(8,128)(2,1)S(1)}, bf16[4,64,3200]{2,1,0:T(8,128)(2,1)S(1)}, u32[]{:S(2)}, u32[]{:S(2)}) collective-permute-start(bf16[4,64,3200]{2,1,0:T(8,128)(2,1)S(1)} %bundle.4.refs_0_), channel_id=1, source_target_pairs={{0,1},{1,0},{2,3},{3,2},{4,5},{5,4},{6,7},{7,6},{8,9},{9,8},{10,11... | collective-permute-start | bytes 4915208 | tf_op jit(solution)/shard_map/ppermute | solution.py:886
  32.1 3.2 %collective-permute-start.11 = (bf16[192,1024]{1,0:T(8,128)(2,1)S(1)}, bf16[192,1024]{1,0:T(8,128)(2,1)S(1)}, u32[]{:S(2)}, u32[]{:S(2)}) collective-permute-start(bf16[192,1024]{1,0:T(8,128)(2,1)S(1)} %copy-done.4), channel_id=1, source_target_pairs={{0,4},{1,5},{2,6},{3,7},{4,0},{5,1},{6,2},{7,3},{8,12},{9,13},{10,... | collective-permute-start | bytes 1179656 | tf_op jit(solution)/shard_map/ppermute | solution.py:886
  35.2 4.2 %scan.1 = (f32[512,512]{1,0:T(8,128)S(1)}, bf16[512,512]{1,0:T(8,128)(2,1)S(1)}, bf16[4,64,128,128]{3,2,1,0:T(8,128)(2,1)S(1)}) custom-call(f32[4,512,128]{2,1,0:T(8,128)S(1)} %get-tuple-element.208.refs_0_.refs_12_.refs_1_, f32[512,128]{1,0:T(8,128)S(1)} %get-tuple-element.168.refs_1_.refs_7_.refs_16_.refs_4_, ...), custom_call_target="tpu_custom_call" | custom-call | bytes 29520000 | tf_op jit(solution)/shard_map/scan/pallas_call | solution.py:1190
  39.4 5.5 %collective-permute-done.11.y.refs_2_ = bf16[192,1024]{1,0:T(8,128)(2,1)S(1)} collective-permute-done((bf16[192,1024]{1,0:T(8,128)(2,1)S(1)}, bf16[192,1024]{1,0:T(8,128)(2,1)S(1)}, u32[]{:S(2)}, u32[]{:S(2)}) %collective-permute-start.11) | collective-permute-done | bytes 393248 | tf_op jit(solution)/shard_map/ppermute | solution.py:886
  44.9 1.5 collective-permute-done.10.x.refs_1_
  46.8 0.9 collective-permute-start.13
  47.7 6.8 %front.1 = (bf16[512,1024]{1,0:T(8,128)(2,1)S(1)}, bf16[512,1024]{1,0:T(8,128)(2,1)S(1)}, f32[512,512]{1,0:T(8,128)S(1)}, f32[512,512]{1,0:T(8,128)S(1)}, f32[51...) custom-call(bf16[4,64,3200]{2,1,0:T(8,128)(2,1)S(1)} %bundle.4.refs_, ...), custom_call_target="tpu_custom_call" | custom-call | bytes 40590000 | tf_op jit(solution)/shard_map/front/pallas_call | solution.py:1210
  54.7 3.4 %collective-permute-done.15.refs_1_ = bf16[4,192,1024]{2,1,0:T(8,128)(2,1)S(1)} collective-permute-done((bf16[4,192,1024]{2,1,0:T(8,128)(2,1)S(1)}, bf16[4,192,1024]{2,1,0:T(8,128)(2,1)S(1)}, u32[]{:S(2)}, u32[]{:S(2)}) %collective-permute-start.15) | collective-permute-done | bytes 1572896 | tf_op jit(solution)/shard_map/ppermute | solution.py:886
  58.1 13.3 %middle.1 = (f32[512,512]{1,0:T(8,128)}, f32[512,512]{1,0:T(8,128)S(1)}, bf16[512,1024]{1,0:T(8,128)(2,1)S(1)}, bf16[512,512]{1,0:T(8,128)(2,1)S(1)}, bf16[512,1...) custom-call(bf16[4,192,1024]{2,1,0:T(8,128)(2,1)S(1)} %bundle.5.refs, ...), custom_call_target="tpu_custom_call" | custom-call | bytes 70110000 | tf_op jit(solution)/shard_map/middle/pallas_call | solution.py:1228
  71.4 11.2 %back.1 = (bf16[512,1024]{1,0:T(8,128)(2,1)S(1)}, bf16[512,128]{1,0:T(8,128)(2,1)S(1)}, f32[4,512,128]{2,1,0:T(8,128)S(1)}, f32[4,512,128]{2,1,0:T(8,128)S(1)}, ...) custom-call(bf16[4,64,3200]{2,1,0:T(8,128)(2,1)S(1)} %bundle.4.refs_, ...), custom_call_target="tpu_custom_call" | custom-call | bytes 55350000 | tf_op jit(solution)/shard_map/back/pallas_call | solution.py:1248
  82.6 2.3 %weights.1 = (bf16[4,4,16,3200]{3,2,1,0:T(8,128)(2,1)S(1)}, bf16[4,4,16,3200]{3,2,1,0:T(8,128)(2,1)S(1)}) custom-call(bf16[512,512]{1,0:T(8,128)(2,1)S(1)} %get-tuple-element.177.refs_2_.nlow, bf16[512,512]{1,0:T(8,128)(2,1)S(1)} %get-tuple-element.178.refs_3_.mlow, bf16[512,1024]{1,0:T(8,128)(2,1)S(1)} %get-tuple-element.203.vgl, ...), custom_call_target="tpu_custom_call" | custom-call | bytes 22140000 | tf_op jit(solution)/shard_map/weights/pallas_call | solution.py:1272
  85.5 1.3 collective-permute-start.18
  86.8 1.3 collective-permute-start.17
  88.1 3.8 %collective-permute-done.18.refs_8_ = bf16[80,512]{1,0:T(8,128)(2,1)S(1)} collective-permute-done((bf16[80,512]{1,0:T(8,128)(2,1)S(1)}, bf16[80,512]{1,0:T(8,128)(2,1)S(1)}, u32[]{:S(2)}, u32[]{:S(2)}) %collective-permute-start.18) | collective-permute-done | bytes 81952 | tf_op jit(solution)/shard_map/ppermute | solution.py:1267
  92.2 2.1 %collective-permute-start.20 = (bf16[4,48,1024]{2,1,0:T(8,128)(2,1)S(1)}, bf16[4,48,1024]{2,1,0:T(8,128)(2,1)S(1)}, u32[]{:S(2)}, u32[]{:S(2)}) collective-permute-start(bf16[4,48,1024]{2,1,0:T(8,128)(2,1)S(1)} %get-tuple-element.224), channel_id=1, source_target_pairs={{0,2},{1,3},{2,0},{3,1},{4,6},{5,7},{6,4},{7,5},{8,10},{9,11},{10,... | collective-permute-start | bytes 1179656 | tf_op jit(solution)/shard_map/ppermute | solution.py:886
  94.3 1.5 collective-permute-start.21
  96.2 1.0 collective-permute-start.27
  97.2 9.8 %last.1 = (f32[512,512]{1,0:T(8,128)}, f32[4,88,128]{2,1,0:T(8,128)S(1)}, f32[4,88,128]{2,1,0:T(8,128)S(1)}) custom-call(bf16[4,64,128,128]{3,2,1,0:T(8,128)(2,1)S(1)} %get-tuple-element.193.refs_0_, f32[4,512,128]{2,1,0:T(8,128)S(1)} %get-tuple-element.208.refs_0_.refs_12_.refs_1_, f32[4,512,128]{2,1,0:T(8,128)S(1)} %get-tuple-element.209.refs_2_, ...), custom_call_target="tpu_custom_call" | custom-call | bytes 44280000 | tf_op jit(solution)/shard_map/last/pallas_call | solution.py:1286
  107.0 1.6 collective-permute-start.22
  108.7 1.5 collective-permute-start.23
  110.2 1.4 collective-permute-done.27.from_x.refs_1_
  111.6 2.6 %collective-permute-done.28.from_y.refs_2_ = bf16[4,16,3200]{2,1,0:T(8,128)(2,1)S(1)} collective-permute-done((bf16[4,16,3200]{2,1,0:T(8,128)(2,1)S(1)}, bf16[4,16,3200]{2,1,0:T(8,128)(2,1)S(1)}, u32[]{:S(2)}, u32[]{:S(2)}) %collective-permute-start.28) | collective-permute-done | bytes 409632 | tf_op jit(solution)/shard_map/ppermute | solution.py:886
  115.1 1.0 collective-permute-start.34
  116.2 1.5 collective-permute-start.30
  118.6 1.7 collective-permute-start.24
  121.1 2.5 %collective-permute-start.36 = (f32[88,128]{1,0:T(8,128)S(1)}, f32[88,128]{1,0:T(8,128)S(1)}, u32[]{:S(2)}, u32[]{:S(2)}) collective-permute-start(f32[88,128]{1,0:T(8,128)S(1)} %get-tuple-element.252), channel_id=1, source_target_pairs={{0,4},{1,5},{2,6},{3,7},{4,0},{5,1},{6,2},{7,3},{8,12},{9,13},{10,... | collective-permute-start | bytes 135176 | tf_op jit(solution)/shard_map/ppermute | solution.py:886
  124.4 1.7 collective-permute-start.31
  126.1 2.6 %collective-permute-start.32 = (bf16[16,3200]{1,0:T(8,128)(2,1)S(1)}, bf16[16,3200]{1,0:T(8,128)(2,1)S(1)}, u32[]{:S(2)}, u32[]{:S(2)}) collective-permute-start(bf16[16,3200]{1,0:T(8,128)(2,1)S(1)} %get-tuple-element.247), channel_id=1, source_target_pairs={{0,16},{8,24},{16,0},{24,8},{1,17},{9,25},{17,1},{25,9},{2,18},{10... | collective-permute-start | bytes 307208 | tf_op jit(solution)/shard_map/ppermute | solution.py:886
  128.9 2.3 %collective-permute-start.25 = (bf16[48,1024]{1,0:T(8,128)(2,1)S(1)}, bf16[48,1024]{1,0:T(8,128)(2,1)S(1)}, u32[]{:S(2)}, u32[]{:S(2)}) collective-permute-start(bf16[48,1024]{1,0:T(8,128)(2,1)S(1)} %get-tuple-element.235), channel_id=1, source_target_pairs={{0,16},{8,24},{16,0},{24,8},{1,17},{9,25},{17,1},{25,9},{2,18},{10... | collective-permute-start | bytes 294920 | tf_op jit(solution)/shard_map/ppermute | solution.py:886
  131.2 1.3 collective-permute-start.26
  132.5 12.2 %collective-permute-done.25.refs_2_ = bf16[48,1024]{1,0:T(8,128)(2,1)S(1)} collective-permute-done((bf16[48,1024]{1,0:T(8,128)(2,1)S(1)}, bf16[48,1024]{1,0:T(8,128)(2,1)S(1)}, u32[]{:S(2)}, u32[]{:S(2)}) %collective-permute-start.25) | collective-permute-done | bytes 98336 | tf_op jit(solution)/shard_map/ppermute | solution.py:886
  144.9 2.7 %collective-permute-start.40 = (bf16[16,7040]{1,0:T(8,128)(2,1)S(1)}, bf16[16,7040]{1,0:T(8,128)(2,1)S(1)}, u32[]{:S(2)}, u32[]{:S(2)}) collective-permute-start(bf16[16,7040]{1,0:T(8,128)(2,1)S(1)} %join.1.refs_0_), channel_id=1, source_target_pairs={{0,24},{8,16},{16,8},{24,0},{1,25},{9,17},{17,9},{25,1},{2,26},{10... | collective-permute-start | bytes 675848 | tf_op jit(solution)/shard_map/ppermute | solution.py:886
  148.0 1.3 collective-permute-start.38
  149.3 5.8 %collective-permute-done.40.refs_3_ = bf16[16,7040]{1,0:T(8,128)(2,1)S(1)} collective-permute-done((bf16[16,7040]{1,0:T(8,128)(2,1)S(1)}, bf16[16,7040]{1,0:T(8,128)(2,1)S(1)}, u32[]{:S(2)}, u32[]{:S(2)}) %collective-permute-start.40) | collective-permute-done | bytes 225312 | tf_op jit(solution)/shard_map/ppermute | solution.py:886
  155.1 11.0 %collective-permute-done.39.refs_2_ = bf16[16,7040]{1,0:T(8,128)(2,1)S(1)} collective-permute-done((bf16[16,7040]{1,0:T(8,128)(2,1)S(1)}, bf16[16,7040]{1,0:T(8,128)(2,1)S(1)}, u32[]{:S(2)}, u32[]{:S(2)}) %collective-permute-start.39) | collective-permute-done | bytes 225312 | tf_op jit(solution)/shard_map/ppermute | solution.py:886
  166.1 1.5 final.1
  (73 shorter events, 12.0 us)
Async XLA Ops:
  2.3 6.5 %collective-permute-start.2 = (f32[88,128]{1,0:T(8,128)}, f32[88,128]{1,0:T(8,128)S(1)}, u32[]{:S(2)}, u32[]{:S(2)}) collective-permute-start(f32[88,128]{1,0:T(8,128)} %place.1.refs_0_), channel_id=1, source_target_pairs={{0,6},{1,7},{2,4},{3,5},{4,2},{5,3},{6,0},{7,1},{8,14},{9,15},{10,... | collective-permute-start | bytes 135176 | tf_op jit(solution)/shard_map/ppermute | solution.py:886
  6.2 4.3 %collective-permute-start.1 = (f32[88,128]{1,0:T(8,128)}, f32[88,128]{1,0:T(8,128)S(1)}, u32[]{:S(2)}, u32[]{:S(2)}) collective-permute-start(f32[88,128]{1,0:T(8,128)} %place.1.refs_0_), channel_id=1, source_target_pairs={{0,4},{1,5},{2,6},{3,7},{4,0},{5,1},{6,2},{7,3},{8,12},{9,13},{10,... | collective-permute-start | bytes 135176 | tf_op jit(solution)/shard_map/ppermute | solution.py:886
  6.7 4.3 %collective-permute-start = (f32[88,128]{1,0:T(8,128)}, f32[88,128]{1,0:T(8,128)S(1)}, u32[]{:S(2)}, u32[]{:S(2)}) collective-permute-start(f32[88,128]{1,0:T(8,128)} %place.1.refs_0_), channel_id=1, source_target_pairs={{0,2},{1,3},{2,0},{3,1},{4,6},{5,7},{6,4},{7,5},{8,10},{9,11},{10,... | collective-permute-start | bytes 135176 | tf_op jit(solution)/shard_map/ppermute | solution.py:886
  11.0 9.9 %collective-permute-start.4 = (bf16[64,3200]{1,0:T(8,128)(2,1)}, bf16[64,3200]{1,0:T(8,128)(2,1)S(1)}, u32[]{:S(2)}, u32[]{:S(2)}) collective-permute-start(bf16[64,3200]{1,0:T(8,128)(2,1)} %get-tuple-element.160.refs_0_), channel_id=1, source_target_pairs={{0,4},{1,5},{2,6},{3,7},{4,0},{5,1},{6,2},{7,3},{8,12},{9,13},{10,... | collective-permute-start | bytes 1228808 | tf_op jit(solution)/shard_map/ppermute | solution.py:886
  12.5 9.7 %collective-permute-start.3 = (bf16[64,3200]{1,0:T(8,128)(2,1)}, bf16[64,3200]{1,0:T(8,128)(2,1)S(1)}, u32[]{:S(2)}, u32[]{:S(2)}) collective-permute-start(bf16[64,3200]{1,0:T(8,128)(2,1)} %get-tuple-element.160.refs_0_), channel_id=1, source_target_pairs={{0,2},{1,3},{2,0},{3,1},{4,6},{5,7},{6,4},{7,5},{8,10},{9,11},{10,... | collective-permute-start | bytes 1228808 | tf_op jit(solution)/shard_map/ppermute | solution.py:886
  13.0 0.8 copy-start.5
  13.8 1.5 collective-permute-start.5
  15.3 1.0 copy-start
  17.1 12.3 %copy-start.3 = (bf16[64,3200]{1,0:T(8,128)(2,1)S(1)}, bf16[64,3200]{1,0:T(8,128)(2,1)}, u32[]{:S(2)}) copy-start(bf16[64,3200]{1,0:T(8,128)(2,1)} %get-tuple-element.160.refs_0_) | copy-start | bytes 1228804
  22.3 6.6 %collective-permute-start.6 = (bf16[32,3200]{1,0:T(8,128)(2,1)S(1)}, bf16[32,3200]{1,0:T(8,128)(2,1)S(1)}, u32[]{:S(2)}, u32[]{:S(2)}) collective-permute-start(bf16[32,3200]{1,0:T(8,128)(2,1)S(1)} %get-tuple-element.158), channel_id=1, source_target_pairs={{0,4},{1,5},{2,6},{3,7},{4,0},{5,1},{6,2},{7,3},{8,12},{9,13},{10,... | collective-permute-start | bytes 614408 | tf_op jit(solution)/shard_map/ppermute | solution.py:886
  22.7 9.4 %copy-start.4 = (bf16[192,1024]{1,0:T(8,128)(2,1)S(1)}, bf16[192,1024]{1,0:T(8,128)(2,1)}, u32[]{:S(2)}) copy-start(bf16[192,1024]{1,0:T(8,128)(2,1)} %get-tuple-element.183.refs_0_) | copy-start | bytes 1179652
  22.7 6.6 %collective-permute-start.7 = (bf16[32,3200]{1,0:T(8,128)(2,1)S(1)}, bf16[32,3200]{1,0:T(8,128)(2,1)S(1)}, u32[]{:S(2)}, u32[]{:S(2)}) collective-permute-start(bf16[32,3200]{1,0:T(8,128)(2,1)S(1)} %get-tuple-element.159), channel_id=1, source_target_pairs={{0,2},{1,3},{2,0},{3,1},{4,6},{5,7},{6,4},{7,5},{8,10},{9,11},{10,... | collective-permute-start | bytes 614408 | tf_op jit(solution)/shard_map/ppermute | solution.py:886
  23.3 5.4 %collective-permute-start.9 = (bf16[80,512]{1,0:T(8,128)(2,1)S(1)}, bf16[80,512]{1,0:T(8,128)(2,1)S(1)}, u32[]{:S(2)}, u32[]{:S(2)}) collective-permute-start(bf16[80,512]{1,0:T(8,128)(2,1)S(1)} %get-tuple-element.155), channel_id=1, source_target_pairs={{0,2},{1,3},{2,4},{3,5},{4,6},{5,7},{8,10},{9,11},{10,12},{11,13},... | collective-permute-start | bytes 245768 | tf_op jit(solution)/shard_map/ppermute | solution.py:1180
  26.7 2.2 %collective-permute-start.8 = (bf16[80,512]{1,0:T(8,128)(2,1)S(1)}, bf16[80,512]{1,0:T(8,128)(2,1)S(1)}, u32[]{:S(2)}, u32[]{:S(2)}) collective-permute-start(bf16[80,512]{1,0:T(8,128)(2,1)S(1)} %get-tuple-element.155), channel_id=1, source_target_pairs={{0,1},{1,2},{2,3},{3,4},{4,5},{5,6},{6,7},{8,9},{9,10},{10,11},{11... | collective-permute-start | bytes 245768 | tf_op jit(solution)/shard_map/ppermute | solution.py:1180
  29.5 18.3 %copy-start.7 = (s32[4,128]{1,0:T(4,128)S(1)}, s32[4,128]{1,0:T(4,128)}, u32[]{:S(2)}) copy-start(s32[4,128]{1,0:T(4,128)} %refs_8_.3) | copy-start | bytes 6148
  29.5 18.3 %collective-permute-start.14 = (bf16[4,64,3200]{2,1,0:T(8,128)(2,1)S(1)}, bf16[4,64,3200]{2,1,0:T(8,128)(2,1)S(1)}, u32[]{:S(2)}, u32[]{:S(2)}) collective-permute-start(bf16[4,64,3200]{2,1,0:T(8,128)(2,1)S(1)} %bundle.4.refs_0_), channel_id=1, source_target_pairs={{0,1},{1,0},{2,3},{3,2},{4,5},{5,4},{6,7},{7,6},{8,9},{9,8},{10,11... | collective-permute-start | bytes 4915208 | tf_op jit(solution)/shard_map/ppermute | solution.py:886
  32.1 12.9 %collective-permute-start.11 = (bf16[192,1024]{1,0:T(8,128)(2,1)S(1)}, bf16[192,1024]{1,0:T(8,128)(2,1)S(1)}, u32[]{:S(2)}, u32[]{:S(2)}) collective-permute-start(bf16[192,1024]{1,0:T(8,128)(2,1)S(1)} %copy-done.4), channel_id=1, source_target_pairs={{0,4},{1,5},{2,6},{3,7},{4,0},{5,1},{6,2},{7,3},{8,12},{9,13},{10,... | collective-permute-start | bytes 1179656 | tf_op jit(solution)/shard_map/ppermute | solution.py:886
  35.2 11.2 %collective-permute-start.10 = (bf16[192,1024]{1,0:T(8,128)(2,1)S(1)}, bf16[192,1024]{1,0:T(8,128)(2,1)S(1)}, u32[]{:S(2)}, u32[]{:S(2)}) collective-permute-start(bf16[192,1024]{1,0:T(8,128)(2,1)S(1)} %copy-done.4), channel_id=1, source_target_pairs={{0,2},{1,3},{2,0},{3,1},{4,6},{5,7},{6,4},{7,5},{8,10},{9,11},{10,... | collective-permute-start | bytes 1179656 | tf_op jit(solution)/shard_map/ppermute | solution.py:886
  46.5 8.1 %collective-permute-start.12 = (bf16[96,1024]{1,0:T(8,128)(2,1)S(1)}, bf16[96,1024]{1,0:T(8,128)(2,1)S(1)}, u32[]{:S(2)}, u32[]{:S(2)}) collective-permute-start(bf16[96,1024]{1,0:T(8,128)(2,1)S(1)} %get-tuple-element.175), channel_id=1, source_target_pairs={{0,4},{1,5},{2,6},{3,7},{4,0},{5,1},{6,2},{7,3},{8,12},{9,13},{10,... | collective-permute-start | bytes 589832 | tf_op jit(solution)/shard_map/ppermute | solution.py:886
  46.8 7.7 %collective-permute-start.13 = (bf16[96,1024]{1,0:T(8,128)(2,1)S(1)}, bf16[96,1024]{1,0:T(8,128)(2,1)S(1)}, u32[]{:S(2)}, u32[]{:S(2)}) collective-permute-start(bf16[96,1024]{1,0:T(8,128)(2,1)S(1)} %get-tuple-element.176), channel_id=1, source_target_pairs={{0,2},{1,3},{2,0},{3,1},{4,6},{5,7},{6,4},{7,5},{8,10},{9,11},{10,... | collective-permute-start | bytes 589832 | tf_op jit(solution)/shard_map/ppermute | solution.py:886
  54.5 3.6 %copy-start.1 = (bf16[4,128,512]{2,1,0:T(8,128)(2,1)S(1)}, bf16[4,128,512]{2,1,0:T(8,128)(2,1)}, u32[]{:S(2)}) copy-start(bf16[4,128,512]{2,1,0:T(8,128)(2,1)} %param.22) | copy-start | bytes 1572868
  54.5 3.6 %copy-start.2 = (f32[4,128,512]{2,1,0:T(8,128)S(1)}, f32[4,128,512]{2,1,0:T(8,128)}, u32[]{:S(2)}) copy-start(f32[4,128,512]{2,1,0:T(8,128)} %param.24) | copy-start | bytes 3145732
  54.7 3.5 %collective-permute-start.15 = (bf16[4,192,1024]{2,1,0:T(8,128)(2,1)S(1)}, bf16[4,192,1024]{2,1,0:T(8,128)(2,1)S(1)}, u32[]{:S(2)}, u32[]{:S(2)}) collective-permute-start(bf16[4,192,1024]{2,1,0:T(8,128)(2,1)S(1)} %bundle.5.refs_0_), channel_id=1, source_target_pairs={{0,1},{1,0},{2,3},{3,2},{4,5},{5,4},{6,7},{7,6},{8,9},{9,8},{10,11... | collective-permute-start | bytes 4718600 | tf_op jit(solution)/shard_map/ppermute | solution.py:886
  84.9 10.9 %collective-permute-start.16 = (bf16[4,4,16,3200]{3,2,1,0:T(8,128)(2,1)S(1)}, bf16[4,4,16,3200]{3,2,1,0:T(8,128)(2,1)S(1)}, u32[]{:S(2)}, u32[]{:S(2)}) collective-permute-start(bf16[4,4,16,3200]{3,2,1,0:T(8,128)(2,1)S(1)} %get-tuple-element.206), channel_id=1, source_target_pairs={{0,1},{1,0},{2,3},{3,2},{4,5},{5,4},{6,7},{7,6},{8,9},{9,8},{10,11... | collective-permute-start | bytes 4915208 | tf_op jit(solution)/shard_map/ppermute | solution.py:886
  85.1 6.7 %collective-permute-start.19 = (bf16[4,4,48,1024]{3,2,1,0:T(8,128)(2,1)S(1)}, bf16[4,4,48,1024]{3,2,1,0:T(8,128)(2,1)S(1)}, u32[]{:S(2)}, u32[]{:S(2)}) collective-permute-start(bf16[4,4,48,1024]{3,2,1,0:T(8,128)(2,1)S(1)} %get-tuple-element.222), channel_id=1, source_target_pairs={{0,1},{1,0},{2,3},{3,2},{4,5},{5,4},{6,7},{7,6},{8,9},{9,8},{10,11... | collective-permute-start | bytes 4718600 | tf_op jit(solution)/shard_map/ppermute | solution.py:886
  85.5 6.4 %collective-permute-start.18 = (bf16[80,512]{1,0:T(8,128)(2,1)S(1)}, bf16[80,512]{1,0:T(8,128)(2,1)S(1)}, u32[]{:S(2)}, u32[]{:S(2)}) collective-permute-start(bf16[80,512]{1,0:T(8,128)(2,1)S(1)} %get-tuple-element.212), channel_id=1, source_target_pairs={{2,0},{3,1},{4,2},{5,3},{6,4},{7,5},{10,8},{11,9},{12,10},{13,11},... | collective-permute-start | bytes 245768 | tf_op jit(solution)/shard_map/ppermute | solution.py:1267
  86.8 5.1 %collective-permute-start.17 = (bf16[80,512]{1,0:T(8,128)(2,1)S(1)}, bf16[80,512]{1,0:T(8,128)(2,1)S(1)}, u32[]{:S(2)}, u32[]{:S(2)}) collective-permute-start(bf16[80,512]{1,0:T(8,128)(2,1)S(1)} %get-tuple-element.212), channel_id=1, source_target_pairs={{1,0},{2,1},{3,2},{4,3},{5,4},{6,5},{7,6},{9,8},{10,9},{11,10},{12... | collective-permute-start | bytes 245768 | tf_op jit(solution)/shard_map/ppermute | solution.py:1267
  92.2 14.8 %collective-permute-start.20 = (bf16[4,48,1024]{2,1,0:T(8,128)(2,1)S(1)}, bf16[4,48,1024]{2,1,0:T(8,128)(2,1)S(1)}, u32[]{:S(2)}, u32[]{:S(2)}) collective-permute-start(bf16[4,48,1024]{2,1,0:T(8,128)(2,1)S(1)} %get-tuple-element.224), channel_id=1, source_target_pairs={{0,2},{1,3},{2,0},{3,1},{4,6},{5,7},{6,4},{7,5},{8,10},{9,11},{10,... | collective-permute-start | bytes 1179656 | tf_op jit(solution)/shard_map/ppermute | solution.py:886
  94.3 12.7 %collective-permute-start.21 = (bf16[4,48,1024]{2,1,0:T(8,128)(2,1)S(1)}, bf16[4,48,1024]{2,1,0:T(8,128)(2,1)S(1)}, u32[]{:S(2)}, u32[]{:S(2)}) collective-permute-start(bf16[4,48,1024]{2,1,0:T(8,128)(2,1)S(1)} %get-tuple-element.225), channel_id=1, source_target_pairs={{0,4},{1,5},{2,6},{3,7},{4,0},{5,1},{6,2},{7,3},{8,12},{9,13},{10,... | collective-permute-start | bytes 1179656 | tf_op jit(solution)/shard_map/ppermute | solution.py:886
  96.2 15.5 %collective-permute-start.27 = (bf16[4,16,3200]{2,1,0:T(8,128)(2,1)S(1)}, bf16[4,16,3200]{2,1,0:T(8,128)(2,1)S(1)}, u32[]{:S(2)}, u32[]{:S(2)}) collective-permute-start(bf16[4,16,3200]{2,1,0:T(8,128)(2,1)S(1)} %get-tuple-element.237), channel_id=1, source_target_pairs={{0,2},{1,3},{2,0},{3,1},{4,6},{5,7},{6,4},{7,5},{8,10},{9,11},{10,... | collective-permute-start | bytes 1228808 | tf_op jit(solution)/shard_map/ppermute | solution.py:886
  97.2 17.1 %collective-permute-start.28 = (bf16[4,16,3200]{2,1,0:T(8,128)(2,1)S(1)}, bf16[4,16,3200]{2,1,0:T(8,128)(2,1)S(1)}, u32[]{:S(2)}, u32[]{:S(2)}) collective-permute-start(bf16[4,16,3200]{2,1,0:T(8,128)(2,1)S(1)} %get-tuple-element.238), channel_id=1, source_target_pairs={{0,4},{1,5},{2,6},{3,7},{4,0},{5,1},{6,2},{7,3},{8,12},{9,13},{10,... | collective-permute-start | bytes 1228808 | tf_op jit(solution)/shard_map/ppermute | solution.py:886
  107.0 10.6 %collective-permute-start.22 = (bf16[2,48,1024]{2,1,0:T(8,128)(2,1)S(1)}, bf16[2,48,1024]{2,1,0:T(8,128)(2,1)S(1)}, u32[]{:S(2)}, u32[]{:S(2)}) collective-permute-start(bf16[2,48,1024]{2,1,0:T(8,128)(2,1)S(1)} %get-tuple-element.231), channel_id=1, source_target_pairs={{0,2},{1,3},{2,0},{3,1},{4,6},{5,7},{6,4},{7,5},{8,10},{9,11},{10,... | collective-permute-start | bytes 589832 | tf_op jit(solution)/shard_map/ppermute | solution.py:886
  108.7 9.7 %collective-permute-start.23 = (bf16[2,48,1024]{2,1,0:T(8,128)(2,1)S(1)}, bf16[2,48,1024]{2,1,0:T(8,128)(2,1)S(1)}, u32[]{:S(2)}, u32[]{:S(2)}) collective-permute-start(bf16[2,48,1024]{2,1,0:T(8,128)(2,1)S(1)} %get-tuple-element.232), channel_id=1, source_target_pairs={{0,4},{1,5},{2,6},{3,7},{4,0},{5,1},{6,2},{7,3},{8,12},{9,13},{10,... | collective-permute-start | bytes 589832 | tf_op jit(solution)/shard_map/ppermute | solution.py:886
  114.3 9.3 %collective-permute-start.29 = (bf16[2,16,3200]{2,1,0:T(8,128)(2,1)S(1)}, bf16[2,16,3200]{2,1,0:T(8,128)(2,1)S(1)}, u32[]{:S(2)}, u32[]{:S(2)}) collective-permute-start(bf16[2,16,3200]{2,1,0:T(8,128)(2,1)S(1)} %get-tuple-element.243), channel_id=1, source_target_pairs={{0,2},{1,3},{2,0},{3,1},{4,6},{5,7},{6,4},{7,5},{8,10},{9,11},{10,... | collective-permute-start | bytes 614408 | tf_op jit(solution)/shard_map/ppermute | solution.py:886
  115.1 5.2 %collective-permute-start.34 = (f32[4,88,128]{2,1,0:T(8,128)S(1)}, f32[4,88,128]{2,1,0:T(8,128)S(1)}, u32[]{:S(2)}, u32[]{:S(2)}) collective-permute-start(f32[4,88,128]{2,1,0:T(8,128)S(1)} %get-tuple-element.249), channel_id=1, source_target_pairs={{0,1},{1,0},{2,3},{3,2},{4,5},{5,4},{6,7},{7,6},{8,9},{9,8},{10,11... | collective-permute-start | bytes 540680 | tf_op jit(solution)/shard_map/ppermute | solution.py:886
  116.2 8.0 %collective-permute-start.30 = (bf16[2,16,3200]{2,1,0:T(8,128)(2,1)S(1)}, bf16[2,16,3200]{2,1,0:T(8,128)(2,1)S(1)}, u32[]{:S(2)}, u32[]{:S(2)}) collective-permute-start(bf16[2,16,3200]{2,1,0:T(8,128)(2,1)S(1)} %get-tuple-element.244), channel_id=1, source_target_pairs={{0,4},{1,5},{2,6},{3,7},{4,0},{5,1},{6,2},{7,3},{8,12},{9,13},{10,... | collective-permute-start | bytes 614408 | tf_op jit(solution)/shard_map/ppermute | solution.py:886
  118.6 12.6 %collective-permute-start.24 = (bf16[48,1024]{1,0:T(8,128)(2,1)S(1)}, bf16[48,1024]{1,0:T(8,128)(2,1)S(1)}, u32[]{:S(2)}, u32[]{:S(2)}) collective-permute-start(bf16[48,1024]{1,0:T(8,128)(2,1)S(1)} %get-tuple-element.234), channel_id=1, source_target_pairs={{0,8},{8,0},{16,24},{24,16},{1,9},{9,1},{17,25},{25,17},{2,10},{10... | collective-permute-start | bytes 294920 | tf_op jit(solution)/shard_map/ppermute | solution.py:886
  120.3 5.7 %collective-permute-start.35 = (f32[88,128]{1,0:T(8,128)S(1)}, f32[88,128]{1,0:T(8,128)S(1)}, u32[]{:S(2)}, u32[]{:S(2)}) collective-permute-start(f32[88,128]{1,0:T(8,128)S(1)} %get-tuple-element.251), channel_id=1, source_target_pairs={{0,2},{1,3},{2,0},{3,1},{4,6},{5,7},{6,4},{7,5},{8,10},{9,11},{10,... | collective-permute-start | bytes 135176 | tf_op jit(solution)/shard_map/ppermute | solution.py:886
  121.1 7.5 %collective-permute-start.36 = (f32[88,128]{1,0:T(8,128)S(1)}, f32[88,128]{1,0:T(8,128)S(1)}, u32[]{:S(2)}, u32[]{:S(2)}) collective-permute-start(f32[88,128]{1,0:T(8,128)S(1)} %get-tuple-element.252), channel_id=1, source_target_pairs={{0,4},{1,5},{2,6},{3,7},{4,0},{5,1},{6,2},{7,3},{8,12},{9,13},{10,... | collective-permute-start | bytes 135176 | tf_op jit(solution)/shard_map/ppermute | solution.py:886
  123.6 5.3 %collective-permute-start.37 = (f32[88,128]{1,0:T(8,128)S(1)}, f32[88,128]{1,0:T(8,128)S(1)}, u32[]{:S(2)}, u32[]{:S(2)}) collective-permute-start(f32[88,128]{1,0:T(8,128)S(1)} %get-tuple-element.253), channel_id=1, source_target_pairs={{0,6},{1,7},{2,4},{3,5},{4,2},{5,3},{6,0},{7,1},{8,14},{9,15},{10,... | collective-permute-start | bytes 135176 | tf_op jit(solution)/shard_map/ppermute | solution.py:886
  124.4 20.3 %collective-permute-start.31 = (bf16[16,3200]{1,0:T(8,128)(2,1)S(1)}, bf16[16,3200]{1,0:T(8,128)(2,1)S(1)}, u32[]{:S(2)}, u32[]{:S(2)}) collective-permute-start(bf16[16,3200]{1,0:T(8,128)(2,1)S(1)} %get-tuple-element.246), channel_id=1, source_target_pairs={{0,8},{8,0},{16,24},{24,16},{1,9},{9,1},{17,25},{25,17},{2,10},{10... | collective-permute-start | bytes 307208 | tf_op jit(solution)/shard_map/ppermute | solution.py:886
  126.1 18.7 %collective-permute-start.32 = (bf16[16,3200]{1,0:T(8,128)(2,1)S(1)}, bf16[16,3200]{1,0:T(8,128)(2,1)S(1)}, u32[]{:S(2)}, u32[]{:S(2)}) collective-permute-start(bf16[16,3200]{1,0:T(8,128)(2,1)S(1)} %get-tuple-element.247), channel_id=1, source_target_pairs={{0,16},{8,24},{16,0},{24,8},{1,17},{9,25},{17,1},{25,9},{2,18},{10... | collective-permute-start | bytes 307208 | tf_op jit(solution)/shard_map/ppermute | solution.py:886
  128.6 16.1 %collective-permute-start.33 = (bf16[16,3200]{1,0:T(8,128)(2,1)S(1)}, bf16[16,3200]{1,0:T(8,128)(2,1)S(1)}, u32[]{:S(2)}, u32[]{:S(2)}) collective-permute-start(bf16[16,3200]{1,0:T(8,128)(2,1)S(1)} %get-tuple-element.248), channel_id=1, source_target_pairs={{0,24},{8,16},{16,8},{24,0},{1,25},{9,17},{17,9},{25,1},{2,26},{10... | collective-permute-start | bytes 307208 | tf_op jit(solution)/shard_map/ppermute | solution.py:886
  128.9 15.8 %collective-permute-start.25 = (bf16[48,1024]{1,0:T(8,128)(2,1)S(1)}, bf16[48,1024]{1,0:T(8,128)(2,1)S(1)}, u32[]{:S(2)}, u32[]{:S(2)}) collective-permute-start(bf16[48,1024]{1,0:T(8,128)(2,1)S(1)} %get-tuple-element.235), channel_id=1, source_target_pairs={{0,16},{8,24},{16,0},{24,8},{1,17},{9,25},{17,1},{25,9},{2,18},{10... | collective-permute-start | bytes 294920 | tf_op jit(solution)/shard_map/ppermute | solution.py:886
  131.2 13.5 %collective-permute-start.26 = (bf16[48,1024]{1,0:T(8,128)(2,1)S(1)}, bf16[48,1024]{1,0:T(8,128)(2,1)S(1)}, u32[]{:S(2)}, u32[]{:S(2)}) collective-permute-start(bf16[48,1024]{1,0:T(8,128)(2,1)S(1)} %get-tuple-element.236), channel_id=1, source_target_pairs={{0,24},{8,16},{16,8},{24,0},{1,25},{9,17},{17,9},{25,1},{2,26},{10... | collective-permute-start | bytes 294920 | tf_op jit(solution)/shard_map/ppermute | solution.py:886
  144.9 10.2 %collective-permute-start.40 = (bf16[16,7040]{1,0:T(8,128)(2,1)S(1)}, bf16[16,7040]{1,0:T(8,128)(2,1)S(1)}, u32[]{:S(2)}, u32[]{:S(2)}) collective-permute-start(bf16[16,7040]{1,0:T(8,128)(2,1)S(1)} %join.1.refs_0_), channel_id=1, source_target_pairs={{0,24},{8,16},{16,8},{24,0},{1,25},{9,17},{17,9},{25,1},{2,26},{10... | collective-permute-start | bytes 675848 | tf_op jit(solution)/shard_map/ppermute | solution.py:886
  147.6 18.5 %collective-permute-start.39 = (bf16[16,7040]{1,0:T(8,128)(2,1)S(1)}, bf16[16,7040]{1,0:T(8,128)(2,1)S(1)}, u32[]{:S(2)}, u32[]{:S(2)}) collective-permute-start(bf16[16,7040]{1,0:T(8,128)(2,1)S(1)} %join.1.refs_0_), channel_id=1, source_target_pairs={{0,16},{8,24},{16,0},{24,8},{1,17},{9,25},{17,1},{25,9},{2,18},{10... | collective-permute-start | bytes 675848 | tf_op jit(solution)/shard_map/ppermute | solution.py:886
  148.0 18.1 %collective-permute-start.38 = (bf16[16,7040]{1,0:T(8,128)(2,1)S(1)}, bf16[16,7040]{1,0:T(8,128)(2,1)S(1)}, u32[]{:S(2)}, u32[]{:S(2)}) collective-permute-start(bf16[16,7040]{1,0:T(8,128)(2,1)S(1)} %join.1.refs_0_), channel_id=1, source_target_pairs={{0,8},{8,0},{16,24},{24,16},{1,9},{9,1},{17,25},{25,17},{2,10},{10... | collective-permute-start | bytes 675848 | tf_op jit(solution)/shard_map/ppermute | solution.py:886
  (1 other events, 0.7 us)

commit v4 on v3

--- a/solution.py
+++ b/solution.py
@@ -891,8 +891,7 @@
         out[...] = (own[k].astype(F32) + got[k].astype(F32)).astype(out.dtype)
 
 
-def fold(own, sib, dtype):
-    got = hop(sib, "seq", 1)
+def fold(own, got, dtype):
     outs = [struct(own.shape[1:], F32)] + [struct(own.shape[1:], dtype)] * (own.shape[0] - 1)
     return whole(fold_kernel, outs, n_in=2, name="fold")(own, got)
 
@@ -917,8 +916,7 @@
     later_y[...] = piece(2, top)
 
 
-def split(own, sib):
-    got = hop(sib, "seq", 1)
+def split(own, got):
     shape = own.shape[1:]
     half = (shape[0] // 2,) + shape[1:]
     return whole(
@@ -935,11 +933,11 @@
     to_y[...] = (later_y[...] + from_x[h:].astype(F32)).astype(BF)
 
 
-def spread_sums(own, sib, devices, tie):
+def spread_sums(own, got, devices):
     if devices != 8:
-        parts = across(fold(own, sib, BF))
+        parts = across(fold(own, got, BF))
         return parts[:1], parts[:1], lambda *first: parts
-    kept, to_x, to_y, later_x, later_y = split(own, sib)
+    kept, to_x, to_y, later_x, later_y = split(own, got)
     from_x, from_y = hop(to_x, "seq", 2), hop(to_y, "seq", 4)
 
     def finish(*first):
@@ -1263,6 +1261,8 @@
         micros=15,
     )(*w1, probs, attg, vlow, dval, qlow, klow, lat, blu, blre, z, nrm, pd, pz, dk, lab)
 
+    got_a = hop(sib_a, "seq", 1)
+    back_msg = after(back_msg, got_a)
     backward = [
         lax.ppermute(back_msg, "seq", [(i + k, i) for i in range(devices - k)])
         for k in range(1, reach + 1)
@@ -1278,8 +1278,8 @@
         micros=6,
     )(nlow, mlow, vgl, blu, bll, blre)
 
-    _, _, finish_a = spread_sums(after(own_a, backward), sib_a, devices, None)
-    tie_b, _, finish_b = spread_sums(own_b, sib_b, devices, None)
+    _, _, finish_a = spread_sums(after(own_a, backward), got_a, devices)
+    tie_b, _, finish_b = spread_sums(own_b, hop(after(sib_b, backward), "seq", 1), devices)
     nrm = after(nrm, tie_b)
     piece_c = struct((half, ROWS_SMALL, TILE), F32)
     wide = ceil_div(nm, TILE) + 2
@@ -1299,7 +1299,7 @@
 
     sum_a = deal(finish_a(own_c), depth, devices)
     sum_b = deal(finish_b(own_c), depth, devices)
-    parts_c = across(fold(own_c, sib_c, F32))
+    parts_c = across(fold(after(own_c, sum_b[0]), hop(sib_c, "seq", 1), F32))
     everything = join(sum_a, sum_b, parts_c)
     grads = whole(
         partial(final_kernel, depth=depth, plan=plan, held=held, dims=dims),

time: 168 us -> 162 us (0.964)
  waiting for transfers between devices: 55.6 us -> 45.4 us
  local copies, waits for them, and re-layouts: 2.54 us -> 4.53 us
  starting transfers between devices: 51.7 us -> 53.5 us
    ppermute x37, waiting for transfers between devices: 50.9 us -> 42.8 us  [hop(): return lax.ppermute(x, axis, [(i, i ^ k) for i in range(length)])]
    ppermute x2, waiting for transfers between devices: 3.81 us -> 1.69 us  [per_device(): lax.ppermute(back_msg, 'seq', [(i + k, i) for i in range(devices - k)])]
    unnamed x16 -> x24, local copies, waits for them, and re-layouts: 2.54 us -> 4.53 us
    ppermute x37, starting transfers between devices: 44.5 us -> 46.3 us  [hop(): return lax.ppermute(x, axis, [(i, i ^ k) for i in range(length)])]
  transfers between devices with their start and end apart: 41 -> 41, of which waited for: 18 -> 22; matrix products, arithmetic and copies ran while one was open for 0% -> 0% of each run, Pallas kernels for 16% -> 25%
where the time goes in v4:
time: 162 us; the launch traced here: 161 us
  Pallas kernels  56.8 us (35%)
  starting transfers between devices  53.5 us (33%)
  waiting for transfers between devices  45.4 us (28%)
  local copies, waits for them, and re-layouts  4.53 us (3%)
    ppermute x37, starting transfers between devices, hop(): return lax.ppermute(x, axis, [(i, i ^ k) for i in range(length)])  46.3 us
    ppermute x37, waiting for transfers between devices, hop(): return lax.ppermute(x, axis, [(i, i ^ k) for i in range(length)])  42.8 us
    pallas_call x1, Pallas kernels, per_device(): whole(partial(middle_kernel, devices=devices, depth=depth, dims=dims), [s...  13.3 us
    pallas_call x1, Pallas kernels, per_device(): whole(partial(back_kernel, devices=devices, dims=dims), [struct((count, n...  11.2 us
    pallas_call x1, Pallas kernels, per_device(): whole(partial(last_kernel, reach=reach, devices=devices, dims=dims, seqs=...  9.81 us
    pallas_call x1, Pallas kernels, per_device(): whole(partial(front_kernel, devices=devices), [struct((count, nv), BF), s...  6.76 us
    ppermute x2, starting transfers between devices, per_device(): lax.ppermute(msg, 'seq', [(i, i + k) for i in range(devices - k)])  4.61 us
    unnamed x24, local copies, waits for them, and re-layouts  4.53 us
  transfers between devices with their start and end apart: 41, of which 22 were waited for; matrix products, arithmetic and copies ran while one was open for 0% of the time, Pallas kernels for 25%

profile of v4, /device:TPU:0, one launch (start us, length us, event | category | flops | bytes accessed | tf_op | source)
XLA Modules:
  0.0 161.3 jit_solution(372891710539796943)
XLA Ops:
  0.7 1.7 %place.1.refs_0_ = f32[88,128]{1,0:T(8,128)} custom-call(bf16[16,64]{1,0:T(8,128)(2,1)} %bitcast.16, bf16[16,64]{1,0:T(8,128)(2,1)} %bitcast.17, bf16[16,64]{1,0:T(8,128)(2,1)} %bitcast.18, bf16[16,64]{1,0:T(8,128)(2,1)} %bitcast.19, bf16[128]{0:T(256)(128)(2,1)} %refs_4_.1, bf16[128]{0:T(256)(128)(2,1)} %refs_5_.1, bf16[272]{0:T(512)(128)(2,1)} %refs_6_.1, ...), custom_call_target="tpu_custom_call" | custom-call | bytes 7380000 | tf_op jit(solution)/shard_map/place/pallas_call | solution.py:1140
  2.3 3.9 %collective-permute-start.2 = (f32[88,128]{1,0:T(8,128)}, f32[88,128]{1,0:T(8,128)S(1)}, u32[]{:S(2)}, u32[]{:S(2)}) collective-permute-start(f32[88,128]{1,0:T(8,128)} %place.1.refs_0_), channel_id=1, source_target_pairs={{0,6},{1,7},{2,4},{3,5},{4,2},{5,3},{6,0},{7,1},{8,14},{9,15},{10,... | collective-permute-start | bytes 135176 | tf_op jit(solution)/shard_map/ppermute | solution.py:886
  6.8 2.1 %pack.1 = (bf16[64,3200]{1,0:T(8,128)(2,1)}, bf16[192,1024]{1,0:T(8,128)(2,1)}) custom-call(bf16[64,1024]{1,0:T(8,128)(2,1)} %value, bf16[64,2176]{1,0:T(8,128)(2,1)} %mix, bf16[128,512]{1,0:T(8,128)(2,1)} %attend, bf16[128,512]{1,0:T(8,128)(2,1)} %down, bf16[64,1024]{1,0:T(8,128)(2,1)} %up), custom_call_target="tpu_custom_call" | custom-call | bytes 7380000 | tf_op jit(solution)/shard_map/pack/pallas_call | solution.py:1147
  8.9 1.6 %collective-permute-done.1.refs_2_ = f32[88,128]{1,0:T(8,128)S(1)} collective-permute-done((f32[88,128]{1,0:T(8,128)}, f32[88,128]{1,0:T(8,128)S(1)}, u32[]{:S(2)}, u32[]{:S(2)}) %collective-permute-start.1) | collective-permute-done | bytes 45088 | tf_op jit(solution)/shard_map/ppermute | solution.py:886
  11.0 1.5 collective-permute-start.4
  13.9 1.4 collective-permute-done.5.refs_1_
  15.3 1.0 copy-done
  17.1 2.5 %head.1 = (f32[72,512]{1,0:T(8,128)S(1)}, f32[8,1024]{1,0:T(8,128)S(1)}, f32[8,128]{1,0:T(8,128)S(1)}, f32[8,2176]{1,0:T(8,128)S(1)}, f32[48,512]{1,0:T(8,128)S(...) custom-call(f32[4,88,128]{2,1,0:T(8,128)S(1)} %bundle.3.refs_0_, ...), custom_call_target="tpu_custom_call" | custom-call | bytes 22140000 | tf_op jit(solution)/shard_map/head/pallas_call | solution.py:1162
  19.6 1.3 collective-permute-done.4.y.refs_2_
  20.9 1.4 collective-permute-done.3.x.refs_1_
  23.3 3.3 %collective-permute-start.9 = (bf16[80,512]{1,0:T(8,128)(2,1)S(1)}, bf16[80,512]{1,0:T(8,128)(2,1)S(1)}, u32[]{:S(2)}, u32[]{:S(2)}) collective-permute-start(bf16[80,512]{1,0:T(8,128)(2,1)S(1)} %get-tuple-element.158), channel_id=1, source_target_pairs={{0,2},{1,3},{2,4},{3,5},{4,6},{5,7},{8,10},{9,11},{10,12},{11,13},... | collective-permute-start | bytes 245768 | tf_op jit(solution)/shard_map/ppermute | solution.py:1178
  26.7 1.3 collective-permute-start.8
  29.5 2.6 %collective-permute-start.14 = (bf16[4,64,3200]{2,1,0:T(8,128)(2,1)S(1)}, bf16[4,64,3200]{2,1,0:T(8,128)(2,1)S(1)}, u32[]{:S(2)}, u32[]{:S(2)}) collective-permute-start(bf16[4,64,3200]{2,1,0:T(8,128)(2,1)S(1)} %bundle.4.refs_0_), channel_id=1, source_target_pairs={{0,1},{1,0},{2,3},{3,2},{4,5},{5,4},{6,7},{7,6},{8,9},{9,8},{10,11... | collective-permute-start | bytes 4915208 | tf_op jit(solution)/shard_map/ppermute | solution.py:886
  32.1 3.2 %collective-permute-start.11 = (bf16[192,1024]{1,0:T(8,128)(2,1)S(1)}, bf16[192,1024]{1,0:T(8,128)(2,1)S(1)}, u32[]{:S(2)}, u32[]{:S(2)}) collective-permute-start(bf16[192,1024]{1,0:T(8,128)(2,1)S(1)} %copy-done.8), channel_id=1, source_target_pairs={{0,4},{1,5},{2,6},{3,7},{4,0},{5,1},{6,2},{7,3},{8,12},{9,13},{10,... | collective-permute-start | bytes 1179656 | tf_op jit(solution)/shard_map/ppermute | solution.py:886
  35.2 4.2 %scan.1 = (f32[512,512]{1,0:T(8,128)S(1)}, bf16[512,512]{1,0:T(8,128)(2,1)S(1)}, bf16[4,64,128,128]{3,2,1,0:T(8,128)(2,1)S(1)}) custom-call(f32[4,512,128]{2,1,0:T(8,128)S(1)} %get-tuple-element.215.refs_0_.refs_12_.refs_1_, f32[512,128]{1,0:T(8,128)S(1)} %get-tuple-element.171.refs_1_.refs_7_.refs_16_.refs_4_, ...), custom_call_target="tpu_custom_call" | custom-call | bytes 29520000 | tf_op jit(solution)/shard_map/scan/pallas_call | solution.py:1188
  39.4 1.0 copy-done.3
  40.5 4.5 %collective-permute-done.11.y.refs_2_ = bf16[192,1024]{1,0:T(8,128)(2,1)S(1)} collective-permute-done((bf16[192,1024]{1,0:T(8,128)(2,1)S(1)}, bf16[192,1024]{1,0:T(8,128)(2,1)S(1)}, u32[]{:S(2)}, u32[]{:S(2)}) %collective-permute-start.11) | collective-permute-done | bytes 393248 | tf_op jit(solution)/shard_map/ppermute | solution.py:886
  44.9 1.5 collective-permute-done.10.x.refs_1_
  47.7 6.8 %front.1 = (bf16[512,1024]{1,0:T(8,128)(2,1)S(1)}, bf16[512,1024]{1,0:T(8,128)(2,1)S(1)}, f32[512,512]{1,0:T(8,128)S(1)}, f32[512,512]{1,0:T(8,128)S(1)}, f32[51...) custom-call(bf16[4,64,3200]{2,1,0:T(8,128)(2,1)S(1)} %bundle.4.refs_, ...), custom_call_target="tpu_custom_call" | custom-call | bytes 40590000 | tf_op jit(solution)/shard_map/front/pallas_call | solution.py:1208
  55.7 3.4 %collective-permute-done.15.refs_1_ = bf16[4,192,1024]{2,1,0:T(8,128)(2,1)S(1)} collective-permute-done((bf16[4,192,1024]{2,1,0:T(8,128)(2,1)S(1)}, bf16[4,192,1024]{2,1,0:T(8,128)(2,1)S(1)}, u32[]{:S(2)}, u32[]{:S(2)}) %collective-permute-start.15) | collective-permute-done | bytes 1572896 | tf_op jit(solution)/shard_map/ppermute | solution.py:886
  59.1 13.3 %middle.1 = (f32[512,512]{1,0:T(8,128)}, f32[512,512]{1,0:T(8,128)S(1)}, bf16[512,1024]{1,0:T(8,128)(2,1)S(1)}, bf16[512,512]{1,0:T(8,128)(2,1)S(1)}, bf16[512,1...) custom-call(bf16[4,192,1024]{2,1,0:T(8,128)(2,1)S(1)} %bundle.5.refs, ...), custom_call_target="tpu_custom_call" | custom-call | bytes 70110000 | tf_op jit(solution)/shard_map/middle/pallas_call | solution.py:1226
  72.6 11.2 %back.1 = (bf16[512,1024]{1,0:T(8,128)(2,1)S(1)}, bf16[512,128]{1,0:T(8,128)(2,1)S(1)}, f32[4,512,128]{2,1,0:T(8,128)S(1)}, f32[4,512,128]{2,1,0:T(8,128)S(1)}, ...) custom-call(bf16[4,64,3200]{2,1,0:T(8,128)(2,1)S(1)} %bundle.4.refs_, ...), custom_call_target="tpu_custom_call" | custom-call | bytes 55350000 | tf_op jit(solution)/shard_map/back/pallas_call | solution.py:1246
  83.8 1.3 collective-permute-start.18
  85.1 1.3 collective-permute-start.17
  86.4 2.3 %weights.1 = (bf16[4,4,16,3200]{3,2,1,0:T(8,128)(2,1)S(1)}, bf16[4,4,16,3200]{3,2,1,0:T(8,128)(2,1)S(1)}) custom-call(bf16[512,512]{1,0:T(8,128)(2,1)S(1)} %get-tuple-element.180.refs_2_.nlow, bf16[512,512]{1,0:T(8,128)(2,1)S(1)} %get-tuple-element.181.refs_3_.mlow, bf16[512,1024]{1,0:T(8,128)(2,1)S(1)} %get-tuple-element.206.vgl, ...), custom_call_target="tpu_custom_call" | custom-call | bytes 22140000 | tf_op jit(solution)/shard_map/weights/pallas_call | solution.py:1272
  88.7 1.7 %collective-permute-done.18.refs_8_ = bf16[80,512]{1,0:T(8,128)(2,1)S(1)} collective-permute-done((bf16[80,512]{1,0:T(8,128)(2,1)S(1)}, bf16[80,512]{1,0:T(8,128)(2,1)S(1)}, u32[]{:S(2)}, u32[]{:S(2)}) %collective-permute-start.18) | collective-permute-done | bytes 81952 | tf_op jit(solution)/shard_map/ppermute | solution.py:1267
  90.4 1.5 collective-permute-start.19
  92.2 2.6 %collective-permute-start.20 = (bf16[4,48,1024]{2,1,0:T(8,128)(2,1)S(1)}, bf16[4,48,1024]{2,1,0:T(8,128)(2,1)S(1)}, u32[]{:S(2)}, u32[]{:S(2)}) collective-permute-start(bf16[4,48,1024]{2,1,0:T(8,128)(2,1)S(1)} %get-tuple-element.229), channel_id=1, source_target_pairs={{0,2},{1,3},{2,0},{3,1},{4,6},{5,7},{6,4},{7,5},{8,10},{9,11},{10,... | collective-permute-start | bytes 1179656 | tf_op jit(solution)/shard_map/ppermute | solution.py:886
  95.4 2.7 %collective-permute-start.27 = (bf16[4,16,3200]{2,1,0:T(8,128)(2,1)S(1)}, bf16[4,16,3200]{2,1,0:T(8,128)(2,1)S(1)}, u32[]{:S(2)}, u32[]{:S(2)}) collective-permute-start(bf16[4,16,3200]{2,1,0:T(8,128)(2,1)S(1)} %get-tuple-element.242), channel_id=1, source_target_pairs={{0,2},{1,3},{2,0},{3,1},{4,6},{5,7},{6,4},{7,5},{8,10},{9,11},{10,... | collective-permute-start | bytes 1228808 | tf_op jit(solution)/shard_map/ppermute | solution.py:886
  98.2 9.8 %last.1 = (f32[512,512]{1,0:T(8,128)}, f32[4,88,128]{2,1,0:T(8,128)S(1)}, f32[4,88,128]{2,1,0:T(8,128)S(1)}) custom-call(bf16[4,64,128,128]{3,2,1,0:T(8,128)(2,1)S(1)} %get-tuple-element.196.refs_0_, f32[4,512,128]{2,1,0:T(8,128)S(1)} %get-tuple-element.215.refs_0_.refs_12_.refs_1_, f32[4,512,128]{2,1,0:T(8,128)S(1)} %get-tuple-element.216.refs_2_, ...), custom_call_target="tpu_custom_call" | custom-call | bytes 44280000 | tf_op jit(solution)/shard_map/last/pallas_call | solution.py:1286
  108.1 1.6 collective-permute-start.22
  110.1 3.5 %collective-permute-done.27.from_x.refs_1_ = bf16[4,16,3200]{2,1,0:T(8,128)(2,1)S(1)} collective-permute-done((bf16[4,16,3200]{2,1,0:T(8,128)(2,1)S(1)}, bf16[4,16,3200]{2,1,0:T(8,128)(2,1)S(1)}, u32[]{:S(2)}, u32[]{:S(2)}) %collective-permute-start.27) | collective-permute-done | bytes 409632 | tf_op jit(solution)/shard_map/ppermute | solution.py:886
  113.6 2.1 %collective-permute-done.28.from_y.refs_2_ = bf16[4,16,3200]{2,1,0:T(8,128)(2,1)S(1)} collective-permute-done((bf16[4,16,3200]{2,1,0:T(8,128)(2,1)S(1)}, bf16[4,16,3200]{2,1,0:T(8,128)(2,1)S(1)}, u32[]{:S(2)}, u32[]{:S(2)}) %collective-permute-start.28) | collective-permute-done | bytes 409632 | tf_op jit(solution)/shard_map/ppermute | solution.py:886
  115.8 1.6 %collective-permute-start.30 = (bf16[2,16,3200]{2,1,0:T(8,128)(2,1)S(1)}, bf16[2,16,3200]{2,1,0:T(8,128)(2,1)S(1)}, u32[]{:S(2)}, u32[]{:S(2)}) collective-permute-start(bf16[2,16,3200]{2,1,0:T(8,128)(2,1)S(1)} %get-tuple-element.249), channel_id=1, source_target_pairs={{0,4},{1,5},{2,6},{3,7},{4,0},{5,1},{6,2},{7,3},{8,12},{9,13},{10,... | collective-permute-start | bytes 614408 | tf_op jit(solution)/shard_map/ppermute | solution.py:886
  117.8 2.1 %collective-permute-done.23.refs_4_ = bf16[2,48,1024]{2,1,0:T(8,128)(2,1)S(1)} collective-permute-done((bf16[2,48,1024]{2,1,0:T(8,128)(2,1)S(1)}, bf16[2,48,1024]{2,1,0:T(8,128)(2,1)S(1)}, u32[]{:S(2)}, u32[]{:S(2)}) %collective-permute-start.23) | collective-permute-done | bytes 196640 | tf_op jit(solution)/shard_map/ppermute | solution.py:886
  120.1 1.6 %collective-permute-start.24 = (bf16[48,1024]{1,0:T(8,128)(2,1)S(1)}, bf16[48,1024]{1,0:T(8,128)(2,1)S(1)}, u32[]{:S(2)}, u32[]{:S(2)}) collective-permute-start(bf16[48,1024]{1,0:T(8,128)(2,1)S(1)} %get-tuple-element.239), channel_id=1, source_target_pairs={{0,8},{8,0},{16,24},{24,16},{1,9},{9,1},{17,25},{25,17},{2,10},{10... | collective-permute-start | bytes 294920 | tf_op jit(solution)/shard_map/ppermute | solution.py:886
  121.7 2.6 %collective-permute-start.25 = (bf16[48,1024]{1,0:T(8,128)(2,1)S(1)}, bf16[48,1024]{1,0:T(8,128)(2,1)S(1)}, u32[]{:S(2)}, u32[]{:S(2)}) collective-permute-start(bf16[48,1024]{1,0:T(8,128)(2,1)S(1)} %get-tuple-element.240), channel_id=1, source_target_pairs={{0,16},{8,24},{16,0},{24,8},{1,17},{9,25},{17,1},{25,9},{2,18},{10... | collective-permute-start | bytes 294920 | tf_op jit(solution)/shard_map/ppermute | solution.py:886
  125.5 3.5 %collective-permute-start.32 = (bf16[16,3200]{1,0:T(8,128)(2,1)S(1)}, bf16[16,3200]{1,0:T(8,128)(2,1)S(1)}, u32[]{:S(2)}, u32[]{:S(2)}) collective-permute-start(bf16[16,3200]{1,0:T(8,128)(2,1)S(1)} %get-tuple-element.252), channel_id=1, source_target_pairs={{0,16},{8,24},{16,0},{24,8},{1,17},{9,25},{17,1},{25,9},{2,18},{10... | collective-permute-start | bytes 307208 | tf_op jit(solution)/shard_map/ppermute | solution.py:886
  129.9 2.0 %collective-permute-done.25.refs_2_ = bf16[48,1024]{1,0:T(8,128)(2,1)S(1)} collective-permute-done((bf16[48,1024]{1,0:T(8,128)(2,1)S(1)}, bf16[48,1024]{1,0:T(8,128)(2,1)S(1)}, u32[]{:S(2)}, u32[]{:S(2)}) %collective-permute-start.25) | collective-permute-done | bytes 98336 | tf_op jit(solution)/shard_map/ppermute | solution.py:886
  132.2 2.0 %collective-permute-start.36 = (f32[88,128]{1,0:T(8,128)S(1)}, f32[88,128]{1,0:T(8,128)S(1)}, u32[]{:S(2)}, u32[]{:S(2)}) collective-permute-start(f32[88,128]{1,0:T(8,128)S(1)} %get-tuple-element.258), channel_id=1, source_target_pairs={{0,4},{1,5},{2,6},{3,7},{4,0},{5,1},{6,2},{7,3},{8,12},{9,13},{10,... | collective-permute-start | bytes 135176 | tf_op jit(solution)/shard_map/ppermute | solution.py:886
  134.2 1.7 %collective-permute-done.35.refs_9_ = f32[88,128]{1,0:T(8,128)S(1)} collective-permute-done((f32[88,128]{1,0:T(8,128)S(1)}, f32[88,128]{1,0:T(8,128)S(1)}, u32[]{:S(2)}, u32[]{:S(2)}) %collective-permute-start.35) | collective-permute-done | bytes 45088 | tf_op jit(solution)/shard_map/ppermute | solution.py:886
  135.9 1.8 %collective-permute-start.37 = (f32[88,128]{1,0:T(8,128)S(1)}, f32[88,128]{1,0:T(8,128)S(1)}, u32[]{:S(2)}, u32[]{:S(2)}) collective-permute-start(f32[88,128]{1,0:T(8,128)S(1)} %get-tuple-element.259), channel_id=1, source_target_pairs={{0,6},{1,7},{2,4},{3,5},{4,2},{5,3},{6,0},{7,1},{8,14},{9,15},{10,... | collective-permute-start | bytes 135176 | tf_op jit(solution)/shard_map/ppermute | solution.py:886
  137.7 3.2 %collective-permute-done.37.refs_11_ = f32[88,128]{1,0:T(8,128)S(1)} collective-permute-done((f32[88,128]{1,0:T(8,128)S(1)}, f32[88,128]{1,0:T(8,128)S(1)}, u32[]{:S(2)}, u32[]{:S(2)}) %collective-permute-start.37) | collective-permute-done | bytes 45088 | tf_op jit(solution)/shard_map/ppermute | solution.py:886
  141.0 3.9 %collective-permute-start.40 = (bf16[16,7040]{1,0:T(8,128)(2,1)S(1)}, bf16[16,7040]{1,0:T(8,128)(2,1)S(1)}, u32[]{:S(2)}, u32[]{:S(2)}) collective-permute-start(bf16[16,7040]{1,0:T(8,128)(2,1)S(1)} %join.1.refs_0_), channel_id=1, source_target_pairs={{0,24},{8,16},{16,8},{24,0},{1,25},{9,17},{17,9},{25,1},{2,26},{10... | collective-permute-start | bytes 675848 | tf_op jit(solution)/shard_map/ppermute | solution.py:886
  144.9 3.0 %collective-permute-start.39 = (bf16[16,7040]{1,0:T(8,128)(2,1)S(1)}, bf16[16,7040]{1,0:T(8,128)(2,1)S(1)}, u32[]{:S(2)}, u32[]{:S(2)}) collective-permute-start(bf16[16,7040]{1,0:T(8,128)(2,1)S(1)} %join.1.refs_0_), channel_id=1, source_target_pairs={{0,16},{8,24},{16,0},{24,8},{1,17},{9,25},{17,1},{25,9},{2,18},{10... | collective-permute-start | bytes 675848 | tf_op jit(solution)/shard_map/ppermute | solution.py:886
  147.9 2.6 %collective-permute-done.40.refs_3_ = bf16[16,7040]{1,0:T(8,128)(2,1)S(1)} collective-permute-done((bf16[16,7040]{1,0:T(8,128)(2,1)S(1)}, bf16[16,7040]{1,0:T(8,128)(2,1)S(1)}, u32[]{:S(2)}, u32[]{:S(2)}) %collective-permute-start.40) | collective-permute-done | bytes 225312 | tf_op jit(solution)/shard_map/ppermute | solution.py:886
  150.5 9.1 %collective-permute-done.39.refs_2_ = bf16[16,7040]{1,0:T(8,128)(2,1)S(1)} collective-permute-done((bf16[16,7040]{1,0:T(8,128)(2,1)S(1)}, bf16[16,7040]{1,0:T(8,128)(2,1)S(1)}, u32[]{:S(2)}, u32[]{:S(2)}) %collective-permute-start.39) | collective-permute-done | bytes 225312 | tf_op jit(solution)/shard_map/ppermute | solution.py:886
  159.6 1.5 final.1
  (81 shorter events, 13.2 us)
Async XLA Ops:
  2.3 6.5 %collective-permute-start.2 = (f32[88,128]{1,0:T(8,128)}, f32[88,128]{1,0:T(8,128)S(1)}, u32[]{:S(2)}, u32[]{:S(2)}) collective-permute-start(f32[88,128]{1,0:T(8,128)} %place.1.refs_0_), channel_id=1, source_target_pairs={{0,6},{1,7},{2,4},{3,5},{4,2},{5,3},{6,0},{7,1},{8,14},{9,15},{10,... | collective-permute-start | bytes 135176 | tf_op jit(solution)/shard_map/ppermute | solution.py:886
  6.2 4.3 %collective-permute-start.1 = (f32[88,128]{1,0:T(8,128)}, f32[88,128]{1,0:T(8,128)S(1)}, u32[]{:S(2)}, u32[]{:S(2)}) collective-permute-start(f32[88,128]{1,0:T(8,128)} %place.1.refs_0_), channel_id=1, source_target_pairs={{0,4},{1,5},{2,6},{3,7},{4,0},{5,1},{6,2},{7,3},{8,12},{9,13},{10,... | collective-permute-start | bytes 135176 | tf_op jit(solution)/shard_map/ppermute | solution.py:886
  6.7 4.3 %collective-permute-start = (f32[88,128]{1,0:T(8,128)}, f32[88,128]{1,0:T(8,128)S(1)}, u32[]{:S(2)}, u32[]{:S(2)}) collective-permute-start(f32[88,128]{1,0:T(8,128)} %place.1.refs_0_), channel_id=1, source_target_pairs={{0,2},{1,3},{2,0},{3,1},{4,6},{5,7},{6,4},{7,5},{8,10},{9,11},{10,... | collective-permute-start | bytes 135176 | tf_op jit(solution)/shard_map/ppermute | solution.py:886
  11.0 9.9 %collective-permute-start.4 = (bf16[64,3200]{1,0:T(8,128)(2,1)}, bf16[64,3200]{1,0:T(8,128)(2,1)S(1)}, u32[]{:S(2)}, u32[]{:S(2)}) collective-permute-start(bf16[64,3200]{1,0:T(8,128)(2,1)} %get-tuple-element.163.refs_0_), channel_id=1, source_target_pairs={{0,4},{1,5},{2,6},{3,7},{4,0},{5,1},{6,2},{7,3},{8,12},{9,13},{10,... | collective-permute-start | bytes 1228808 | tf_op jit(solution)/shard_map/ppermute | solution.py:886
  12.5 9.7 %collective-permute-start.3 = (bf16[64,3200]{1,0:T(8,128)(2,1)}, bf16[64,3200]{1,0:T(8,128)(2,1)S(1)}, u32[]{:S(2)}, u32[]{:S(2)}) collective-permute-start(bf16[64,3200]{1,0:T(8,128)(2,1)} %get-tuple-element.163.refs_0_), channel_id=1, source_target_pairs={{0,2},{1,3},{2,0},{3,1},{4,6},{5,7},{6,4},{7,5},{8,10},{9,11},{10,... | collective-permute-start | bytes 1228808 | tf_op jit(solution)/shard_map/ppermute | solution.py:886
  13.8 1.5 collective-permute-start.5
  17.1 12.3 %copy-start.7 = (bf16[64,3200]{1,0:T(8,128)(2,1)S(1)}, bf16[64,3200]{1,0:T(8,128)(2,1)}, u32[]{:S(2)}) copy-start(bf16[64,3200]{1,0:T(8,128)(2,1)} %get-tuple-element.163.refs_0_) | copy-start | bytes 1228804
  22.3 6.6 %collective-permute-start.6 = (bf16[32,3200]{1,0:T(8,128)(2,1)S(1)}, bf16[32,3200]{1,0:T(8,128)(2,1)S(1)}, u32[]{:S(2)}, u32[]{:S(2)}) collective-permute-start(bf16[32,3200]{1,0:T(8,128)(2,1)S(1)} %get-tuple-element.161), channel_id=1, source_target_pairs={{0,4},{1,5},{2,6},{3,7},{4,0},{5,1},{6,2},{7,3},{8,12},{9,13},{10,... | collective-permute-start | bytes 614408 | tf_op jit(solution)/shard_map/ppermute | solution.py:886
  22.7 9.4 %copy-start.8 = (bf16[192,1024]{1,0:T(8,128)(2,1)S(1)}, bf16[192,1024]{1,0:T(8,128)(2,1)}, u32[]{:S(2)}) copy-start(bf16[192,1024]{1,0:T(8,128)(2,1)} %get-tuple-element.186.refs_0_) | copy-start | bytes 1179652
  22.7 6.6 %collective-permute-start.7 = (bf16[32,3200]{1,0:T(8,128)(2,1)S(1)}, bf16[32,3200]{1,0:T(8,128)(2,1)S(1)}, u32[]{:S(2)}, u32[]{:S(2)}) collective-permute-start(bf16[32,3200]{1,0:T(8,128)(2,1)S(1)} %get-tuple-element.162), channel_id=1, source_target_pairs={{0,2},{1,3},{2,0},{3,1},{4,6},{5,7},{6,4},{7,5},{8,10},{9,11},{10,... | collective-permute-start | bytes 614408 | tf_op jit(solution)/shard_map/ppermute | solution.py:886
  23.3 5.4 %collective-permute-start.9 = (bf16[80,512]{1,0:T(8,128)(2,1)S(1)}, bf16[80,512]{1,0:T(8,128)(2,1)S(1)}, u32[]{:S(2)}, u32[]{:S(2)}) collective-permute-start(bf16[80,512]{1,0:T(8,128)(2,1)S(1)} %get-tuple-element.158), channel_id=1, source_target_pairs={{0,2},{1,3},{2,4},{3,5},{4,6},{5,7},{8,10},{9,11},{10,12},{11,13},... | collective-permute-start | bytes 245768 | tf_op jit(solution)/shard_map/ppermute | solution.py:1178
  26.7 2.2 %collective-permute-start.8 = (bf16[80,512]{1,0:T(8,128)(2,1)S(1)}, bf16[80,512]{1,0:T(8,128)(2,1)S(1)}, u32[]{:S(2)}, u32[]{:S(2)}) collective-permute-start(bf16[80,512]{1,0:T(8,128)(2,1)S(1)} %get-tuple-element.158), channel_id=1, source_target_pairs={{0,1},{1,2},{2,3},{3,4},{4,5},{5,6},{6,7},{8,9},{9,10},{10,11},{11... | collective-permute-start | bytes 245768 | tf_op jit(solution)/shard_map/ppermute | solution.py:1178
  29.5 18.3 %copy-start.11 = (s32[4,128]{1,0:T(4,128)S(1)}, s32[4,128]{1,0:T(4,128)}, u32[]{:S(2)}) copy-start(s32[4,128]{1,0:T(4,128)} %refs_8_.3) | copy-start | bytes 6148
  29.5 18.3 %collective-permute-start.14 = (bf16[4,64,3200]{2,1,0:T(8,128)(2,1)S(1)}, bf16[4,64,3200]{2,1,0:T(8,128)(2,1)S(1)}, u32[]{:S(2)}, u32[]{:S(2)}) collective-permute-start(bf16[4,64,3200]{2,1,0:T(8,128)(2,1)S(1)} %bundle.4.refs_0_), channel_id=1, source_target_pairs={{0,1},{1,0},{2,3},{3,2},{4,5},{5,4},{6,7},{7,6},{8,9},{9,8},{10,11... | collective-permute-start | bytes 4915208 | tf_op jit(solution)/shard_map/ppermute | solution.py:886
  32.1 12.9 %collective-permute-start.11 = (bf16[192,1024]{1,0:T(8,128)(2,1)S(1)}, bf16[192,1024]{1,0:T(8,128)(2,1)S(1)}, u32[]{:S(2)}, u32[]{:S(2)}) collective-permute-start(bf16[192,1024]{1,0:T(8,128)(2,1)S(1)} %copy-done.8), channel_id=1, source_target_pairs={{0,4},{1,5},{2,6},{3,7},{4,0},{5,1},{6,2},{7,3},{8,12},{9,13},{10,... | collective-permute-start | bytes 1179656 | tf_op jit(solution)/shard_map/ppermute | solution.py:886
  35.2 11.2 %collective-permute-start.10 = (bf16[192,1024]{1,0:T(8,128)(2,1)S(1)}, bf16[192,1024]{1,0:T(8,128)(2,1)S(1)}, u32[]{:S(2)}, u32[]{:S(2)}) collective-permute-start(bf16[192,1024]{1,0:T(8,128)(2,1)S(1)} %copy-done.8), channel_id=1, source_target_pairs={{0,2},{1,3},{2,0},{3,1},{4,6},{5,7},{6,4},{7,5},{8,10},{9,11},{10,... | collective-permute-start | bytes 1179656 | tf_op jit(solution)/shard_map/ppermute | solution.py:886
  46.5 9.0 %collective-permute-start.12 = (bf16[96,1024]{1,0:T(8,128)(2,1)S(1)}, bf16[96,1024]{1,0:T(8,128)(2,1)S(1)}, u32[]{:S(2)}, u32[]{:S(2)}) collective-permute-start(bf16[96,1024]{1,0:T(8,128)(2,1)S(1)} %get-tuple-element.178), channel_id=1, source_target_pairs={{0,4},{1,5},{2,6},{3,7},{4,0},{5,1},{6,2},{7,3},{8,12},{9,13},{10,... | collective-permute-start | bytes 589832 | tf_op jit(solution)/shard_map/ppermute | solution.py:886
  46.8 8.7 %collective-permute-start.13 = (bf16[96,1024]{1,0:T(8,128)(2,1)S(1)}, bf16[96,1024]{1,0:T(8,128)(2,1)S(1)}, u32[]{:S(2)}, u32[]{:S(2)}) collective-permute-start(bf16[96,1024]{1,0:T(8,128)(2,1)S(1)} %get-tuple-element.179), channel_id=1, source_target_pairs={{0,2},{1,3},{2,0},{3,1},{4,6},{5,7},{6,4},{7,5},{8,10},{9,11},{10,... | collective-permute-start | bytes 589832 | tf_op jit(solution)/shard_map/ppermute | solution.py:886
  55.5 3.6 %copy-start.1 = (bf16[4,128,512]{2,1,0:T(8,128)(2,1)S(1)}, bf16[4,128,512]{2,1,0:T(8,128)(2,1)}, u32[]{:S(2)}) copy-start(bf16[4,128,512]{2,1,0:T(8,128)(2,1)} %param.22) | copy-start | bytes 1572868
  55.5 3.6 %copy-start.2 = (f32[4,128,512]{2,1,0:T(8,128)S(1)}, f32[4,128,512]{2,1,0:T(8,128)}, u32[]{:S(2)}) copy-start(f32[4,128,512]{2,1,0:T(8,128)} %param.24) | copy-start | bytes 3145732
  55.6 3.5 %collective-permute-start.15 = (bf16[4,192,1024]{2,1,0:T(8,128)(2,1)S(1)}, bf16[4,192,1024]{2,1,0:T(8,128)(2,1)S(1)}, u32[]{:S(2)}, u32[]{:S(2)}) collective-permute-start(bf16[4,192,1024]{2,1,0:T(8,128)(2,1)S(1)} %bundle.5.refs_0_), channel_id=1, source_target_pairs={{0,1},{1,0},{2,3},{3,2},{4,5},{5,4},{6,7},{7,6},{8,9},{9,8},{10,11... | collective-permute-start | bytes 4718600 | tf_op jit(solution)/shard_map/ppermute | solution.py:886
  59.1 13.5 %copy-start.4 = (f32[512,512]{1,0:T(8,128)S(1)}, f32[512,512]{1,0:T(8,128)}, u32[]{:S(2)}) copy-start(f32[512,512]{1,0:T(8,128)} %copy-done.3) | copy-start | bytes 3145732
  59.1 13.5 %copy-start.6 = (bf16[512,1024]{1,0:T(8,128)(2,1)S(1)}, bf16[512,1024]{1,0:T(8,128)(2,1)}, u32[]{:S(2)}) copy-start(bf16[512,1024]{1,0:T(8,128)(2,1)} %copy-done.5) | copy-start | bytes 3145732
  72.4 11.4 %collective-permute-start.16 = (bf16[4,4,48,1024]{3,2,1,0:T(8,128)(2,1)S(1)}, bf16[4,4,48,1024]{3,2,1,0:T(8,128)(2,1)S(1)}, u32[]{:S(2)}, u32[]{:S(2)}) collective-permute-start(bf16[4,4,48,1024]{3,2,1,0:T(8,128)(2,1)S(1)} %get-tuple-element.211), channel_id=1, source_target_pairs={{0,1},{1,0},{2,3},{3,2},{4,5},{5,4},{6,7},{7,6},{8,9},{9,8},{10,11... | collective-permute-start | bytes 4718600 | tf_op jit(solution)/shard_map/ppermute | solution.py:886
  83.8 6.6 %collective-permute-start.18 = (bf16[80,512]{1,0:T(8,128)(2,1)S(1)}, bf16[80,512]{1,0:T(8,128)(2,1)S(1)}, u32[]{:S(2)}, u32[]{:S(2)}) collective-permute-start(bf16[80,512]{1,0:T(8,128)(2,1)S(1)} %get-tuple-element.212), channel_id=1, source_target_pairs={{2,0},{3,1},{4,2},{5,3},{6,4},{7,5},{10,8},{11,9},{12,10},{13,11},... | collective-permute-start | bytes 245768 | tf_op jit(solution)/shard_map/ppermute | solution.py:1267
  85.1 5.3 %collective-permute-start.17 = (bf16[80,512]{1,0:T(8,128)(2,1)S(1)}, bf16[80,512]{1,0:T(8,128)(2,1)S(1)}, u32[]{:S(2)}, u32[]{:S(2)}) collective-permute-start(bf16[80,512]{1,0:T(8,128)(2,1)S(1)} %get-tuple-element.212), channel_id=1, source_target_pairs={{1,0},{2,1},{3,2},{4,3},{5,4},{6,5},{7,6},{9,8},{10,9},{11,10},{12... | collective-permute-start | bytes 245768 | tf_op jit(solution)/shard_map/ppermute | solution.py:1267
  90.4 4.6 %collective-permute-start.19 = (bf16[4,4,16,3200]{3,2,1,0:T(8,128)(2,1)S(1)}, bf16[4,4,16,3200]{3,2,1,0:T(8,128)(2,1)S(1)}, u32[]{:S(2)}, u32[]{:S(2)}) collective-permute-start(bf16[4,4,16,3200]{3,2,1,0:T(8,128)(2,1)S(1)} %get-tuple-element.213), channel_id=1, source_target_pairs={{0,1},{1,0},{2,3},{3,2},{4,5},{5,4},{6,7},{7,6},{8,9},{9,8},{10,11... | collective-permute-start | bytes 4915208 | tf_op jit(solution)/shard_map/ppermute | solution.py:886
  92.2 15.8 %collective-permute-start.20 = (bf16[4,48,1024]{2,1,0:T(8,128)(2,1)S(1)}, bf16[4,48,1024]{2,1,0:T(8,128)(2,1)S(1)}, u32[]{:S(2)}, u32[]{:S(2)}) collective-permute-start(bf16[4,48,1024]{2,1,0:T(8,128)(2,1)S(1)} %get-tuple-element.229), channel_id=1, source_target_pairs={{0,2},{1,3},{2,0},{3,1},{4,6},{5,7},{6,4},{7,5},{8,10},{9,11},{10,... | collective-permute-start | bytes 1179656 | tf_op jit(solution)/shard_map/ppermute | solution.py:886
  94.9 13.1 %collective-permute-start.21 = (bf16[4,48,1024]{2,1,0:T(8,128)(2,1)S(1)}, bf16[4,48,1024]{2,1,0:T(8,128)(2,1)S(1)}, u32[]{:S(2)}, u32[]{:S(2)}) collective-permute-start(bf16[4,48,1024]{2,1,0:T(8,128)(2,1)S(1)} %get-tuple-element.230), channel_id=1, source_target_pairs={{0,4},{1,5},{2,6},{3,7},{4,0},{5,1},{6,2},{7,3},{8,12},{9,13},{10,... | collective-permute-start | bytes 1179656 | tf_op jit(solution)/shard_map/ppermute | solution.py:886
  95.4 18.2 %collective-permute-start.27 = (bf16[4,16,3200]{2,1,0:T(8,128)(2,1)S(1)}, bf16[4,16,3200]{2,1,0:T(8,128)(2,1)S(1)}, u32[]{:S(2)}, u32[]{:S(2)}) collective-permute-start(bf16[4,16,3200]{2,1,0:T(8,128)(2,1)S(1)} %get-tuple-element.242), channel_id=1, source_target_pairs={{0,2},{1,3},{2,0},{3,1},{4,6},{5,7},{6,4},{7,5},{8,10},{9,11},{10,... | collective-permute-start | bytes 1228808 | tf_op jit(solution)/shard_map/ppermute | solution.py:886
  98.0 17.6 %collective-permute-start.28 = (bf16[4,16,3200]{2,1,0:T(8,128)(2,1)S(1)}, bf16[4,16,3200]{2,1,0:T(8,128)(2,1)S(1)}, u32[]{:S(2)}, u32[]{:S(2)}) collective-permute-start(bf16[4,16,3200]{2,1,0:T(8,128)(2,1)S(1)} %get-tuple-element.243), channel_id=1, source_target_pairs={{0,4},{1,5},{2,6},{3,7},{4,0},{5,1},{6,2},{7,3},{8,12},{9,13},{10,... | collective-permute-start | bytes 1228808 | tf_op jit(solution)/shard_map/ppermute | solution.py:886
  108.1 9.7 %collective-permute-start.22 = (bf16[2,48,1024]{2,1,0:T(8,128)(2,1)S(1)}, bf16[2,48,1024]{2,1,0:T(8,128)(2,1)S(1)}, u32[]{:S(2)}, u32[]{:S(2)}) collective-permute-start(bf16[2,48,1024]{2,1,0:T(8,128)(2,1)S(1)} %get-tuple-element.236), channel_id=1, source_target_pairs={{0,2},{1,3},{2,0},{3,1},{4,6},{5,7},{6,4},{7,5},{8,10},{9,11},{10,... | collective-permute-start | bytes 589832 | tf_op jit(solution)/shard_map/ppermute | solution.py:886
  109.6 10.2 %collective-permute-start.23 = (bf16[2,48,1024]{2,1,0:T(8,128)(2,1)S(1)}, bf16[2,48,1024]{2,1,0:T(8,128)(2,1)S(1)}, u32[]{:S(2)}, u32[]{:S(2)}) collective-permute-start(bf16[2,48,1024]{2,1,0:T(8,128)(2,1)S(1)} %get-tuple-element.237), channel_id=1, source_target_pairs={{0,4},{1,5},{2,6},{3,7},{4,0},{5,1},{6,2},{7,3},{8,12},{9,13},{10,... | collective-permute-start | bytes 589832 | tf_op jit(solution)/shard_map/ppermute | solution.py:886
  115.7 8.6 %collective-permute-start.29 = (bf16[2,16,3200]{2,1,0:T(8,128)(2,1)S(1)}, bf16[2,16,3200]{2,1,0:T(8,128)(2,1)S(1)}, u32[]{:S(2)}, u32[]{:S(2)}) collective-permute-start(bf16[2,16,3200]{2,1,0:T(8,128)(2,1)S(1)} %get-tuple-element.248), channel_id=1, source_target_pairs={{0,2},{1,3},{2,0},{3,1},{4,6},{5,7},{6,4},{7,5},{8,10},{9,11},{10,... | collective-permute-start | bytes 614408 | tf_op jit(solution)/shard_map/ppermute | solution.py:886
  115.8 9.3 %collective-permute-start.30 = (bf16[2,16,3200]{2,1,0:T(8,128)(2,1)S(1)}, bf16[2,16,3200]{2,1,0:T(8,128)(2,1)S(1)}, u32[]{:S(2)}, u32[]{:S(2)}) collective-permute-start(bf16[2,16,3200]{2,1,0:T(8,128)(2,1)S(1)} %get-tuple-element.249), channel_id=1, source_target_pairs={{0,4},{1,5},{2,6},{3,7},{4,0},{5,1},{6,2},{7,3},{8,12},{9,13},{10,... | collective-permute-start | bytes 614408 | tf_op jit(solution)/shard_map/ppermute | solution.py:886
  117.5 8.0 %collective-permute-start.34 = (f32[4,88,128]{2,1,0:T(8,128)S(1)}, f32[4,88,128]{2,1,0:T(8,128)S(1)}, u32[]{:S(2)}, u32[]{:S(2)}) collective-permute-start(f32[4,88,128]{2,1,0:T(8,128)S(1)} %get-tuple-element.255), channel_id=1, source_target_pairs={{0,1},{1,0},{2,3},{3,2},{4,5},{5,4},{6,7},{7,6},{8,9},{9,8},{10,11... | collective-permute-start | bytes 540680 | tf_op jit(solution)/shard_map/ppermute | solution.py:886
  120.1 8.9 %collective-permute-start.24 = (bf16[48,1024]{1,0:T(8,128)(2,1)S(1)}, bf16[48,1024]{1,0:T(8,128)(2,1)S(1)}, u32[]{:S(2)}, u32[]{:S(2)}) collective-permute-start(bf16[48,1024]{1,0:T(8,128)(2,1)S(1)} %get-tuple-element.239), channel_id=1, source_target_pairs={{0,8},{8,0},{16,24},{24,16},{1,9},{9,1},{17,25},{25,17},{2,10},{10... | collective-permute-start | bytes 294920 | tf_op jit(solution)/shard_map/ppermute | solution.py:886
  121.7 10.2 %collective-permute-start.25 = (bf16[48,1024]{1,0:T(8,128)(2,1)S(1)}, bf16[48,1024]{1,0:T(8,128)(2,1)S(1)}, u32[]{:S(2)}, u32[]{:S(2)}) collective-permute-start(bf16[48,1024]{1,0:T(8,128)(2,1)S(1)} %get-tuple-element.240), channel_id=1, source_target_pairs={{0,16},{8,24},{16,0},{24,8},{1,17},{9,25},{17,1},{25,9},{2,18},{10... | collective-permute-start | bytes 294920 | tf_op jit(solution)/shard_map/ppermute | solution.py:886
  124.3 7.9 %collective-permute-start.26 = (bf16[48,1024]{1,0:T(8,128)(2,1)S(1)}, bf16[48,1024]{1,0:T(8,128)(2,1)S(1)}, u32[]{:S(2)}, u32[]{:S(2)}) collective-permute-start(bf16[48,1024]{1,0:T(8,128)(2,1)S(1)} %get-tuple-element.241), channel_id=1, source_target_pairs={{0,24},{8,16},{16,8},{24,0},{1,25},{9,17},{17,9},{25,1},{2,26},{10... | collective-permute-start | bytes 294920 | tf_op jit(solution)/shard_map/ppermute | solution.py:886
  125.4 15.5 %collective-permute-start.31 = (bf16[16,3200]{1,0:T(8,128)(2,1)S(1)}, bf16[16,3200]{1,0:T(8,128)(2,1)S(1)}, u32[]{:S(2)}, u32[]{:S(2)}) collective-permute-start(bf16[16,3200]{1,0:T(8,128)(2,1)S(1)} %get-tuple-element.251), channel_id=1, source_target_pairs={{0,8},{8,0},{16,24},{24,16},{1,9},{9,1},{17,25},{25,17},{2,10},{10... | collective-permute-start | bytes 307208 | tf_op jit(solution)/shard_map/ppermute | solution.py:886
  125.5 15.4 %collective-permute-start.32 = (bf16[16,3200]{1,0:T(8,128)(2,1)S(1)}, bf16[16,3200]{1,0:T(8,128)(2,1)S(1)}, u32[]{:S(2)}, u32[]{:S(2)}) collective-permute-start(bf16[16,3200]{1,0:T(8,128)(2,1)S(1)} %get-tuple-element.252), channel_id=1, source_target_pairs={{0,16},{8,24},{16,0},{24,8},{1,17},{9,25},{17,1},{25,9},{2,18},{10... | collective-permute-start | bytes 307208 | tf_op jit(solution)/shard_map/ppermute | solution.py:886
  129.0 11.9 %collective-permute-start.33 = (bf16[16,3200]{1,0:T(8,128)(2,1)S(1)}, bf16[16,3200]{1,0:T(8,128)(2,1)S(1)}, u32[]{:S(2)}, u32[]{:S(2)}) collective-permute-start(bf16[16,3200]{1,0:T(8,128)(2,1)S(1)} %get-tuple-element.253), channel_id=1, source_target_pairs={{0,24},{8,16},{16,8},{24,0},{1,25},{9,17},{17,9},{25,1},{2,26},{10... | collective-permute-start | bytes 307208 | tf_op jit(solution)/shard_map/ppermute | solution.py:886
  131.9 4.0 %collective-permute-start.35 = (f32[88,128]{1,0:T(8,128)S(1)}, f32[88,128]{1,0:T(8,128)S(1)}, u32[]{:S(2)}, u32[]{:S(2)}) collective-permute-start(f32[88,128]{1,0:T(8,128)S(1)} %get-tuple-element.257), channel_id=1, source_target_pairs={{0,2},{1,3},{2,0},{3,1},{4,6},{5,7},{6,4},{7,5},{8,10},{9,11},{10,... | collective-permute-start | bytes 135176 | tf_op jit(solution)/shard_map/ppermute | solution.py:886
  132.2 5.5 %collective-permute-start.36 = (f32[88,128]{1,0:T(8,128)S(1)}, f32[88,128]{1,0:T(8,128)S(1)}, u32[]{:S(2)}, u32[]{:S(2)}) collective-permute-start(f32[88,128]{1,0:T(8,128)S(1)} %get-tuple-element.258), channel_id=1, source_target_pairs={{0,4},{1,5},{2,6},{3,7},{4,0},{5,1},{6,2},{7,3},{8,12},{9,13},{10,... | collective-permute-start | bytes 135176 | tf_op jit(solution)/shard_map/ppermute | solution.py:886
  135.9 4.9 %collective-permute-start.37 = (f32[88,128]{1,0:T(8,128)S(1)}, f32[88,128]{1,0:T(8,128)S(1)}, u32[]{:S(2)}, u32[]{:S(2)}) collective-permute-start(f32[88,128]{1,0:T(8,128)S(1)} %get-tuple-element.259), channel_id=1, source_target_pairs={{0,6},{1,7},{2,4},{3,5},{4,2},{5,3},{6,0},{7,1},{8,14},{9,15},{10,... | collective-permute-start | bytes 135176 | tf_op jit(solution)/shard_map/ppermute | solution.py:886
  141.0 9.5 %collective-permute-start.40 = (bf16[16,7040]{1,0:T(8,128)(2,1)S(1)}, bf16[16,7040]{1,0:T(8,128)(2,1)S(1)}, u32[]{:S(2)}, u32[]{:S(2)}) collective-permute-start(bf16[16,7040]{1,0:T(8,128)(2,1)S(1)} %join.1.refs_0_), channel_id=1, source_target_pairs={{0,24},{8,16},{16,8},{24,0},{1,25},{9,17},{17,9},{25,1},{2,26},{10... | collective-permute-start | bytes 675848 | tf_op jit(solution)/shard_map/ppermute | solution.py:886
  144.9 14.7 %collective-permute-start.39 = (bf16[16,7040]{1,0:T(8,128)(2,1)S(1)}, bf16[16,7040]{1,0:T(8,128)(2,1)S(1)}, u32[]{:S(2)}, u32[]{:S(2)}) collective-permute-start(bf16[16,7040]{1,0:T(8,128)(2,1)S(1)} %join.1.refs_0_), channel_id=1, source_target_pairs={{0,16},{8,24},{16,0},{24,8},{1,17},{9,25},{17,1},{25,9},{2,18},{10... | collective-permute-start | bytes 675848 | tf_op jit(solution)/shard_map/ppermute | solution.py:886
  147.9 11.7 %collective-permute-start.38 = (bf16[16,7040]{1,0:T(8,128)(2,1)S(1)}, bf16[16,7040]{1,0:T(8,128)(2,1)S(1)}, u32[]{:S(2)}, u32[]{:S(2)}) collective-permute-start(bf16[16,7040]{1,0:T(8,128)(2,1)S(1)} %join.1.refs_0_), channel_id=1, source_target_pairs={{0,8},{8,0},{16,24},{24,16},{1,9},{9,1},{17,25},{25,17},{2,10},{10... | collective-permute-start | bytes 675848 | tf_op jit(solution)/shard_map/ppermute | solution.py:886
  (5 other events, 4.5 us)
